TPU v7x, 512 devices: a whole 4x4x16 slice. The times are simulated.
512 devices in a mesh: tm: 32 (over x, y, core), col: 16 (over z).
Axes of the slice: x: 4, y: 4, z: 16, core: 2. Of those that a mesh axis runs over, the one named last changes fastest.
Arguments:
- initial: float32 [512], replicated, may hold values from 1 to 3
- offsets: int32 [512, 4], P('tm'), may hold values from -32 to 32
- upwind: int32 [512, 512], P('tm'), may hold values from 0 to 3
- courant: float32 [512, 512], P('tm'), may hold values from 0.02 to 0.4
- obs_cells: int32 [512, 64], P('tm'), may hold values from 0 to 511
- gains: float32 [512, 64, 512], P('tm'), may hold values from -0.05 to 0.05
- observed: float32 [512, 64], P('tm'), may hold values from -1 to 5
- smooth_gain: float32 [512, 512], P('tm'), may hold values from 0.3 to 1
Outputs:
- filtered: float32 [512, 512], P('tm')
- smoothed: float32 [512, 512], P('tm')
All inputs are finite; a program needn't handle non-finite values.
Results may differ from a plain program's by a relative error of at most 0.0003.
Values sent between devices are 32-bit elements; how exact they have to be, the bound alone decides.
No kernel may reach another device: no remote copies, remote signals or barrier semaphores. Data moves between devices by JAX's collectives and lax.ppermute only.
A program may use at most 64 MiB of HBM per device.

v0:
```python
import jax
import jax.numpy as jnp
from jax import lax
from jax.sharding import PartitionSpec as P

STATE_CELLS = 512
BANDS = 4
MAXOFF = 32


HIGHEST_PRECISION = lax.Precision.HIGHEST
DIFFUSION = 0.25
RELAXATION = 0.02


def passed_along(block, axis, distance):
    devices = range(lax.axis_size(axis))
    route = [(i - distance, i) for i in devices if i - distance in devices]
    return lax.ppermute(block, axis, route)


def joined_along(parts, dim):
    parts = jnp.moveaxis(parts, 0, dim)
    dims = parts.shape
    return parts.reshape(*dims[:dim], dims[dim] * dims[dim + 1], *dims[dim + 2 :])


def sent_to_all(shard, axis):
    copies = jnp.broadcast_to(shard, (lax.axis_size(axis), *shard.shape))
    return lax.all_to_all(copies, axis, split_axis=0, concat_axis=0, tiled=True)


def collect(shard, axis, dim):
    return joined_along(sent_to_all(shard, axis), dim)


def shifted(values, offset):
    widths = [(0, 0)] * (values.ndim - 1) + [(MAXOFF, MAXOFF)]
    padded = jnp.pad(values, widths)
    return lax.dynamic_slice_in_dim(padded, MAXOFF + offset, STATE_CELLS, values.ndim - 1)


def transition(values, offsets, upwind, courant):
    result = (1.0 - courant - DIFFUSION) * values + 0.5 * DIFFUSION * (
        shifted(values, 1) + shifted(values, -1)
    )
    for band in range(BANDS):
        weight = jnp.where(upwind == band, courant, 0.0)
        result = result + weight * shifted(values, offsets[band])
    return result


def transpose_apply(values, offsets, upwind, courant):
    result = (1.0 - courant - DIFFUSION) * values + 0.5 * DIFFUSION * (
        shifted(values, 1) + shifted(values, -1)
    )
    for band in range(BANDS):
        weight = jnp.where(upwind == band, courant, 0.0)
        result = result + shifted(weight * values, 0 - offsets[band])
    return result


def observe(predicted, obs_cells, gains, observed):
    innovation = predicted[..., obs_cells] - observed
    corrected = predicted.at[..., obs_cells].add(-RELAXATION * innovation)
    return corrected - jnp.dot(innovation, gains, precision=HIGHEST_PRECISION)


def filter_step(current, offsets, upwind, courant, obs_cells, gains, observed):
    return observe(transition(current, offsets, upwind, courant), obs_cells, gains, observed)


def smooth_step(current, offsets, upwind, courant, smooth_gain, previous):
    mismatch = current - transition(previous, offsets, upwind, courant)
    return previous + smooth_gain * transpose_apply(mismatch, offsets, upwind, courant)


def panel_identity():
    panel_width = STATE_CELLS // lax.axis_size("col")
    panel_rows = lax.axis_index("col") * panel_width + jnp.arange(panel_width)
    return (panel_rows[:, None] == jnp.arange(STATE_CELLS)[None, :]).astype(jnp.float32)


def from_neighbour(values, direction):
    return passed_along(values, "tm", direction)


def block_ends(build_map, direction):
    tm_place = lax.axis_index("tm")
    tm_count = lax.axis_size("tm")
    map_panel, offset_state = build_map()
    whole_map = collect(map_panel, "col", 0)
    for depth_level in range((tm_count - 1).bit_length()):
        distance = direction * (1 << depth_level)
        source = tm_place - distance
        active = (source >= 0) & (source < tm_count)
        earlier_map, earlier_state = passed_along((whole_map, offset_state), "tm", distance)
        joined_map = jnp.dot(earlier_map, whole_map, precision=HIGHEST_PRECISION)
        joined_state = offset_state + jnp.dot(earlier_state, whole_map, precision=HIGHEST_PRECISION)
        whole_map = jnp.where(active, joined_map, whole_map)
        offset_state = jnp.where(active, joined_state, offset_state)
    return offset_state


def on_device(initial, offsets, upwind, courant, obs_cells, gains, observed, smooth_gain):
    tm_place = lax.axis_index("tm")
    tm_count = lax.axis_size("tm")
    at_first = tm_place == 0
    at_last = tm_place == tm_count - 1
    filter_inputs = (offsets, upwind, courant, obs_cells, gains, observed)

    def build_filter():

        def grow(totals, inputs):
            moved = observe(
                transition(totals[0], inputs[0], inputs[1], inputs[2]), inputs[3], inputs[4], 0.0
            )
            return ((moved, filter_step(totals[1], *inputs)), None)

        seed_state = jnp.where(at_first, initial, jnp.zeros_like(initial))
        seed_panel = panel_identity() * jnp.where(at_first, 0.0, 1.0)
        return lax.scan(grow, (seed_panel, seed_state), filter_inputs)[0]

    filter_ends = block_ends(build_filter, 1)
    begin_state = jnp.where(at_first, initial, from_neighbour(filter_ends, 1))

    def forward(current, inputs):
        current = filter_step(current, *inputs)
        return (current, current)

    _, filtered = lax.scan(forward, begin_state, filter_inputs)
    previous = jnp.concatenate([begin_state[None, :], filtered[:-1]], axis=0)
    smooth_inputs = (offsets, upwind, courant, smooth_gain, previous)
    terminal = filtered[-1]

    def build_smooth():

        def grow(totals, inputs):
            moved = inputs[3] * transpose_apply(totals[0], inputs[0], inputs[1], inputs[2])
            return ((moved, smooth_step(totals[1], *inputs)), None)

        seed_state = jnp.where(at_last, terminal, jnp.zeros_like(terminal))
        seed_panel = panel_identity() * jnp.where(at_last, 0.0, 1.0)
        return lax.scan(grow, (seed_panel, seed_state), smooth_inputs, reverse=True)[0]

    smooth_ends = block_ends(build_smooth, -1)
    top_state = jnp.where(at_last, terminal, from_neighbour(smooth_ends, -1))

    def backward(current, inputs):
        return (smooth_step(current, *inputs), current)

    _, smoothed = lax.scan(backward, top_state, smooth_inputs, reverse=True)
    return (filtered, smoothed)


def solution(mesh):
    in_specs = (
        P(),
        P("tm", None),
        P("tm", None),
        P("tm", None),
        P("tm", None),
        P("tm", None, None),
        P("tm", None),
        P("tm", None),
    )
    out_specs = (P("tm", None), P("tm", None))
    return jax.shard_map(
        on_device, mesh=mesh, in_specs=in_specs, out_specs=out_specs, check_vma=False
    )
```

profile of v0, /device:TPU:43, one launch (start us, length us, event | category | flops | bytes accessed | tf_op | source)
XLA Modules:
  0.0 1169.3 jit_solution(8605320908881136066)
XLA Ops:
  0.8 235.9 %while.68 = (s32[]{:T(128)}, f32[32,512]{1,0:T(8,128)S(1)}, f32[512]{0:T(512)S(1)}, f32[16,512]{1,0:T(8,128)}, s32[16,512]{1,0:T(8,128)}, /*index=5*/s32[16,4]{0...) while((s32[]{:T(128)}, f32[32,512]{1,0:T(8,128)S(1)}, ...), condition=%wide.region_3.4_spmd, body=%wide.region_0.3_spmd.sunk | while | flops 13205970 | bytes 966333 | solution.py:122
  236.8 61.7 %all_to_all.10 = f32[16,32,512]{2,1,0:T(8,128)S(1)} all-to-all(f32[16,32,512]{2,1,0:T(8,128)S(1)} %broadcast_in_dim.120), channel_id=1, replica_groups=mesh['tm'=32,'col'=16] {'col'}, dimensions={0} | all-to-all | bytes 2097152 | tf_op jit(solution)/shard_map/all_to_all | solution.py:30
  298.5 7.9 collective-permute-start.2
  306.5 11.7 %collective-permute-done.2 = f32[512,512]{1,0:T(8,128)S(1)} collective-permute-done((f32[512,512]{1,0:T(8,128)S(1)}, f32[512,512]{1,0:T(8,128)S(1)}, u32[]{:S(2)}, u32[]{:S(2)}) %collective-permute-start.2) | collective-permute-done | bytes 1048608 | tf_op jit(solution)/shard_map/ppermute | solution.py:19
  318.2 1.8 convolution_select_fusion.7
  320.0 2.9 collective-permute-start.4
  323.0 21.9 %collective-permute-done.4 = f32[512,512]{1,0:T(8,128)} collective-permute-done((f32[512,512]{1,0:T(8,128)S(1)}, f32[512,512]{1,0:T(8,128)}, u32[]{:S(2)}, u32[]{:S(2)}) %collective-permute-start.4) | collective-permute-done | bytes 1048608 | tf_op jit(solution)/shard_map/ppermute | solution.py:19
  344.9 3.1 convolution_select_fusion.6
  348.0 3.6 collective-permute-start.6
  351.6 7.5 collective-permute-start
  360.4 2.0 collective-permute-start.1
  362.4 14.5 %collective-permute-done.1 = f32[512]{0:T(512)S(1)} collective-permute-done((f32[512]{0:T(512)S(1)}, f32[512]{0:T(512)S(1)}, u32[]{:S(2)}, u32[]{:S(2)}) %collective-permute-start.1) | collective-permute-done | bytes 2080 | tf_op jit(solution)/shard_map/ppermute | solution.py:19
  377.5 3.1 convolution_select_fusion.5
  380.6 3.1 collective-permute-start.8
  383.7 3.7 collective-permute-start.3
  387.4 17.8 %collective-permute-done.3 = f32[512]{0:T(512)S(1)} collective-permute-done((f32[512]{0:T(512)S(1)}, f32[512]{0:T(512)S(1)}, u32[]{:S(2)}, u32[]{:S(2)}) %collective-permute-start.3) | collective-permute-done | bytes 2080 | tf_op jit(solution)/shard_map/ppermute | solution.py:19
  405.8 2.8 collective-permute-start.5
  408.7 1.5 collective-permute-done.5
  410.8 3.2 collective-permute-start.7
  414.0 1.9 convolution_select_fusion.4
  416.5 3.6 collective-permute-start.9
  420.0 4.8 collective-permute-done.9
  424.9 174.2 %while.69 = (s32[]{:T(128)}, f32[512]{0:T(512)S(1)}, f32[16,512]{1,0:T(8,128)S(1)}, f32[16,512]{1,0:T(8,128)}, s32[16,512]{1,0:T(8,128)}, /*index=5*/s32[16,4]{0...) while((s32[]{:T(128)}, f32[512]{0:T(512)S(1)}, ...), condition=%wide.region_6.7_spmd, body=%wide.region_4.6_spmd.sunk | while | flops 405970 | bytes 181665 | solution.py:131
  599.7 190.1 %while.70 = (s32[]{:T(128)}, f32[32,512]{1,0:T(8,128)S(1)}, f32[512]{0:T(512)S(1)}, f32[16,512]{1,0:T(8,128)S(1)}, f32[16,512]{1,0:T(8,128)}, /*index=5*/s32[16,...) while((s32[]{:T(128)}, f32[32,512]{1,0:T(8,128)S(1)}, ...), condition=%wide.region_8.9_spmd, body=%wide.region_7.8_spmd.sunk | while | flops 231459 | bytes 938621 | solution.py:144
  789.9 53.0 %all_to_all.11 = f32[16,32,512]{2,1,0:T(8,128)S(1)} all-to-all(f32[16,32,512]{2,1,0:T(8,128)S(1)} %broadcast_in_dim.122), channel_id=1, replica_groups=mesh['tm'=32,'col'=16] {'col'}, dimensions={0} | all-to-all | bytes 2097152 | tf_op jit(solution)/shard_map/all_to_all | solution.py:30
  842.9 7.7 collective-permute-start.12
  850.6 10.8 collective-permute-done.12
  861.4 1.8 convolution_select_fusion.3
  863.2 4.9 collective-permute-start.14
  868.2 22.9 %collective-permute-done.14 = f32[512,512]{1,0:T(8,128)} collective-permute-done((f32[512,512]{1,0:T(8,128)S(1)}, f32[512,512]{1,0:T(8,128)}, u32[]{:S(2)}, u32[]{:S(2)}) %collective-permute-start.14) | collective-permute-done | bytes 1048608 | tf_op jit(solution)/shard_map/ppermute | solution.py:19
  891.1 3.1 convolution_select_fusion.2
  894.2 7.1 collective-permute-start.16
  901.3 1.9 collective-permute-start.10
  903.3 3.6 collective-permute-done.10
  907.5 1.9 collective-permute-start.11
  909.4 17.3 %collective-permute-done.11 = f32[512]{0:T(512)S(1)} collective-permute-done((f32[512]{0:T(512)S(1)}, f32[512]{0:T(512)S(1)}, u32[]{:S(2)}, u32[]{:S(2)}) %collective-permute-start.11) | collective-permute-done | bytes 2080 | tf_op jit(solution)/shard_map/ppermute | solution.py:19
  927.3 3.1 convolution_select_fusion.1
  930.4 4.4 collective-permute-start.18
  934.8 5.2 collective-permute-start.13
  940.0 15.8 %collective-permute-done.13 = f32[512]{0:T(512)S(1)} collective-permute-done((f32[512]{0:T(512)S(1)}, f32[512]{0:T(512)S(1)}, u32[]{:S(2)}, u32[]{:S(2)}) %collective-permute-start.13) | collective-permute-done | bytes 2080 | tf_op jit(solution)/shard_map/ppermute | solution.py:19
  956.4 2.1 collective-permute-start.15
  958.6 2.5 collective-permute-done.15
  961.6 1.3 collective-permute-start.17
  963.0 1.9 convolution_select_fusion
  964.8 2.7 collective-permute-done.17
  968.1 3.4 collective-permute-start.19
  971.5 8.1 collective-permute-done.19
  979.6 189.1 %while.71 = (s32[]{:T(128)}, f32[512]{0:T(512)S(1)}, f32[16,512]{1,0:T(8,128)S(1)}, f32[16,512]{1,0:T(8,128)S(1)}, f32[16,512]{1,0:T(8,128)S(1)}, /*index=5*/f32...) while((s32[]{:T(128)}, f32[512]{0:T(512)S(1)}, ...), condition=%wide.region_10.11_spmd, body=%wide.region_9.10_spmd.sunk | while | flops 18467 | bytes 78449 | solution.py:152
  (801 shorter events, 314.9 us)
Async XLA Ops:
  298.5 19.7 %collective-permute-start.2 = (f32[512,512]{1,0:T(8,128)S(1)}, f32[512,512]{1,0:T(8,128)S(1)}, u32[]{:S(2)}, u32[]{:S(2)}) collective-permute-start(f32[512,512]{1,0:T(8,128)S(1)} %bitcast.368), channel_id=1, source_target_pairs={{0,16},{16,32},{32,48},{48,64},{64,80},{80,96},{96,112},{112,128},... | collective-permute-start | bytes 3145736 | tf_op jit(solution)/shard_map/ppermute | solution.py:19
  320.0 24.9 %collective-permute-start.4 = (f32[512,512]{1,0:T(8,128)S(1)}, f32[512,512]{1,0:T(8,128)}, u32[]{:S(2)}, u32[]{:S(2)}) collective-permute-start(f32[512,512]{1,0:T(8,128)S(1)} %convolution_select_fusion.7), channel_id=1, source_target_pairs={{0,32},{16,48},{32,64},{48,80},{64,96},{80,112},{96,128},{112,144}... | collective-permute-start | bytes 3145736 | tf_op jit(solution)/shard_map/ppermute | solution.py:19
  348.0 29.5 %collective-permute-start.6 = (f32[512,512]{1,0:T(8,128)S(1)}, f32[512,512]{1,0:T(8,128)}, u32[]{:S(2)}, u32[]{:S(2)}) collective-permute-start(f32[512,512]{1,0:T(8,128)S(1)} %convolution_select_fusion.6), channel_id=1, source_target_pairs={{0,64},{16,80},{32,96},{48,112},{64,128},{80,144},{96,160},{112,17... | collective-permute-start | bytes 3145736 | tf_op jit(solution)/shard_map/ppermute | solution.py:19
  351.6 8.2 collective-permute-start
  360.4 16.5 %collective-permute-start.1 = (f32[512]{0:T(512)S(1)}, f32[512]{0:T(512)S(1)}, u32[]{:S(2)}, u32[]{:S(2)}) collective-permute-start(f32[512]{0:T(512)S(1)} %add_select_fusion.9), channel_id=1, source_target_pairs={{0,32},{16,48},{32,64},{48,80},{64,96},{80,112},{96,128},{112,144}... | collective-permute-start | bytes 6152 | tf_op jit(solution)/shard_map/ppermute | solution.py:19
  380.6 33.4 %collective-permute-start.8 = (f32[512,512]{1,0:T(8,128)S(1)}, f32[512,512]{1,0:T(8,128)S(1)}, u32[]{:S(2)}, u32[]{:S(2)}) collective-permute-start(f32[512,512]{1,0:T(8,128)S(1)} %convolution_select_fusion.5), channel_id=1, source_target_pairs={{0,128},{16,144},{32,160},{48,176},{64,192},{80,208},{96,224},{112... | collective-permute-start | bytes 3145736 | tf_op jit(solution)/shard_map/ppermute | solution.py:19
  383.7 21.5 %collective-permute-start.3 = (f32[512]{0:T(512)S(1)}, f32[512]{0:T(512)S(1)}, u32[]{:S(2)}, u32[]{:S(2)}) collective-permute-start(f32[512]{0:T(512)S(1)} %add_select_fusion.8), channel_id=1, source_target_pairs={{0,64},{16,80},{32,96},{48,112},{64,128},{80,144},{96,160},{112,17... | collective-permute-start | bytes 6152 | tf_op jit(solution)/shard_map/ppermute | solution.py:19
  405.8 4.3 collective-permute-start.5
  410.8 14.0 %copy-start.4 = (f32[512]{0:T(512)S(1)}, f32[512]{0:T(512)}, u32[]{:S(2)}) copy-start(f32[512]{0:T(512)} %param.16) | copy-start | bytes 6148
  410.8 14.1 %copy-start = (s32[16,4]{0,1:T(4,128)S(1)}, s32[16,4]{0,1:T(4,128)}, u32[]{:S(2)}) copy-start(s32[16,4]{0,1:T(4,128)} %get-tuple-element.1443) | copy-start | bytes 772
  410.8 5.0 collective-permute-start.7
  416.5 8.4 collective-permute-start.9
  424.9 174.3 %copy-start.3 = (f32[16,512]{1,0:T(8,128)S(1)}, f32[16,512]{1,0:T(8,128)}, u32[]{:S(2)}) copy-start(f32[16,512]{1,0:T(8,128)} %param.23) | copy-start | bytes 98308
  599.1 0.6 copy-start.1
  842.9 18.5 %collective-permute-start.12 = (f32[512,512]{1,0:T(8,128)S(1)}, f32[512,512]{1,0:T(8,128)S(1)}, u32[]{:S(2)}, u32[]{:S(2)}) collective-permute-start(f32[512,512]{1,0:T(8,128)S(1)} %bitcast.371), channel_id=1, source_target_pairs={{16,0},{32,16},{48,32},{64,48},{80,64},{96,80},{112,96},{128,112},... | collective-permute-start | bytes 3145736 | tf_op jit(solution)/shard_map/ppermute | solution.py:19
  863.2 27.9 %collective-permute-start.14 = (f32[512,512]{1,0:T(8,128)S(1)}, f32[512,512]{1,0:T(8,128)}, u32[]{:S(2)}, u32[]{:S(2)}) collective-permute-start(f32[512,512]{1,0:T(8,128)S(1)} %convolution_select_fusion.3), channel_id=1, source_target_pairs={{32,0},{48,16},{64,32},{80,48},{96,64},{112,80},{128,96},{144,112}... | collective-permute-start | bytes 3145736 | tf_op jit(solution)/shard_map/ppermute | solution.py:19
  894.2 33.1 %collective-permute-start.16 = (f32[512,512]{1,0:T(8,128)S(1)}, f32[512,512]{1,0:T(8,128)}, u32[]{:S(2)}, u32[]{:S(2)}) collective-permute-start(f32[512,512]{1,0:T(8,128)S(1)} %convolution_select_fusion.2), channel_id=1, source_target_pairs={{64,0},{80,16},{96,32},{112,48},{128,64},{144,80},{160,96},{176,11... | collective-permute-start | bytes 3145736 | tf_op jit(solution)/shard_map/ppermute | solution.py:19
  901.3 5.5 collective-permute-start.10
  907.5 19.2 %collective-permute-start.11 = (f32[512]{0:T(512)S(1)}, f32[512]{0:T(512)S(1)}, u32[]{:S(2)}, u32[]{:S(2)}) collective-permute-start(f32[512]{0:T(512)S(1)} %add_select_fusion.4), channel_id=1, source_target_pairs={{32,0},{48,16},{64,32},{80,48},{96,64},{112,80},{128,96},{144,112}... | collective-permute-start | bytes 6152 | tf_op jit(solution)/shard_map/ppermute | solution.py:19
  930.4 32.6 %collective-permute-start.18 = (f32[512,512]{1,0:T(8,128)S(1)}, f32[512,512]{1,0:T(8,128)S(1)}, u32[]{:S(2)}, u32[]{:S(2)}) collective-permute-start(f32[512,512]{1,0:T(8,128)S(1)} %convolution_select_fusion.1), channel_id=1, source_target_pairs={{128,0},{144,16},{160,32},{176,48},{192,64},{208,80},{224,96},{240... | collective-permute-start | bytes 3145736 | tf_op jit(solution)/shard_map/ppermute | solution.py:19
  934.8 21.0 %collective-permute-start.13 = (f32[512]{0:T(512)S(1)}, f32[512]{0:T(512)S(1)}, u32[]{:S(2)}, u32[]{:S(2)}) collective-permute-start(f32[512]{0:T(512)S(1)} %add_select_fusion.3), channel_id=1, source_target_pairs={{64,0},{80,16},{96,32},{112,48},{128,64},{144,80},{160,96},{176,11... | collective-permute-start | bytes 6152 | tf_op jit(solution)/shard_map/ppermute | solution.py:19
  956.4 4.6 collective-permute-start.15
  961.6 5.8 collective-permute-start.17
  968.1 11.5 collective-permute-start.19
  1168.7 0.6 copy-start.2
where the time goes:
time: 1190 us; the launch traced here: 1170 us
  loops' own time  483 us (41%)
  other arithmetic  159 us (13%)
  waiting for transfers between devices  157 us (13%)
  blocking collectives  115 us (10%)
  local copies, waits for them, and re-layouts  95.6 us (8%)
  starting transfers between devices  80.3 us (7%)
  matrix products  79.6 us (7%)
    another operation x1, loops' own time, on_device(): _, smoothed = lax.scan(backward, top_state, smooth_inputs, reverse=True)  162 us
    another operation x1, loops' own time, build_smooth(): lax.scan(grow, (seed_panel, seed_state), smooth_inputs, reverse=True)[0]  160 us
    ppermute x20, waiting for transfers between devices, passed_along(): return lax.ppermute(block, axis, route)  157 us
    all_to_all x2, blocking collectives, sent_to_all(): return lax.all_to_all(copies, axis, split_axis=0, concat_axis=0, tiled=True)  115 us
    another operation x1, loops' own time, build_filter(): return lax.scan(grow, (seed_panel, seed_state), filter_inputs)[0]  80.5 us
    ppermute x20, starting transfers between devices, passed_along(): return lax.ppermute(block, axis, route)  80.3 us
    another operation x1, loops' own time, on_device(): _, filtered = lax.scan(forward, begin_state, filter_inputs)  80.2 us
    dot_general x48, matrix products, observe(): return corrected - jnp.dot(innovation, gains, precision=HIGHEST_PRECISION)  53.9 us
  transfers between devices with their start and end apart: 20, of which 15 were waited for; matrix products, arithmetic and copies ran while one was open for 1% of the time, Pallas kernels for 0%

commit v1 on v0

v1 whole, which is shorter than its diff:
```python
import functools

import jax
import jax.numpy as jnp
from jax import lax
from jax.experimental import pallas as pl
from jax.experimental.pallas import tpu as pltpu
from jax.sharding import PartitionSpec as P

N = 512
OBS = 64
BANDS = 4
DIFFUSION = 0.25
RELAXATION = 0.02
ROWS = N + 8
F32 = jnp.float32
BF16 = jnp.bfloat16
NT = (((1,), (1,)), ((), ()))
NN = (((1,), (0,)), ((), ()))


def lanes(rows):
    return lax.broadcasted_iota(jnp.int32, (rows, N), 1)


def back(off):
    return jnp.where(off > 0, N - off, -off)


def step_weights(offs, up, courant):
    reach = jnp.full_like(up, offs[0])
    for band in range(1, BANDS):
        reach = jnp.where(up == band, offs[band], reach)
    at = lanes(1) + reach
    inside = (at >= 0) & (at < N)
    return 1.0 - courant - DIFFUSION, jnp.where(inside, courant, 0.0)


def neighbours(v):
    lane = lanes(1)
    left = jnp.where(lane > 0, 0.5 * DIFFUSION, 0.0)
    right = jnp.where(lane < N - 1, 0.5 * DIFFUSION, 0.0)
    return right * pltpu.roll(v, N - 1, 1) + left * pltpu.roll(v, 1, 1)


def transition(v, offs, up, centre, adv):
    moved = pltpu.roll(v, back(offs[0]), 1)
    for band in range(1, BANDS):
        moved = jnp.where(up == band, pltpu.roll(v, back(offs[band]), 1), moved)
    return centre * v + neighbours(v) + adv * moved


def transpose_apply(v, offs, up, centre, adv):
    total = centre * v + neighbours(v)
    out = adv * v
    for band in range(BANDS):
        total = total + pltpu.roll(jnp.where(up == band, out, 0.0), back(-offs[band]), 1)
    return total


def split2(v):
    hi = v.astype(BF16)
    return hi, (v - hi.astype(F32)).astype(BF16)


def split3(v):
    hi = v.astype(BF16)
    rest = v - hi.astype(F32)
    mid = rest.astype(BF16)
    return hi, mid, (rest - mid.astype(F32)).astype(BF16)


def dot(a, b, dims=NN):
    return lax.dot_general(a, b, dims, preferred_element_type=F32)


def dot3(a, b):
    ah, al = split2(a)
    bh, bl = split2(b)
    return dot(ah, bh) + (dot(ah, bl) + dot(al, bh))


def observed_part(p, s4):
    hi, mid, lo = split3(p)
    return dot(hi, s4, NT) + (dot(mid, s4, NT) + dot(lo, s4, NT))


def gain_rows(s, gains):
    hi, lo = split2(RELAXATION * s.astype(F32) + gains)
    return jnp.concatenate([hi, hi, lo, lo], axis=0)


def correction(e4, kk):
    hi, lo = split2(e4)
    lane = lax.broadcasted_iota(jnp.int32, e4.shape, 1)
    odd = (lane // OBS) % 2 == 1
    return dot(jnp.where(odd, lo.astype(F32), hi.astype(F32)).astype(BF16), kk)


def one_hots(obs_t_ref, s_ref, steps):
    lane = lanes(OBS)
    for k in range(steps):
        s_ref[k] = jnp.where(obs_t_ref[:, k : k + 1] == lane, 1.0, 0.0).astype(BF16)


def read_step(k, offs_ref, up_ref, c_ref):
    offs = [offs_ref[k, band] for band in range(BANDS)]
    up = up_ref[pl.ds(k, 1), :]
    centre, adv = step_weights(offs, up, c_ref[pl.ds(k, 1), :])
    return offs, up, centre, adv


def vmem():
    return pl.BlockSpec(memory_space=pltpu.VMEM)


def smem():
    return pl.BlockSpec(memory_space=pltpu.SMEM)


def filter_map(offsets, upwind, courant, obs_t, gains, y4):
    steps, chunk = offsets.shape[0], 128

    def kernel(offs_ref, up_ref, c_ref, obs_t_ref, gains_ref, y4_ref, map_ref, s_ref):
        one_hots(obs_t_ref, s_ref, steps)
        row = lax.broadcasted_iota(jnp.int32, (ROWS, N), 0)
        map_ref[...] = jnp.where(row == lanes(ROWS), 1.0, 0.0)
        first = lax.broadcasted_iota(jnp.int32, (8, 1), 0) == 0

        def one(k, carry):
            offs, up, centre, adv = read_step(k, offs_ref, up_ref, c_ref)
            s = s_ref[k]
            kk = gain_rows(s, gains_ref[k])
            s4 = jnp.concatenate([s] * 4, axis=0)
            for r in range(0, N, chunk):
                at = pl.ds(r, chunk)
                p = transition(map_ref[at, :], offs, up, centre, adv)
                map_ref[at, :] = p - correction(observed_part(p, s4), kk)
            tail = pl.ds(N, 8)
            p = transition(map_ref[tail, :], offs, up, centre, adv)
            e4 = observed_part(p, s4) - jnp.where(first, y4_ref[pl.ds(k, 1), :], 0.0)
            map_ref[tail, :] = p - correction(e4, kk)
            return carry

        lax.fori_loop(0, steps, one, 0)

    return pl.pallas_call(
        kernel,
        out_shape=jax.ShapeDtypeStruct((ROWS, N), F32),
        in_specs=[smem()] + [vmem()] * 5,
        out_specs=vmem(),
        scratch_shapes=[pltpu.VMEM((steps, OBS, N), BF16)],
        cost_estimate=pl.CostEstimate(flops=16 * 10**9, bytes_accessed=4 << 20, transcendentals=0),
        name="filter_map",
    )(offsets, upwind, courant, obs_t, gains, y4)


def smoother_map(offsets, upwind, courant, smooth_gain):
    steps, chunk = offsets.shape[0], 64

    def kernel(offs_ref, up_ref, c_ref, sg_ref, map_ref):
        row = lax.broadcasted_iota(jnp.int32, (N, N), 0)
        map_ref[...] = jnp.where(row == lanes(N), 1.0, 0.0)

        def one(i, carry):
            k = steps - 1 - i
            offs, up, centre, adv = read_step(k, offs_ref, up_ref, c_ref)
            gain = sg_ref[pl.ds(k, 1), :]
            for r in range(0, N, chunk):
                at = pl.ds(r, chunk)
                map_ref[at, :] = gain * transpose_apply(map_ref[at, :], offs, up, centre, adv)
            return carry

        lax.fori_loop(0, steps, one, 0)

    return pl.pallas_call(
        kernel,
        out_shape=jax.ShapeDtypeStruct((N, N), F32),
        in_specs=[smem()] + [vmem()] * 3,
        out_specs=vmem(),
        cost_estimate=pl.CostEstimate(flops=8 * 10**9, bytes_accessed=1 << 20, transcendentals=0),
        name="smoother_map",
    )(offsets, upwind, courant, smooth_gain)


def forward(offsets, upwind, courant, obs_t, gains, y4, start):
    steps = offsets.shape[0]

    def kernel(offs_ref, up_ref, c_ref, obs_t_ref, gains_ref, y4_ref, start_ref, filt_ref, upd_ref, vec_ref, s_ref):
        one_hots(obs_t_ref, s_ref, steps)
        first = lax.broadcasted_iota(jnp.int32, (8, 1), 0) == 0
        vec_ref[...] = start_ref[...]

        def one(k, carry):
            offs, up, centre, adv = read_step(k, offs_ref, up_ref, c_ref)
            s = s_ref[k]
            kk = gain_rows(s, gains_ref[k])
            s4 = jnp.concatenate([s] * 4, axis=0)
            p = transition(vec_ref[...], offs, up, centre, adv)
            e4 = observed_part(p, s4) - jnp.where(first, y4_ref[pl.ds(k, 1), :], 0.0)
            update = -correction(e4, kk)
            vec_ref[...] = p + update
            filt_ref[pl.ds(k, 1), :] = (p + update)[0:1]
            upd_ref[pl.ds(k, 1), :] = update[0:1]
            return carry

        lax.fori_loop(0, steps, one, 0)

    out = jax.ShapeDtypeStruct((steps, N), F32)
    return pl.pallas_call(
        kernel,
        out_shape=(out, out),
        in_specs=[smem()] + [vmem()] * 6,
        out_specs=(vmem(), vmem()),
        scratch_shapes=[pltpu.VMEM((8, N), F32), pltpu.VMEM((steps, OBS, N), BF16)],
        cost_estimate=pl.CostEstimate(flops=4 * 10**9, bytes_accessed=2 << 20, transcendentals=0),
        name="forward",
    )(offsets, upwind, courant, obs_t, gains, y4, start)


def smooth(offsets, upwind, courant, smooth_gain, updates, filtered, top):
    steps = offsets.shape[0]

    def kernel(offs_ref, up_ref, c_ref, sg_ref, u_ref, x_ref, top_ref, out_ref, end_ref):
        def one(i, diff):
            k = steps - 1 - i
            offs, up, centre, adv = read_step(k, offs_ref, up_ref, c_ref)
            at = pl.ds(k, 1)
            out_ref[at, :] = x_ref[at, :] + diff[0:1]
            return sg_ref[at, :] * transpose_apply(diff + u_ref[at, :], offs, up, centre, adv)

        end_ref[...] = lax.fori_loop(0, steps, one, top_ref[...])

    return pl.pallas_call(
        kernel,
        out_shape=(jax.ShapeDtypeStruct((steps, N), F32), jax.ShapeDtypeStruct((8, N), F32)),
        in_specs=[smem()] + [vmem()] * 6,
        out_specs=(vmem(), vmem()),
        cost_estimate=pl.CostEstimate(flops=10**9, bytes_accessed=1 << 18, transcendentals=0),
        name="smooth",
    )(offsets, upwind, courant, smooth_gain, updates, filtered, top)


def compose(flag, mine, other):
    rows = mine.shape[0]

    def kernel(flag_ref, mine_ref, other_ref, out_ref):
        def product(a_ref, b_ref):
            bh, bl = split2(b_ref[0:N, :])
            for r in range(0, rows, 104 if rows == ROWS else 128):
                at = pl.ds(r, 104 if rows == ROWS else 128)
                ah, al = split2(a_ref[at, :])
                out_ref[at, :] = dot(ah, bh) + (dot(ah, bl) + dot(al, bh))
            if rows == ROWS:
                out_ref[N:ROWS, :] = out_ref[N:ROWS, :] + b_ref[N:ROWS, :]

        @pl.when(flag_ref[0] == 1)
        def _():
            product(other_ref, mine_ref)

        @pl.when(flag_ref[0] == 0)
        def _():
            product(mine_ref, other_ref)

    return pl.pallas_call(
        kernel,
        out_shape=jax.ShapeDtypeStruct((rows, N), F32),
        in_specs=[smem(), vmem(), vmem()],
        out_specs=vmem(),
        cost_estimate=pl.CostEstimate(flops=10**9, bytes_accessed=3 << 20, transcendentals=0),
        name="compose",
    )(flag, mine, other)


def through(state, maps, offset):
    def kernel(v_ref, m_ref, o_ref, out_ref):
        out_ref[...] = dot3(v_ref[...], m_ref[0:N, :]) + o_ref[...]

    return pl.pallas_call(
        kernel,
        out_shape=jax.ShapeDtypeStruct((8, N), F32),
        in_specs=[vmem()] * 3,
        out_specs=vmem(),
        cost_estimate=pl.CostEstimate(flops=10**8, bytes_accessed=1 << 20, transcendentals=0),
        name="through",
    )(state, maps, offset)


def on_device(initial, offsets, upwind, courant, obs_cells, gains, observed, smooth_gain):
    place = lax.axis_index("tm")
    x, y, core = place // 8, (place // 2) % 4, place % 2

    def moved(values, to, senders):
        return lax.ppermute(values, "tm", [(i, to(i)) for i in range(32) if senders(i)])

    even = lambda i: i % 2 == 0
    odd = lambda i: i % 2 == 1
    flag = lambda on: on.astype(jnp.int32).reshape(1)
    never = jnp.zeros((1,), jnp.int32)

    obs_t = obs_cells.T
    y4 = jnp.tile(observed, (1, 4))
    start_row = jnp.broadcast_to(initial[None, :], (8, N))
    zeros = jnp.zeros((8, N), F32)

    fmap = filter_map(offsets, upwind, courant, obs_t, gains, y4)
    fmap_odd = moved(fmap, lambda i: i - 1, odd)
    smap = smoother_map(offsets, upwind, courant, smooth_gain)
    fpair = compose(never, fmap, fmap_odd)
    fpair_other = moved(fpair, lambda i: i ^ 2, even)
    smap_even = moved(smap, lambda i: i + 1, even)
    spair = compose(never, smap, smap_even)
    fquad = compose(flag(y % 2 == 1), fpair, fpair_other)
    fquad_other = moved(fquad, lambda i: i ^ 4, even)
    spair_other = moved(spair, lambda i: i ^ 2, odd)
    foct = compose(flag(y >= 2), fquad, fquad_other)
    squad = compose(flag(y % 2 == 0), spair, spair_other)
    squad_other = moved(squad, lambda i: i ^ 4, odd)

    state = start_row
    for hop in range(3):
        sent = through(state, foct, foct[N:ROWS])
        got = moved(sent, lambda i: i + 8, lambda i: even(i) and i < 24)
        state = jnp.where(x == hop + 1, got, state)
    soct = compose(flag(y < 2), squad, squad_other)
    state = jnp.where(y >= 2, through(state, fquad_other, fquad_other[N:ROWS]), state)
    state = jnp.where(y % 2 == 1, through(state, fpair_other, fpair_other[N:ROWS]), state)
    sent = through(state, fmap, fmap[N:ROWS])
    got = moved(sent, lambda i: i + 1, even)
    state = jnp.where(core == 1, got, state)
    filtered, updates = forward(offsets, upwind, courant, obs_t, gains, y4, state)

    steps = (offsets, upwind, courant, smooth_gain, updates, filtered)
    own = smooth(*steps, zeros)[1]
    pair = through(own, smap_even, moved(own, lambda i: i + 1, even))
    pair_other = moved(pair, lambda i: i ^ 2, odd)
    later = y % 2 == 0
    quad = jnp.where(
        later, through(pair_other, spair, pair), through(pair, spair_other, pair_other)
    )
    quad_other = moved(quad, lambda i: i ^ 4, odd)
    oct_ = jnp.where(
        y < 2, through(quad_other, squad, quad), through(quad, squad_other, quad_other)
    )
    top = zeros
    for hop in range(3):
        sent = through(top, soct, oct_)
        got = moved(sent, lambda i: i - 8, lambda i: odd(i) and i >= 8)
        top = jnp.where(x == 2 - hop, got, top)
    top = jnp.where(y < 2, through(top, squad_other, quad_other), top)
    top = jnp.where(later, through(top, spair_other, pair_other), top)
    sent = through(top, smap, own)
    got = moved(sent, lambda i: i - 1, odd)
    top = jnp.where(core == 0, got, top)
    smoothed = smooth(*steps, top)[0]
    return filtered, smoothed


def solution(mesh):
    row = P("tm", None)
    in_specs = (P(), row, row, row, row, P("tm", None, None), row, row)
    return jax.shard_map(on_device, mesh=mesh, in_specs=in_specs, out_specs=(row, row), check_vma=False)
```

time: 1190 us -> 284 us (0.24)
  the two profiles are of different devices: /device:TPU:43 before, /device:TPU:1 now
where the time goes in v1:
time: 284 us; the launch traced here: 283 us
  Pallas kernels  170 us (60%)
  waiting for transfers between devices  50.1 us (18%)
  starting transfers between devices  31.9 us (11%)
  local copies, waits for them, and re-layouts  18.4 us (6%)
  other arithmetic  10.8 us (4%)
    pallas_call x1, Pallas kernels, filter_map(): pl.pallas_call(kernel, out_shape=jax.ShapeDtypeStruct((ROWS, N), F32), in...  56.5 us
    ppermute x17, waiting for transfers between devices, moved(): lax.ppermute(values, 'tm', [(i, to(i)) for i in range(32) if senders(i)])  50.1 us
    pallas_call x17, Pallas kernels, through(): pl.pallas_call(kernel, out_shape=jax.ShapeDtypeStruct((8, N), F32), in_sp...  37 us
    pallas_call x1, Pallas kernels, smoother_map(): pl.pallas_call(kernel, out_shape=jax.ShapeDtypeStruct((N, N), F32), in_sp...  36.6 us
    ppermute x17, starting transfers between devices, moved(): lax.ppermute(values, 'tm', [(i, to(i)) for i in range(32) if senders(i)])  31.9 us
    pallas_call x6, Pallas kernels, compose(): pl.pallas_call(kernel, out_shape=jax.ShapeDtypeStruct((rows, N), F32), in...  22.1 us
    pallas_call x1, Pallas kernels, forward(): pl.pallas_call(kernel, out_shape=(out, out), in_specs=[smem()] + [vmem()]...  11.8 us
    unnamed x44, local copies, waits for them, and re-layouts  10.6 us
  transfers between devices with their start and end apart: 17, of which 9 were waited for; matrix products, arithmetic and copies ran while one was open for 4% of the time, Pallas kernels for 32%

profile of v1, /device:TPU:1, one launch (start us, length us, event | category | flops | bytes accessed | tf_op | source)
XLA Modules:
  0.0 282.6 jit_solution(10422526368019549726)
XLA Ops:
  0.6 1.4 copy.12.offs_ref
  3.4 1.4 copy.10
  4.8 56.5 %filter_map.1.mine_ref.m_ref = f32[520,512]{1,0:T(8,128)} custom-call(s32[16,4]{1,0:T(8,128)} %copy.12.offs_ref, s32[16,512]{1,0:T(8,128)} %up_ref.9, f32[16,512]{1,0:T(8,128)} %c_ref.9, s32[64,16]{1,0:T(8,128)} %bitcast.5, f32[16,64,512]{2,1,0:T(8,128)} %gains_ref.3, f32[16,256]{1,0:T(8,128)} %tile.10.y4_ref), custom_call_target="tpu_custom_call" | custom-call | flops 16000000000 | bytes 4194304 | tf_op jit(solution)/shard_map/filter_map/pallas_call | solution.py:147
  61.3 8.8 %collective-permute-start = (f32[520,512]{1,0:T(8,128)}, f32[520,512]{1,0:T(8,128)S(1)}, u32[]{:S(2)}, u32[]{:S(2)}) collective-permute-start(f32[520,512]{1,0:T(8,128)} %filter_map.1.mine_ref.m_ref), channel_id=1, source_target_pairs={{16,0},{48,32},{80,64},{112,96},{144,128},{176,160},{208,192},{240... | collective-permute-start | bytes 3194888 | tf_op jit(solution)/shard_map/ppermute | solution.py:294
  70.1 2.4 collective-permute-done.other_ref
  73.5 3.8 %compose.6.mine_ref = f32[520,512]{1,0:T(8,128)} custom-call(s32[1]{0:T(128)} %constant.65.clone.1.flag_ref, f32[520,512]{1,0:T(8,128)} %filter_map.1.mine_ref.m_ref, f32[520,512]{1,0:T(8,128)} %copy-done.20), custom_call_target="tpu_custom_call" | custom-call | flops 1000000000 | bytes 3145728 | tf_op jit(solution)/shard_map/compose/pallas_call | solution.py:265
  78.1 36.6 %smoother_map.1.mine_ref.m_ref = f32[512,512]{1,0:T(8,128)} custom-call(s32[16,4]{1,0:T(8,128)} %copy.12.offs_ref, s32[16,512]{1,0:T(8,128)} %up_ref.9, f32[16,512]{1,0:T(8,128)} %c_ref.9, f32[16,512]{1,0:T(8,128)} %sg_ref.5), custom_call_target="tpu_custom_call" | custom-call | flops 8000000000 | bytes 1048576 | tf_op jit(solution)/shard_map/smoother_map/pallas_call | solution.py:176
  117.1 3.8 %compose.7.mine_ref = f32[520,512]{1,0:T(8,128)} custom-call(s32[1]{0:T(128)} %bitcast.2.flag_ref, f32[520,512]{1,0:T(8,128)} %compose.6.mine_ref, f32[520,512]{1,0:T(8,128)} %copy-done.2), custom_call_target="tpu_custom_call" | custom-call | flops 1000000000 | bytes 3145728 | tf_op jit(solution)/shard_map/compose/pallas_call | solution.py:265
  122.6 3.5 %compose.9.mine_ref.m_ref = f32[512,512]{1,0:T(8,128)} custom-call(s32[1]{0:T(128)} %constant.65.clone.1.flag_ref, f32[512,512]{1,0:T(8,128)} %smoother_map.1.mine_ref.m_ref, f32[512,512]{1,0:T(8,128)} %copy-done.4), custom_call_target="tpu_custom_call" | custom-call | flops 1000000000 | bytes 3145728 | tf_op jit(solution)/shard_map/compose/pallas_call | solution.py:265
  126.2 1.9 collective-permute-start.8
  129.2 3.8 %compose.8.m_ref = f32[520,512]{1,0:T(8,128)} custom-call(s32[1]{0:T(128)} %bitcast.1.flag_ref, f32[520,512]{1,0:T(8,128)} %compose.7.mine_ref, f32[520,512]{1,0:T(8,128)} %copy-done.3), custom_call_target="tpu_custom_call" | custom-call | flops 1000000000 | bytes 3145728 | tf_op jit(solution)/shard_map/compose/pallas_call | solution.py:265
  134.9 2.2 through.17
  138.4 2.2 through.18
  141.2 1.3 slice.21.o_ref
  143.2 2.2 through.19
  146.0 4.4 %collective-permute-done.8.other_ref.m_ref = f32[512,512]{1,0:T(8,128)S(1)} collective-permute-done((f32[512,512]{1,0:T(8,128)}, f32[512,512]{1,0:T(8,128)S(1)}, u32[]{:S(2)}, u32[]{:S(2)}) %collective-permute-start.8) | collective-permute-done | bytes 1048608 | tf_op jit(solution)/shard_map/ppermute | solution.py:294
  151.4 3.6 %compose.10.mine_ref.m_ref = f32[512,512]{1,0:T(8,128)} custom-call(s32[1]{0:T(128)} %bitcast.4.flag_ref, f32[512,512]{1,0:T(8,128)} %compose.9.mine_ref.m_ref, f32[512,512]{1,0:T(8,128)} %copy-done), custom_call_target="tpu_custom_call" | custom-call | flops 1000000000 | bytes 3145728 | tf_op jit(solution)/shard_map/compose/pallas_call | solution.py:265
  155.0 1.9 collective-permute-start.9
  156.9 1.3 slice.20.o_ref
  160.1 2.2 through.20
  162.9 2.2 through.21
  165.7 2.2 through.22
  169.2 27.9 %collective-permute-done.6 = f32[8,512]{1,0:T(8,128)S(1)} collective-permute-done((f32[8,512]{1,0:T(8,128)}, f32[8,512]{1,0:T(8,128)S(1)}, u32[]{:S(2)}, u32[]{:S(2)}) %collective-permute-start.6) | collective-permute-done | bytes 16416 | tf_op jit(solution)/shard_map/ppermute | solution.py:294
  197.7 11.8 %forward.1 = (f32[16,512]{1,0:T(8,128)}, f32[16,512]{1,0:T(8,128)}) custom-call(s32[16,4]{1,0:T(8,128)} %copy.12.offs_ref, s32[16,512]{1,0:T(8,128)} %up_ref.9, f32[16,512]{1,0:T(8,128)} %c_ref.9, s32[64,16]{1,0:T(8,128)} %bitcast.6, f32[16,64,512]{2,1,0:T(8,128)} %gains_ref.3, f32[16,256]{1,0:T(8,128)} %tile.10.y4_ref, ...), custom_call_target="tpu_custom_call" | custom-call | flops 4000000000 | bytes 2097152 | tf_op jit(solution)/shard_map/forward/pallas_call | solution.py:210
  210.1 3.1 %smooth.2 = (f32[16,512]{1,0:T(8,128)}, f32[8,512]{1,0:T(8,128)}) custom-call(s32[16,4]{1,0:T(8,128)} %copy.12.offs_ref, s32[16,512]{1,0:T(8,128)} %up_ref.9, f32[16,512]{1,0:T(8,128)} %c_ref.9, f32[16,512]{1,0:T(8,128)} %sg_ref.5, f32[16,512]{1,0:T(8,128)} %get-tuple-element.7.u_ref, f32[16,512]{1,0:T(8,128)} %get-tuple-element.4.x_ref, ...), custom_call_target="tpu_custom_call" | custom-call | flops 1000000000 | bytes 262144 | tf_op jit(solution)/shard_map/smooth/pallas_call | solution.py:234
  214.5 2.0 collective-permute-done.10.o_ref
  217.1 2.2 through.23.o_ref.v_ref
  219.3 2.4 collective-permute-start.11
  221.7 2.2 collective-permute-done.11.v_ref.o_ref
  224.5 2.2 through.25
  226.7 2.2 through.24
  229.6 4.5 %collective-permute-start.12 = (f32[8,512]{1,0:T(8,128)S(1)}, f32[8,512]{1,0:T(8,128)S(1)}, u32[]{:S(2)}, u32[]{:S(2)}) collective-permute-start(f32[8,512]{1,0:T(8,128)S(1)} %broadcast_select_fusion.6.o_ref.v_ref), channel_id=1, source_target_pairs={{16,80},{48,112},{80,16},{112,48},{144,208},{176,240},{208,144},{2... | collective-permute-start | bytes 49160 | tf_op jit(solution)/shard_map/ppermute | solution.py:294
  235.1 3.5 %compose.11.m_ref = f32[512,512]{1,0:T(8,128)} custom-call(s32[1]{0:T(128)} %bitcast.3.flag_ref, f32[512,512]{1,0:T(8,128)} %compose.10.mine_ref.m_ref, f32[512,512]{1,0:T(8,128)} %copy-done.1), custom_call_target="tpu_custom_call" | custom-call | flops 1000000000 | bytes 3145728 | tf_op jit(solution)/shard_map/compose/pallas_call | solution.py:265
  239.3 2.2 through.27
  241.4 2.2 through.26
  243.6 1.3 broadcast_select_fusion.4.o_ref
  244.9 2.2 through.28
  248.4 3.4 %collective-permute-done.13 = f32[8,512]{1,0:T(8,128)S(1)} collective-permute-done((f32[8,512]{1,0:T(8,128)}, f32[8,512]{1,0:T(8,128)S(1)}, u32[]{:S(2)}, u32[]{:S(2)}) %collective-permute-start.13) | collective-permute-done | bytes 16416 | tf_op jit(solution)/shard_map/ppermute | solution.py:294
  252.4 2.2 through.29
  255.8 3.4 %collective-permute-done.14 = f32[8,512]{1,0:T(8,128)S(1)} collective-permute-done((f32[8,512]{1,0:T(8,128)}, f32[8,512]{1,0:T(8,128)S(1)}, u32[]{:S(2)}, u32[]{:S(2)}) %collective-permute-start.14) | collective-permute-done | bytes 16416 | tf_op jit(solution)/shard_map/ppermute | solution.py:294
  259.9 2.2 through.30
  263.3 3.4 %collective-permute-done.15 = f32[8,512]{1,0:T(8,128)S(1)} collective-permute-done((f32[8,512]{1,0:T(8,128)}, f32[8,512]{1,0:T(8,128)S(1)}, u32[]{:S(2)}, u32[]{:S(2)}) %collective-permute-start.15) | collective-permute-done | bytes 16416 | tf_op jit(solution)/shard_map/ppermute | solution.py:294
  267.3 2.2 through.31
  269.5 1.3 broadcast_select_fusion.3.v_ref
  270.8 2.2 through.32
  273.0 1.3 broadcast_select_fusion.5.v_ref
  274.3 2.2 through.33
  279.4 3.1 %smooth.3 = (f32[16,512]{1,0:T(8,128)}, f32[8,512]{1,0:T(8,128)}) custom-call(s32[16,4]{1,0:T(8,128)} %copy.12.offs_ref, s32[16,512]{1,0:T(8,128)} %up_ref.9, f32[16,512]{1,0:T(8,128)} %c_ref.9, f32[16,512]{1,0:T(8,128)} %sg_ref.5, f32[16,512]{1,0:T(8,128)} %get-tuple-element.7.u_ref, f32[16,512]{1,0:T(8,128)} %get-tuple-element.4.x_ref, ...), custom_call_target="tpu_custom_call" | custom-call | flops 1000000000 | bytes 262144 | tf_op jit(solution)/shard_map/smooth/pallas_call | solution.py:234
  (80 shorter events, 33.2 us)
Async XLA Ops:
  61.3 11.2 %collective-permute-start = (f32[520,512]{1,0:T(8,128)}, f32[520,512]{1,0:T(8,128)S(1)}, u32[]{:S(2)}, u32[]{:S(2)}) collective-permute-start(f32[520,512]{1,0:T(8,128)} %filter_map.1.mine_ref.m_ref), channel_id=1, source_target_pairs={{16,0},{48,32},{80,64},{112,96},{144,128},{176,160},{208,192},{240... | collective-permute-start | bytes 3194888 | tf_op jit(solution)/shard_map/ppermute | solution.py:294
  72.5 1.0 copy-start.20
  77.4 38.7 %collective-permute-start.1 = (f32[520,512]{1,0:T(8,128)}, f32[520,512]{1,0:T(8,128)S(1)}, u32[]{:S(2)}, u32[]{:S(2)}) collective-permute-start(f32[520,512]{1,0:T(8,128)} %compose.6.mine_ref), channel_id=1, source_target_pairs={{0,32},{32,0},{64,96},{96,64},{128,160},{160,128},{192,224},{224,1... | collective-permute-start | bytes 3194888 | tf_op jit(solution)/shard_map/ppermute | solution.py:294
  114.7 6.9 %collective-permute-start.7 = (f32[512,512]{1,0:T(8,128)}, f32[512,512]{1,0:T(8,128)S(1)}, u32[]{:S(2)}, u32[]{:S(2)}) collective-permute-start(f32[512,512]{1,0:T(8,128)} %smoother_map.1.mine_ref.m_ref), channel_id=1, source_target_pairs={{0,16},{32,48},{64,80},{96,112},{128,144},{160,176},{192,208},{224... | collective-permute-start | bytes 3145736 | tf_op jit(solution)/shard_map/ppermute | solution.py:294
  116.1 1.0 copy-start.2
  120.9 7.3 %collective-permute-start.2 = (f32[520,512]{1,0:T(8,128)}, f32[520,512]{1,0:T(8,128)S(1)}, u32[]{:S(2)}, u32[]{:S(2)}) collective-permute-start(f32[520,512]{1,0:T(8,128)} %compose.7.mine_ref), channel_id=1, source_target_pairs={{0,64},{32,96},{64,0},{96,32},{128,192},{160,224},{192,128},{224,1... | collective-permute-start | bytes 3194888 | tf_op jit(solution)/shard_map/ppermute | solution.py:294
  121.6 1.1 copy-start.4
  126.2 24.2 %collective-permute-start.8 = (f32[512,512]{1,0:T(8,128)}, f32[512,512]{1,0:T(8,128)S(1)}, u32[]{:S(2)}, u32[]{:S(2)}) collective-permute-start(f32[512,512]{1,0:T(8,128)} %compose.9.mine_ref.m_ref), channel_id=1, source_target_pairs={{16,48},{48,16},{80,112},{112,80},{144,176},{176,144},{208,240},{2... | collective-permute-start | bytes 3145736 | tf_op jit(solution)/shard_map/ppermute | solution.py:294
  128.2 1.0 copy-start.3
  129.2 5.2 %copy-start.18 = (f32[512]{0:T(512)S(1)}, f32[512]{0:T(512)}, u32[]{:S(2)}) copy-start(f32[512]{0:T(512)} %param.8) | copy-start | bytes 6148
  137.1 0.7 collective-permute-start.3
  140.6 2.0 collective-permute-start.4
  145.3 14.2 %collective-permute-start.5 = (f32[8,512]{1,0:T(8,128)}, f32[8,512]{1,0:T(8,128)S(1)}, u32[]{:S(2)}, u32[]{:S(2)}) collective-permute-start(f32[8,512]{1,0:T(8,128)} %through.19), channel_id=1, source_target_pairs={{0,128},{32,160},{64,192},{96,224},{128,256},{160,288},{192,320},{... | collective-permute-start | bytes 49160 | tf_op jit(solution)/shard_map/ppermute | solution.py:294
  150.4 1.0 copy-start
  151.4 8.1 %copy-start.8 = (f32[8,512]{1,0:T(8,128)S(1)}, f32[8,512]{1,0:T(8,128)}, u32[]{:S(2)}) copy-start(f32[8,512]{1,0:T(8,128)} %broadcast_select_fusion.9.v_ref) | copy-start | bytes 49156
  155.0 79.2 %collective-permute-start.9 = (f32[512,512]{1,0:T(8,128)}, f32[512,512]{1,0:T(8,128)S(1)}, u32[]{:S(2)}, u32[]{:S(2)}) collective-permute-start(f32[512,512]{1,0:T(8,128)} %compose.10.mine_ref.m_ref), channel_id=1, source_target_pairs={{16,80},{48,112},{80,16},{112,48},{144,208},{176,240},{208,144},{2... | collective-permute-start | bytes 3145736 | tf_op jit(solution)/shard_map/ppermute | solution.py:294
  160.1 2.2 copy-start.12
  162.9 2.2 copy-start.13
  165.7 31.4 %copy-start.9 = (f32[8,512]{1,0:T(8,128)S(1)}, f32[8,512]{1,0:T(8,128)}, u32[]{:S(2)}) copy-start(f32[8,512]{1,0:T(8,128)} %broadcast_select_fusion.12.v_ref) | copy-start | bytes 49156
  167.9 29.2 %collective-permute-start.6 = (f32[8,512]{1,0:T(8,128)}, f32[8,512]{1,0:T(8,128)S(1)}, u32[]{:S(2)}, u32[]{:S(2)}) collective-permute-start(f32[8,512]{1,0:T(8,128)} %through.22), channel_id=1, source_target_pairs={{0,16},{32,48},{64,80},{96,112},{128,144},{160,176},{192,208},{224... | collective-permute-start | bytes 49160 | tf_op jit(solution)/shard_map/ppermute | solution.py:294
  213.2 3.3 %collective-permute-start.10 = (f32[8,512]{1,0:T(8,128)}, f32[8,512]{1,0:T(8,128)S(1)}, u32[]{:S(2)}, u32[]{:S(2)}) collective-permute-start(f32[8,512]{1,0:T(8,128)} %get-tuple-element.8.v_ref.o_ref), channel_id=1, source_target_pairs={{0,16},{32,48},{64,80},{96,112},{128,144},{160,176},{192,208},{224... | collective-permute-start | bytes 49160 | tf_op jit(solution)/shard_map/ppermute | solution.py:294
  216.5 0.6 copy-start.19
  219.3 4.7 %collective-permute-start.11 = (f32[8,512]{1,0:T(8,128)}, f32[8,512]{1,0:T(8,128)S(1)}, u32[]{:S(2)}, u32[]{:S(2)}) collective-permute-start(f32[8,512]{1,0:T(8,128)} %through.23.o_ref.v_ref), channel_id=1, source_target_pairs={{16,48},{48,16},{80,112},{112,80},{144,176},{176,144},{208,240},{2... | collective-permute-start | bytes 49160 | tf_op jit(solution)/shard_map/ppermute | solution.py:294
  223.9 0.6 copy-start.5
  226.7 2.2 copy-start.16
  229.6 9.0 %copy-start.7 = (f32[8,512]{1,0:T(8,128)}, f32[8,512]{1,0:T(8,128)S(1)}, u32[]{:S(2)}) copy-start(f32[8,512]{1,0:T(8,128)S(1)} %broadcast_select_fusion.6.o_ref.v_ref) | copy-start | bytes 49156
  229.6 9.0 %collective-permute-start.12 = (f32[8,512]{1,0:T(8,128)S(1)}, f32[8,512]{1,0:T(8,128)S(1)}, u32[]{:S(2)}, u32[]{:S(2)}) collective-permute-start(f32[8,512]{1,0:T(8,128)S(1)} %broadcast_select_fusion.6.o_ref.v_ref), channel_id=1, source_target_pairs={{16,80},{48,112},{80,16},{112,48},{144,208},{176,240},{208,144},{2... | collective-permute-start | bytes 49160 | tf_op jit(solution)/shard_map/ppermute | solution.py:294
  234.1 1.0 copy-start.1
  238.7 0.6 copy-start.6
  241.4 2.2 copy-start.17
  247.1 4.7 %collective-permute-start.13 = (f32[8,512]{1,0:T(8,128)}, f32[8,512]{1,0:T(8,128)S(1)}, u32[]{:S(2)}, u32[]{:S(2)}) collective-permute-start(f32[8,512]{1,0:T(8,128)} %through.28), channel_id=1, source_target_pairs={{144,16},{176,48},{208,80},{240,112},{272,144},{304,176},{336,208}... | collective-permute-start | bytes 49160 | tf_op jit(solution)/shard_map/ppermute | solution.py:294
  254.6 4.7 %collective-permute-start.14 = (f32[8,512]{1,0:T(8,128)}, f32[8,512]{1,0:T(8,128)S(1)}, u32[]{:S(2)}, u32[]{:S(2)}) collective-permute-start(f32[8,512]{1,0:T(8,128)} %through.29), channel_id=1, source_target_pairs={{144,16},{176,48},{208,80},{240,112},{272,144},{304,176},{336,208}... | collective-permute-start | bytes 49160 | tf_op jit(solution)/shard_map/ppermute | solution.py:294
  259.8 6.9 %copy-start.10 = (f32[8,512]{1,0:T(8,128)S(1)}, f32[8,512]{1,0:T(8,128)}, u32[]{:S(2)}) copy-start(f32[8,512]{1,0:T(8,128)} %broadcast_select_fusion.8.v_ref) | copy-start | bytes 49156
  262.0 4.7 %collective-permute-start.15 = (f32[8,512]{1,0:T(8,128)}, f32[8,512]{1,0:T(8,128)S(1)}, u32[]{:S(2)}, u32[]{:S(2)}) collective-permute-start(f32[8,512]{1,0:T(8,128)} %through.30), channel_id=1, source_target_pairs={{144,16},{176,48},{208,80},{240,112},{272,144},{304,176},{336,208}... | collective-permute-start | bytes 49160 | tf_op jit(solution)/shard_map/ppermute | solution.py:294
  267.3 2.2 copy-start.14
  270.8 2.2 copy-start.15
  274.3 4.5 %copy-start.11 = (f32[8,512]{1,0:T(8,128)S(1)}, f32[8,512]{1,0:T(8,128)}, u32[]{:S(2)}) copy-start(f32[8,512]{1,0:T(8,128)} %broadcast_select_fusion.5.v_ref) | copy-start | bytes 49156
  276.5 2.3 collective-permute-start.16

commit v2 on v0

v2 whole, which is shorter than its diff:
```python
import jax
import jax.numpy as jnp
from jax import lax
from jax.experimental import pallas as pl
from jax.experimental.pallas import tpu as pltpu
from jax.sharding import PartitionSpec as P

N = 512
OBS = 64
BANDS = 4
REACH = 32
DIFFUSION = 0.25
RELAXATION = 0.02
ROWS = N + 8
LANES = 128
PIECES = N // LANES
CELLS = 32
F32 = jnp.float32
BF16 = jnp.bfloat16
NT = (((1,), (1,)), ((), ()))
NN = (((1,), (0,)), ((), ()))


def lanes(rows, count=N):
    return lax.broadcasted_iota(jnp.int32, (rows, count), 1)


def pieces(v):
    return [v[:, LANES * j : LANES * (j + 1)] for j in range(PIECES)]


def ahead(parts, by):
    turn = jnp.where(by == 0, 0, LANES - by)
    turned = [pltpu.roll(part, turn, 1) for part in parts]
    here = lanes(1, LANES) + by < LANES
    return [jnp.where(here, turned[j], turned[(j + 1) % PIECES]) for j in range(PIECES)]


def neighbours(v):
    lane = lanes(1)
    left = jnp.where(lane > 0, 0.5 * DIFFUSION, 0.0)
    right = jnp.where(lane < N - 1, 0.5 * DIFFUSION, 0.0)
    return right * pltpu.roll(v, N - 1, 1) + left * pltpu.roll(v, 1, 1)


class Step:
    def __init__(self, k, offs_ref, up_ref, c_ref):
        self.offs = [offs_ref[k, band] for band in range(BANDS)]
        self.up = up_ref[pl.ds(k, 1), :]
        courant = c_ref[pl.ds(k, 1), :]
        reach = jnp.full_like(self.up, self.offs[0])
        for band in range(1, BANDS):
            reach = jnp.where(self.up == band, self.offs[band], reach)
        at = lanes(1) + reach
        inside = (at >= 0) & (at < N)
        self.centre = 1.0 - courant - DIFFUSION
        self.advected = jnp.where(inside, courant, 0.0)

    def apply(self, v):
        base = pieces(pltpu.roll(v, REACH, 1))
        ups = pieces(self.up)
        moved = ahead(base, self.offs[0] + REACH)
        for band in range(1, BANDS):
            other = ahead(base, self.offs[band] + REACH)
            moved = [jnp.where(ups[j] == band, other[j], moved[j]) for j in range(PIECES)]
        return self.centre * v + neighbours(v) + self.advected * jnp.concatenate(moved, axis=1)

    def apply_transposed(self, v):
        out = pieces(pltpu.roll(self.advected * v, REACH, 1))
        ups = pieces(pltpu.roll(self.up, REACH, 1))
        total = pieces(self.centre * v + neighbours(v))
        for band in range(BANDS):
            own = [jnp.where(ups[j] == band, out[j], 0.0) for j in range(PIECES)]
            shifted = ahead(own, REACH - self.offs[band])
            total = [total[j] + shifted[j] for j in range(PIECES)]
        return jnp.concatenate(total, axis=1)


def dot(a, b, dims=NN):
    return lax.dot_general(a, b, dims, preferred_element_type=F32)


def split2(v):
    hi = v.astype(BF16)
    return hi, (v - hi.astype(F32)).astype(BF16)


def stacked(v):
    hi = v.astype(BF16).astype(F32)
    return jnp.concatenate([hi, v - hi], axis=0).astype(BF16)


def observed_part(p, s4):
    rows = p.shape[0]
    both = dot(stacked(p), s4, NT)
    return both[:rows] + both[rows:]


def gain_rows(s, gains):
    hi, lo = split2(RELAXATION * s.astype(F32) + gains)
    return jnp.concatenate([hi, hi, lo, lo], axis=0)


def correction(e4, kk):
    hi = e4.astype(BF16).astype(F32)
    odd = (lanes(1, 4 * OBS) // OBS) % 2 == 1
    return dot(jnp.where(odd, e4 - hi, hi).astype(BF16), kk)


def one_hot(obs_row):
    own = lax.broadcasted_iota(jnp.int32, (OBS, OBS), 0) == lanes(OBS, OBS)
    column = jnp.sum(jnp.where(own, obs_row.astype(F32), 0.0), axis=1, keepdims=True)
    return jnp.where(column.astype(jnp.int32) == lanes(OBS), 1.0, 0.0).astype(BF16)


def through(v, parts_ref):
    rows = v.shape[0]
    both = stacked(v)
    high, low = dot(both, parts_ref[0], NT), dot(both, parts_ref[1], NT)
    return high[:rows] + (high[rows:] + low[:rows] + low[rows:])


def call(kernel, name, outs, operands, scratch=(), scalars=1, flops=10**8, moved=1 << 20):
    vmem, smem = pl.BlockSpec(memory_space=pltpu.VMEM), pl.BlockSpec(memory_space=pltpu.SMEM)
    return pl.pallas_call(
        kernel,
        out_shape=tuple(jax.ShapeDtypeStruct(*out) for out in outs),
        in_specs=[smem] * scalars + [vmem] * (len(operands) - scalars),
        out_specs=(vmem,) * len(outs),
        scratch_shapes=list(scratch),
        cost_estimate=pl.CostEstimate(flops=flops, bytes_accessed=moved, transcendentals=0),
        compiler_params=pltpu.CompilerParams(vmem_limit_bytes=32 << 20),
        name=name,
    )(*operands)


PARTS = ((2, N, N), BF16)
VECTOR = ((8, N), F32)


def keep_parts(values_ref, parts_ref):
    for r in range(0, N, 64):
        at = pl.ds(r, 64)
        parts_ref[0, at, :], parts_ref[1, at, :] = split2(values_ref[at, :])


def keep_columns(rows_ref, kept_ref, start):
    turned = jnp.transpose(rows_ref[...].astype(F32))
    for k in range(rows_ref.shape[0]):
        kept_ref[k, start : start + N, :] = jnp.broadcast_to(turned[:, k : k + 1], (N, LANES))


def clear_edges(padded_ref):
    edge = jnp.zeros((PIECES, REACH, LANES), F32)
    padded_ref[:, 0:REACH, :] = edge
    padded_ref[:, REACH + N : N + 2 * REACH, :] = edge


def start_identity(padded_ref):
    clear_edges(padded_ref)
    row = lax.broadcasted_iota(jnp.int32, (N, LANES), 0)
    for j in range(PIECES):
        padded_ref[j, REACH : REACH + N, :] = jnp.where(row == lanes(N, LANES) + LANES * j, 1.0, 0.0)


def keep_map(padded_ref, map_ref, parts_ref):
    for r in range(0, N, 64):
        for j in range(PIECES):
            at, cols = slice(r, r + 64), slice(LANES * j, LANES * (j + 1))
            value = padded_ref[j, REACH + r : REACH + r + 64, :]
            map_ref[at, cols] = value
            parts_ref[0, at, cols], parts_ref[1, at, cols] = split2(value)


def diffused(padded_ref, j, first, size, centre):
    at = lambda by: padded_ref[j, pl.ds(first + by, size), :]
    return centre * at(0) + (0.5 * DIFFUSION) * (at(1) + at(-1))


def filter_map(offsets, upwind, courant, obs_cells, gains, observed):
    steps = offsets.shape[0]

    def kernel(
        offs_ref, cells_ref, up_ref, c_ref, obs_ref, gains_ref, y_ref,
        map_ref, parts_ref, off_ref, s_ref, held_ref, moved_ref, picked_ref, ups_ref, cs_ref
    ):
        keep_columns(up_ref, ups_ref, 0)
        keep_columns(c_ref, cs_ref, 0)
        start_identity(held_ref)
        head = lax.broadcasted_iota(jnp.int32, (8, 1), 0) == 0

        def one(k, vec):
            step = Step(k, offs_ref, up_ref, c_ref)
            s = one_hot(obs_ref[pl.ds(k, 1), :])
            s_ref[k] = s
            gain = RELAXATION * s.astype(F32) + gains_ref[k]
            for r in range(0, N, CELLS):
                ups, cs = ups_ref[k, r : r + CELLS, :], cs_ref[k, r : r + CELLS, :]
                for j in range(PIECES):
                    at = lambda by: held_ref[j, pl.ds(REACH + r + by, CELLS), :]
                    arrived = at(step.offs[0])
                    for band in range(1, BANDS):
                        arrived = jnp.where(ups == band, at(step.offs[band]), arrived)
                    spread = diffused(held_ref, j, REACH + r, CELLS, 1.0 - cs - DIFFUSION)
                    moved_ref[j, r : r + CELLS, :] = spread + cs * arrived
            for o in range(OBS):
                for j in range(PIECES):
                    cols = slice(LANES * j, LANES * (j + 1))
                    picked_ref[o : o + 1, cols] = moved_ref[j, pl.ds(cells_ref[k, o], 1), :]
            seen_hi, seen_lo = split2(picked_ref[...])
            seen = jnp.concatenate([seen_hi, seen_lo] * 2, axis=0)
            turned = jnp.transpose(jnp.concatenate([gain, gain], axis=0))
            factors = jnp.concatenate(split2(turned), axis=1)
            for r in range(0, N, 256):
                at = slice(r, r + 256)
                corrected = pieces(dot(factors[at], seen))
                for j in range(PIECES):
                    held_ref[j, REACH + r : REACH + r + 256, :] = moved_ref[j, at, :] - corrected[j]

            high, low = split2(gain)
            kk = jnp.concatenate([high, high, low, low], axis=0)
            s4 = jnp.concatenate([s] * 4, axis=0)
            y4 = jnp.concatenate([y_ref[pl.ds(k, 1), :]] * 4, axis=1)
            p = step.apply(vec)
            return p - correction(observed_part(p, s4) - jnp.where(head, y4, 0.0), kk)

        vec = lax.fori_loop(0, steps, one, jnp.zeros((8, N), F32))
        off_ref[...] = vec
        map_ref[N:ROWS, :] = vec
        keep_map(held_ref, map_ref, parts_ref)

    return call(
        kernel,
        "filter_map",
        (((ROWS, N), F32), PARTS, VECTOR, ((steps, OBS, N), BF16)),
        (offsets, obs_cells, upwind, courant, obs_cells, gains, observed),
        scratch=[
            pltpu.VMEM((PIECES, N + 2 * REACH, LANES), F32),
            pltpu.VMEM((PIECES, N, LANES), F32),
            pltpu.VMEM((OBS, N), F32),
            pltpu.VMEM((steps, N, LANES), F32),
            pltpu.VMEM((steps, N, LANES), F32),
        ],
        scalars=2,
        flops=16 * 10**9,
        moved=4 << 20,
    )


def smoother_map(offsets, upwind, courant, smooth_gain):
    steps = offsets.shape[0]

    def kernel(offs_ref, up_ref, c_ref, sg_ref, map_ref, parts_ref, held_ref, out_ref, ups_ref, cs_ref, gains_ref):
        outside = jnp.full((REACH, LANES), -1.0, F32)
        for k in range(steps):
            ups_ref[k, 0:REACH, :] = outside
            ups_ref[k, REACH + N : N + 2 * REACH, :] = outside
        keep_columns(up_ref, ups_ref, REACH)
        keep_columns(c_ref, cs_ref, 0)
        keep_columns(sg_ref, gains_ref, 0)
        start_identity(held_ref.at[0])
        clear_edges(held_ref.at[1])
        clear_edges(out_ref)

        def one(i, carry):
            k = steps - 1 - i
            offs = [offs_ref[k, band] for band in range(BANDS)]
            now, later = held_ref.at[lax.rem(i, 2)], held_ref.at[lax.rem(i + 1, 2)]
            for r in range(0, N, CELLS):
                cs = cs_ref[k, r : r + CELLS, :]
                for j in range(PIECES):
                    at = slice(REACH + r, REACH + r + CELLS)
                    out_ref[j, at, :] = cs * now[j, at, :]
            for r in range(0, N, CELLS):
                froms = [pl.ds(REACH + r - offs[band], CELLS) for band in range(BANDS)]
                taken = [ups_ref[k, froms[band], :] == band for band in range(BANDS)]
                centre = 1.0 - cs_ref[k, r : r + CELLS, :] - DIFFUSION
                gain = gains_ref[k, r : r + CELLS, :]
                for j in range(PIECES):
                    total = diffused(now, j, REACH + r, CELLS, centre)
                    for band in range(BANDS):
                        total = total + jnp.where(taken[band], out_ref[j, froms[band], :], 0.0)
                    later[j, REACH + r : REACH + r + CELLS, :] = gain * total
            return carry

        lax.fori_loop(0, steps, one, 0)
        keep_map(held_ref.at[steps % 2], map_ref, parts_ref)

    return call(
        kernel,
        "smoother_map",
        (((N, N), F32), PARTS),
        (offsets, upwind, courant, smooth_gain),
        scratch=[
            pltpu.VMEM((2, PIECES, N + 2 * REACH, LANES), F32),
            pltpu.VMEM((PIECES, N + 2 * REACH, LANES), F32),
            pltpu.VMEM((steps, N + 2 * REACH, LANES), F32),
            pltpu.VMEM((steps, N, LANES), F32),
            pltpu.VMEM((steps, N, LANES), F32),
        ],
        flops=8 * 10**9,
        moved=2 << 20,
    )


def compose(flag, mine, other):
    rows = mine.shape[0]
    affine = rows > N

    def kernel(flag_ref, mine_ref, other_ref, out_ref, parts_ref, other_parts_ref, *offs):
        keep_parts(other_ref, other_parts_ref)
        if affine:
            offs[1][...] = other_ref[N:ROWS, :]

        def product(first_ref, second_ref):
            high, low = split2(first_ref[0:N, :])
            for start in (0, 256):
                at = pl.ds(start, 256)
                both = stacked(second_ref[at, :])
                big = dot(both, high)
                out_ref[at, :] = big[:256] + (big[256:] + dot(both[:256], low))
            if affine:
                both = stacked(first_ref[N:ROWS, :])
                keep = split2(second_ref[0:N, :])
                big, small = dot(both, keep[0], NT), dot(both, keep[1], NT)
                offset = big[:8] + (big[8:] + small[:8] + small[8:]) + second_ref[N:ROWS, :]
                out_ref[N:ROWS, :] = offset
                offs[0][...] = offset

        @pl.when(flag_ref[0] == 1)
        def _():
            product(other_ref, mine_ref)

        @pl.when(flag_ref[0] == 0)
        def _():
            product(mine_ref, other_ref)

        keep_parts(out_ref, parts_ref)

    outs = (((rows, N), F32), PARTS, PARTS) + ((VECTOR, VECTOR) if affine else ())
    return call(kernel, "compose", outs, (flag, mine, other), flops=10**9, moved=5 << 20)


def hop(place, mark, state, got, parts, offset):
    def kernel(place_ref, state_ref, got_ref, parts_ref, off_ref, new_ref, sent_ref):
        new = jnp.where(place_ref[0] == mark, got_ref[...], state_ref[...])
        new_ref[...] = new
        sent_ref[...] = through(new, parts_ref) + off_ref[...]

    return call(kernel, "hop", (VECTOR, VECTOR), (place, state, got, parts, offset))


def descend(place, mark, state, got, quad, quad_off, pair, pair_off, own, own_off):
    def kernel(place_ref, state_ref, got_ref, quad_ref, qo_ref, pair_ref, po_ref, own_ref, oo_ref, new_ref, sent_ref):
        new_ref[...] = jnp.where(place_ref[0] == mark, got_ref[...], state_ref[...])

        @pl.when(place_ref[1] == 1)
        def _():
            new_ref[...] = through(new_ref[...], quad_ref) + qo_ref[...]

        @pl.when(place_ref[2] == 1)
        def _():
            new_ref[...] = through(new_ref[...], pair_ref) + po_ref[...]

        sent_ref[...] = through(new_ref[...], own_ref) + oo_ref[...]

    operands = (place, state, got, quad, quad_off, pair, pair_off, own, own_off)
    return call(kernel, "descend", (VECTOR, VECTOR), operands)


def joined(flag, mine, other, my_parts, other_parts):
    def kernel(flag_ref, mine_ref, other_ref, mp_ref, op_ref, out_ref):
        @pl.when(flag_ref[0] == 1)
        def _():
            out_ref[...] = through(other_ref[...], mp_ref) + mine_ref[...]

        @pl.when(flag_ref[0] == 0)
        def _():
            out_ref[...] = through(mine_ref[...], op_ref) + other_ref[...]

    return call(kernel, "joined", (VECTOR,), (flag, mine, other, my_parts, other_parts))[0]


def smoothing(steps, diff, offs_ref, up_ref, c_ref, sg_ref, u_ref, store=None):
    def one(i, diff):
        k = steps - 1 - i
        step = Step(k, offs_ref, up_ref, c_ref)
        if store is not None:
            store(k, diff)
        at = pl.ds(k, 1)
        return sg_ref[at, :] * step.apply_transposed(diff + u_ref[at, :])

    return lax.fori_loop(0, steps, one, diff)


def forward(place, offsets, upwind, courant, smooth_gain, hots, gains, observed, state, got):
    steps = offsets.shape[0]

    def kernel(
        place_ref, offs_ref, up_ref, c_ref, sg_ref, s_ref, gains_ref, y_ref, state_ref, got_ref, filt_ref, upd_ref, end_ref
    ):
        first = lax.broadcasted_iota(jnp.int32, (8, 1), 0) == 0

        def one(k, vec):
            step = Step(k, offs_ref, up_ref, c_ref)
            s = s_ref[k]
            kk = gain_rows(s, gains_ref[k])
            s4 = jnp.concatenate([s] * 4, axis=0)
            y4 = jnp.concatenate([y_ref[pl.ds(k, 1), :]] * 4, axis=1)
            p = step.apply(vec)
            update = -correction(observed_part(p, s4) - jnp.where(first, y4, 0.0), kk)
            vec = p + update
            filt_ref[pl.ds(k, 1), :] = vec[0:1]
            upd_ref[pl.ds(k, 1), :] = update[0:1]
            return vec

        start = jnp.where(place_ref[0] == 1, got_ref[...], state_ref[...])
        lax.fori_loop(0, steps, one, start)
        zeros = jnp.zeros((8, N), F32)
        end_ref[...] = smoothing(steps, zeros, offs_ref, up_ref, c_ref, sg_ref, upd_ref)

    return call(
        kernel,
        "forward",
        (((steps, N), F32), ((steps, N), F32), VECTOR),
        (place, offsets, upwind, courant, smooth_gain, hots, gains, observed, state, got),
        scalars=2,
        flops=4 * 10**9,
        moved=3 << 20,
    )


def smooth(place, offsets, upwind, courant, smooth_gain, updates, filtered, top, got):
    steps = offsets.shape[0]

    def kernel(place_ref, offs_ref, up_ref, c_ref, sg_ref, u_ref, x_ref, top_ref, got_ref, out_ref):
        def store(k, diff):
            at = pl.ds(k, 1)
            out_ref[at, :] = x_ref[at, :] + diff[0:1]

        diff = jnp.where(place_ref[0] == 0, got_ref[...], top_ref[...])
        smoothing(steps, diff, offs_ref, up_ref, c_ref, sg_ref, u_ref, store)

    return call(
        kernel,
        "smooth",
        (((steps, N), F32),),
        (place, offsets, upwind, courant, smooth_gain, updates, filtered, top, got),
        scalars=2,
    )[0]


def on_device(initial, offsets, upwind, courant, obs_cells, gains, observed, smooth_gain):
    place = lax.axis_index("tm")
    x, y, core = place // 8, (place // 2) % 4, place % 2

    def moved(values, to, senders):
        return lax.ppermute(values, "tm", [(i, to(i)) for i in range(32) if senders(i)])

    even = lambda i: i % 2 == 0
    odd = lambda i: i % 2 == 1
    ints = lambda *values: jnp.stack([jnp.asarray(v, jnp.int32) for v in values])
    never = jnp.zeros((1,), jnp.int32)
    at_core = ints(core)
    y_odd, y_even, y_high, y_low = ints(y % 2 == 1), ints(y % 2 == 0), ints(y >= 2), ints(y < 2)
    start_row = jnp.broadcast_to(initial[None, :], (8, N))
    zeros = jnp.zeros((8, N), F32)

    fmap, fmap_p, fmap_o, hots = filter_map(offsets, upwind, courant, obs_cells, gains, observed)
    fmap_odd = moved(fmap, lambda i: i - 1, odd)
    fpair, fpair_p, _, _, _ = compose(never, fmap, fmap_odd)
    fpair_other = moved(fpair, lambda i: i ^ 2, even)
    smap, smap_p = smoother_map(offsets, upwind, courant, smooth_gain)
    smap_even = moved(smap, lambda i: i + 1, even)
    fquad, fquad_p, fpair_op, _, fpair_oo = compose(y_odd, fpair, fpair_other)
    fquad_other = moved(fquad, lambda i: i ^ 4, even)
    spair, spair_p, smap_ep = compose(never, smap, smap_even)
    spair_other = moved(spair, lambda i: i ^ 2, odd)
    foct, foct_p, fquad_op, foct_o, fquad_oo = compose(y_high, fquad, fquad_other)

    place3 = ints(x, y >= 2, y % 2 == 1)
    ahead_of = lambda v: moved(v, lambda i: i + 8, lambda i: even(i) and i < 24)
    state, sent = hop(place3, 0, start_row, start_row, foct_p, foct_o)
    got = ahead_of(sent)
    squad, squad_p, spair_op = compose(y_even, spair, spair_other)
    squad_other = moved(squad, lambda i: i ^ 4, odd)
    state, sent = hop(place3, 1, state, got, foct_p, foct_o)
    got = ahead_of(sent)
    state, sent = hop(place3, 2, state, got, foct_p, foct_o)
    got = ahead_of(sent)
    state, sent = descend(
        place3, 3, state, got, fquad_op, fquad_oo, fpair_op, fpair_oo, fmap_p, fmap_o
    )
    got = moved(sent, lambda i: i + 1, even)
    _, soct_p, squad_op = compose(y_low, squad, squad_other)
    filtered, updates, own = forward(
        at_core, offsets, upwind, courant, smooth_gain, hots, gains, observed, state, got
    )

    pair = joined(never, own, moved(own, lambda i: i + 1, even), smap_p, smap_ep)
    pair_other = moved(pair, lambda i: i ^ 2, odd)
    quad = joined(y_even, pair, pair_other, spair_p, spair_op)
    quad_other = moved(quad, lambda i: i ^ 4, odd)
    octet = joined(y_low, quad, quad_other, squad_p, squad_op)
    place3 = ints(x, y < 2, y % 2 == 0)
    behind = lambda v: moved(v, lambda i: i - 8, lambda i: odd(i) and i >= 8)
    got = behind(octet)
    top, sent = hop(place3, 2, zeros, got, soct_p, octet)
    got = behind(sent)
    top, sent = hop(place3, 1, top, got, soct_p, octet)
    got = behind(sent)
    top, sent = descend(place3, 0, top, got, squad_op, quad_other, spair_op, pair_other, smap_p, own)
    got = moved(sent, lambda i: i - 1, odd)
    smoothed = smooth(
        at_core, offsets, upwind, courant, smooth_gain, updates, filtered, top, got
    )
    return filtered, smoothed


def solution(mesh):
    row = P("tm", None)
    in_specs = (P(), row, row, row, row, P("tm", None, None), row, row)
    return jax.shard_map(on_device, mesh=mesh, in_specs=in_specs, out_specs=(row, row), check_vma=False)
```

time: 1190 us -> 200 us (0.17)
  the two profiles are of different devices: /device:TPU:43 before, /device:TPU:1 now
where the time goes in v2:
time: 200 us; the launch traced here: 199 us
  Pallas kernels  86.4 us (43%)
  waiting for transfers between devices  70.7 us (35%)
  starting transfers between devices  30.9 us (15%)
  local copies, waits for them, and re-layouts  10.1 us (5%)
    pallas_call x20, Pallas kernels, call(): pl.pallas_call(kernel, out_shape=tuple((jax.ShapeDtypeStruct(*out) for ou...  86.4 us
    ppermute x17, waiting for transfers between devices, moved(): lax.ppermute(values, 'tm', [(i, to(i)) for i in range(32) if senders(i)])  70.7 us
    ppermute x17, starting transfers between devices, moved(): lax.ppermute(values, 'tm', [(i, to(i)) for i in range(32) if senders(i)])  30.9 us
    unnamed x45, local copies, waits for them, and re-layouts  10.1 us
  transfers between devices with their start and end apart: 17, of which 9 were waited for; matrix products, arithmetic and copies ran while one was open for 0% of the time, Pallas kernels for 27%

profile of v2, /device:TPU:1, one launch (start us, length us, event | category | flops | bytes accessed | tf_op | source)
XLA Modules:
  0.0 199.3 jit_solution(14172132488531417571)
XLA Ops:
  0.6 0.8 copy.11.offs_ref
  1.4 1.6 copy-done.8
  3.0 0.8 copy-done.10
  3.7 0.8 copy-done.12
  4.5 0.7 copy-done.15
  5.9 24.5 %filter_map.1 = (f32[520,512]{1,0:T(8,128)S(1)}, bf16[2,512,512]{2,1,0:T(8,128)(2,1)S(1)}, f32[8,512]{1,0:T(8,128)S(1)}, bf16[16,64,512]{2,1,0:T(8,128)(2,1)S(1)}) custom-call(s32[16,4]{1,0:T(8,128)S(1)} %copy.11.offs_ref, s32[16,64]{1,0:T(8,128)S(1)} %copy-done.15, s32[16,512]{1,0:T(8,128)S(1)} %copy-done.10, f32[16,512]{1,0:T(8,128)S(1)} %copy-done.12, ...), custom_call_target="tpu_custom_call" | custom-call | flops 16000000000 | bytes 4194304 | tf_op jit(solution)/shard_map/filter_map/pallas_call | solution.py:125
  30.5 8.8 %collective-permute-start = (f32[520,512]{1,0:T(8,128)S(1)}, f32[520,512]{1,0:T(8,128)S(1)}, u32[]{:S(2)}, u32[]{:S(2)}) collective-permute-start(f32[520,512]{1,0:T(8,128)S(1)} %get-tuple-element.42.mine_ref), channel_id=1, source_target_pairs={{16,0},{48,32},{80,64},{112,96},{144,128},{176,160},{208,192},{240... | collective-permute-start | bytes 3194888 | tf_op jit(solution)/shard_map/ppermute | solution.py:458
  39.3 16.9 %smoother_map.1 = (f32[512,512]{1,0:T(8,128)S(1)}, bf16[2,512,512]{2,1,0:T(8,128)(2,1)S(1)}) custom-call(s32[16,4]{1,0:T(8,128)S(1)} %copy.11.offs_ref, s32[16,512]{1,0:T(8,128)S(1)} %copy-done.11, f32[16,512]{1,0:T(8,128)S(1)} %copy-done.13, f32[16,512]{1,0:T(8,128)S(1)} %copy-done.14), custom_call_target="tpu_custom_call" | custom-call | flops 8000000000 | bytes 2097152 | tf_op jit(solution)/shard_map/smoother_map/pallas_call | solution.py:125
  56.3 1.3 collective-permute-start.8
  57.6 3.0 %compose.6 = (f32[520,512]{1,0:T(8,128)}, bf16[2,512,512]{2,1,0:T(8,128)(2,1)}, bf16[2,512,512]{2,1,0:T(8,128)(2,1)}, f32[8,512]{1,0:T(8,128)}, f32[8,512]{1,0:T(8,128)}) custom-call(s32[1]{0:T(128)} %constant.64.clone.1.flag_ref, f32[520,512]{1,0:T(8,128)S(1)} %get-tuple-element.42.mine_ref, f32[520,512]{1,0:T(8,128)S(1)} %collective-permute-done.other_ref), custom_call_target="tpu_custom_call" | custom-call | flops 1000000000 | bytes 5242880 | tf_op jit(solution)/shard_map/compose/pallas_call | solution.py:125
  60.6 1.6 collective-permute-start.1
  62.3 2.4 %compose.9 = (f32[512,512]{1,0:T(8,128)}, bf16[2,512,512]{2,1,0:T(8,128)(2,1)S(1)}, bf16[2,512,512]{2,1,0:T(8,128)(2,1)S(1)}) custom-call(s32[1]{0:T(128)} %constant.64.clone.1.flag_ref, f32[512,512]{1,0:T(8,128)S(1)} %get-tuple-element.65.mine_ref, f32[512,512]{1,0:T(8,128)S(1)} %collective-permute-done.8.other_ref), custom_call_target="tpu_custom_call" | custom-call | flops 1000000000 | bytes 5242880 | tf_op jit(solution)/shard_map/compose/pallas_call | solution.py:125
  64.6 1.9 collective-permute-start.10
  66.6 4.2 %compose.7 = (f32[520,512]{1,0:T(8,128)}, bf16[2,512,512]{2,1,0:T(8,128)(2,1)}, bf16[2,512,512]{2,1,0:T(8,128)(2,1)S(1)}, f32[8,512]{1,0:T(8,128)}, f32[8,512]{1,0:T(8,128)S(1)}) custom-call(s32[1]{0:T(128)} %bitcast.3.flag_ref, f32[520,512]{1,0:T(8,128)} %get-tuple-element.43.mine_ref, f32[520,512]{1,0:T(8,128)} %collective-permute-done.1.other_ref), custom_call_target="tpu_custom_call" | custom-call | flops 1000000000 | bytes 5242880 | tf_op jit(solution)/shard_map/compose/pallas_call | solution.py:125
  70.9 1.0 copy-done.6
  71.8 1.6 collective-permute-start.2
  73.5 16.1 %collective-permute-done.10.other_ref = f32[512,512]{1,0:T(8,128)} collective-permute-done((f32[512,512]{1,0:T(8,128)}, f32[512,512]{1,0:T(8,128)}, u32[]{:S(2)}, u32[]{:S(2)}) %collective-permute-start.10) | collective-permute-done | bytes 1048608 | tf_op jit(solution)/shard_map/ppermute | solution.py:458
  89.5 3.6 %compose.10 = (f32[512,512]{1,0:T(8,128)}, bf16[2,512,512]{2,1,0:T(8,128)(2,1)S(1)}, bf16[2,512,512]{2,1,0:T(8,128)(2,1)S(1)}) custom-call(s32[1]{0:T(128)} %bitcast.5.flag_ref, f32[512,512]{1,0:T(8,128)} %get-tuple-element.68.mine_ref, f32[512,512]{1,0:T(8,128)} %collective-permute-done.10.other_ref), custom_call_target="tpu_custom_call" | custom-call | flops 1000000000 | bytes 5242880 | tf_op jit(solution)/shard_map/compose/pallas_call | solution.py:125
  93.2 1.0 copy-done.2
  94.2 1.9 collective-permute-start.12
  96.2 3.9 %compose.8 = (f32[520,512]{1,0:T(8,128)}, bf16[2,512,512]{2,1,0:T(8,128)(2,1)S(1)}, bf16[2,512,512]{2,1,0:T(8,128)(2,1)S(1)}, f32[8,512]{1,0:T(8,128)S(1)}, f32[8,512]{1,0:T(8,128)S(1)}) custom-call(s32[1]{0:T(128)} %bitcast.2.flag_ref, f32[520,512]{1,0:T(8,128)} %get-tuple-element.44.mine_ref, f32[520,512]{1,0:T(8,128)} %collective-permute-done.2.other_ref), custom_call_target="tpu_custom_call" | custom-call | flops 1000000000 | bytes 5242880 | tf_op jit(solution)/shard_map/compose/pallas_call | solution.py:125
  100.1 0.9 hop.5
  101.7 0.9 hop.6
  103.3 0.9 hop.7
  105.0 0.9 descend.2
  105.9 1.3 collective-permute-start.6
  107.2 39.1 %collective-permute-done.6.got_ref = f32[8,512]{1,0:T(8,128)S(1)} collective-permute-done((f32[8,512]{1,0:T(8,128)S(1)}, f32[8,512]{1,0:T(8,128)S(1)}, u32[]{:S(2)}, u32[]{:S(2)}) %collective-permute-start.6) | collective-permute-done | bytes 16416 | tf_op jit(solution)/shard_map/ppermute | solution.py:458
  146.3 1.6 copy-done.9
  147.9 1.2 copy-done.20
  149.2 11.9 %forward.1 = (f32[16,512]{1,0:T(8,128)}, f32[16,512]{1,0:T(8,128)S(1)}, f32[8,512]{1,0:T(8,128)S(1)}) custom-call(s32[1]{0:T(128)} %bitcast.place_ref, s32[16,4]{1,0:T(8,128)S(1)} %copy.11.offs_ref, s32[16,512]{1,0:T(8,128)S(1)} %copy-done.11, f32[16,512]{1,0:T(8,128)S(1)} %copy-done.13, f32[16,512]{1,0:T(8,128)S(1)} %copy-done.14, ...), custom_call_target="tpu_custom_call" | custom-call | flops 4000000000 | bytes 3145728 | tf_op jit(solution)/shard_map/forward/pallas_call | solution.py:125
  161.1 1.3 collective-permute-start.7
  162.4 1.8 collective-permute-done.7.other_ref
  164.5 1.9 collective-permute-start.9
  166.5 2.5 %collective-permute-done.9.other_ref.po_ref = f32[8,512]{1,0:T(8,128)S(1)} collective-permute-done((f32[8,512]{1,0:T(8,128)S(1)}, f32[8,512]{1,0:T(8,128)S(1)}, u32[]{:S(2)}, u32[]{:S(2)}) %collective-permute-start.9) | collective-permute-done | bytes 16416 | tf_op jit(solution)/shard_map/ppermute | solution.py:458
  169.4 1.9 collective-permute-start.11
  171.3 3.7 %compose.11 = (f32[512,512]{1,0:T(8,128)}, bf16[2,512,512]{2,1,0:T(8,128)(2,1)S(1)}, bf16[2,512,512]{2,1,0:T(8,128)(2,1)S(1)}) custom-call(s32[1]{0:T(128)} %bitcast.4.flag_ref, f32[512,512]{1,0:T(8,128)} %get-tuple-element.71.mine_ref, f32[512,512]{1,0:T(8,128)} %collective-permute-done.12.other_ref), custom_call_target="tpu_custom_call" | custom-call | flops 1000000000 | bytes 5242880 | tf_op jit(solution)/shard_map/compose/pallas_call | solution.py:125
  175.7 1.3 collective-permute-start.13
  177.1 3.7 %collective-permute-done.13.got_ref = f32[8,512]{1,0:T(8,128)S(1)} collective-permute-done((f32[8,512]{1,0:T(8,128)S(1)}, f32[8,512]{1,0:T(8,128)S(1)}, u32[]{:S(2)}, u32[]{:S(2)}) %collective-permute-start.13) | collective-permute-done | bytes 16416 | tf_op jit(solution)/shard_map/ppermute | solution.py:458
  180.8 0.9 hop.8
  181.7 1.3 collective-permute-start.14
  183.0 3.2 %collective-permute-done.14.got_ref = f32[8,512]{1,0:T(8,128)S(1)} collective-permute-done((f32[8,512]{1,0:T(8,128)S(1)}, f32[8,512]{1,0:T(8,128)S(1)}, u32[]{:S(2)}, u32[]{:S(2)}) %collective-permute-start.14) | collective-permute-done | bytes 16416 | tf_op jit(solution)/shard_map/ppermute | solution.py:458
  186.2 0.9 hop.9
  187.1 1.3 collective-permute-start.15
  188.4 3.2 %collective-permute-done.15.got_ref = f32[8,512]{1,0:T(8,128)S(1)} collective-permute-done((f32[8,512]{1,0:T(8,128)S(1)}, f32[8,512]{1,0:T(8,128)S(1)}, u32[]{:S(2)}, u32[]{:S(2)}) %collective-permute-start.15) | collective-permute-done | bytes 16416 | tf_op jit(solution)/shard_map/ppermute | solution.py:458
  191.6 1.7 descend.3
  193.3 1.3 collective-permute-start.16
  194.6 0.8 collective-permute-done.16.got_ref
  195.4 3.9 %smooth.1 = f32[16,512]{1,0:T(8,128)} custom-call(s32[1]{0:T(128)} %bitcast.place_ref, s32[16,4]{1,0:T(8,128)S(1)} %copy.11.offs_ref, s32[16,512]{1,0:T(8,128)S(1)} %copy-done.11, f32[16,512]{1,0:T(8,128)S(1)} %copy-done.13, f32[16,512]{1,0:T(8,128)S(1)} %copy-done.14, f32[16,512]{1,0:T(8,128)S(1)} %get-tuple-element.62.u_ref, f32[16,512]{1,0:T(8,128)S(1)} %copy-done.18, ...), custom_call_target="tpu_custom_call" | custom-call | flops 100000000 | bytes 1048576 | tf_op jit(solution)/shard_map/smooth/pallas_call | solution.py:125
  (55 shorter events, 4.4 us)
Async XLA Ops:
  1.4 1.6 copy-start.8
  3.0 0.8 copy-start.10
  3.7 0.8 copy-start.12
  4.5 0.7 copy-start.15
  5.2 0.7 copy-start.16
  5.9 33.4 %copy-start.11 = (s32[16,512]{1,0:T(8,128)S(1)}, s32[16,512]{1,0:T(8,128)}, u32[]{:S(2)}) copy-start(s32[16,512]{1,0:T(8,128)} %up_ref.7) | copy-start | bytes 98308
  5.9 33.4 %copy-start.13 = (f32[16,512]{1,0:T(8,128)S(1)}, f32[16,512]{1,0:T(8,128)}, u32[]{:S(2)}) copy-start(f32[16,512]{1,0:T(8,128)} %c_ref.7) | copy-start | bytes 98308
  5.9 33.4 %copy-start.14 = (f32[16,512]{1,0:T(8,128)S(1)}, f32[16,512]{1,0:T(8,128)}, u32[]{:S(2)}) copy-start(f32[16,512]{1,0:T(8,128)} %sg_ref.5) | copy-start | bytes 98308
  30.5 25.8 %copy-start.4 = (bf16[2,512,512]{2,1,0:T(8,128)(2,1)}, bf16[2,512,512]{2,1,0:T(8,128)(2,1)S(1)}, u32[]{:S(2)}) copy-start(bf16[2,512,512]{2,1,0:T(8,128)(2,1)S(1)} %get-tuple-element.57.own_ref) | copy-start | bytes 3145732
  30.5 25.8 %copy-start.19 = (bf16[16,64,512]{2,1,0:T(8,128)(2,1)}, bf16[16,64,512]{2,1,0:T(8,128)(2,1)S(1)}, u32[]{:S(2)}) copy-start(bf16[16,64,512]{2,1,0:T(8,128)(2,1)S(1)} %get-tuple-element.41.s_ref) | copy-start | bytes 3145732
  30.5 27.1 %collective-permute-start = (f32[520,512]{1,0:T(8,128)S(1)}, f32[520,512]{1,0:T(8,128)S(1)}, u32[]{:S(2)}, u32[]{:S(2)}) collective-permute-start(f32[520,512]{1,0:T(8,128)S(1)} %get-tuple-element.42.mine_ref), channel_id=1, source_target_pairs={{16,0},{48,32},{80,64},{112,96},{144,128},{176,160},{208,192},{240... | collective-permute-start | bytes 3194888 | tf_op jit(solution)/shard_map/ppermute | solution.py:458
  56.3 6.0 %collective-permute-start.8 = (f32[512,512]{1,0:T(8,128)S(1)}, f32[512,512]{1,0:T(8,128)S(1)}, u32[]{:S(2)}, u32[]{:S(2)}) collective-permute-start(f32[512,512]{1,0:T(8,128)S(1)} %get-tuple-element.65.mine_ref), channel_id=1, source_target_pairs={{0,16},{32,48},{64,80},{96,112},{128,144},{160,176},{192,208},{224... | collective-permute-start | bytes 3145736 | tf_op jit(solution)/shard_map/ppermute | solution.py:458
  60.6 6.0 %collective-permute-start.1 = (f32[520,512]{1,0:T(8,128)}, f32[520,512]{1,0:T(8,128)}, u32[]{:S(2)}, u32[]{:S(2)}) collective-permute-start(f32[520,512]{1,0:T(8,128)} %get-tuple-element.43.mine_ref), channel_id=1, source_target_pairs={{0,32},{32,0},{64,96},{96,64},{128,160},{160,128},{192,224},{224,1... | collective-permute-start | bytes 3194888 | tf_op jit(solution)/shard_map/ppermute | solution.py:458
  64.6 6.2 %copy-start = (bf16[2,512,512]{2,1,0:T(8,128)(2,1)}, bf16[2,512,512]{2,1,0:T(8,128)(2,1)S(1)}, u32[]{:S(2)}) copy-start(bf16[2,512,512]{2,1,0:T(8,128)(2,1)S(1)} %get-tuple-element.66.op_ref) | copy-start | bytes 3145732
  64.6 24.9 %collective-permute-start.10 = (f32[512,512]{1,0:T(8,128)}, f32[512,512]{1,0:T(8,128)}, u32[]{:S(2)}, u32[]{:S(2)}) collective-permute-start(f32[512,512]{1,0:T(8,128)} %get-tuple-element.68.mine_ref), channel_id=1, source_target_pairs={{16,48},{48,16},{80,112},{112,80},{144,176},{176,144},{208,240},{2... | collective-permute-start | bytes 3145736 | tf_op jit(solution)/shard_map/ppermute | solution.py:458
  70.9 1.0 copy-start.6
  71.8 24.4 %collective-permute-start.2 = (f32[520,512]{1,0:T(8,128)}, f32[520,512]{1,0:T(8,128)}, u32[]{:S(2)}, u32[]{:S(2)}) collective-permute-start(f32[520,512]{1,0:T(8,128)} %get-tuple-element.44.mine_ref), channel_id=1, source_target_pairs={{0,64},{32,96},{64,0},{96,32},{128,192},{160,224},{192,128},{224,1... | collective-permute-start | bytes 3194888 | tf_op jit(solution)/shard_map/ppermute | solution.py:458
  93.2 1.0 copy-start.2
  94.2 77.1 %collective-permute-start.12 = (f32[512,512]{1,0:T(8,128)}, f32[512,512]{1,0:T(8,128)}, u32[]{:S(2)}, u32[]{:S(2)}) collective-permute-start(f32[512,512]{1,0:T(8,128)} %get-tuple-element.71.mine_ref), channel_id=1, source_target_pairs={{16,80},{48,112},{80,16},{112,48},{144,208},{176,240},{208,144},{2... | collective-permute-start | bytes 3145736 | tf_op jit(solution)/shard_map/ppermute | solution.py:458
  96.2 3.9 %copy-start.21 = (f32[512]{0:T(512)S(1)}, f32[512]{0:T(512)}, u32[]{:S(2)}) copy-start(f32[512]{0:T(512)} %param.8) | copy-start | bytes 6148
  101.0 0.7 collective-permute-start.3
  101.7 3.2 %copy-start.5 = (bf16[2,512,512]{2,1,0:T(8,128)(2,1)S(1)}, bf16[2,512,512]{2,1,0:T(8,128)(2,1)}, u32[]{:S(2)}) copy-start(bf16[2,512,512]{2,1,0:T(8,128)(2,1)} %copy-done.4) | copy-start | bytes 3145732
  101.7 3.2 %copy-start.7 = (bf16[2,512,512]{2,1,0:T(8,128)(2,1)S(1)}, bf16[2,512,512]{2,1,0:T(8,128)(2,1)}, u32[]{:S(2)}) copy-start(bf16[2,512,512]{2,1,0:T(8,128)(2,1)} %copy-done.6) | copy-start | bytes 3145732
  102.6 0.7 collective-permute-start.4
  104.2 0.7 collective-permute-start.5
  104.9 41.4 %copy-start.17 = (f32[16,64]{1,0:T(8,128)S(1)}, f32[16,64]{1,0:T(8,128)}, u32[]{:S(2)}) copy-start(f32[16,64]{1,0:T(8,128)} %y_ref.3) | copy-start | bytes 12292
  105.9 40.4 %collective-permute-start.6 = (f32[8,512]{1,0:T(8,128)S(1)}, f32[8,512]{1,0:T(8,128)S(1)}, u32[]{:S(2)}, u32[]{:S(2)}) collective-permute-start(f32[8,512]{1,0:T(8,128)S(1)} %get-tuple-element.60), channel_id=1, source_target_pairs={{0,16},{32,48},{64,80},{96,112},{128,144},{160,176},{192,208},{224... | collective-permute-start | bytes 49160 | tf_op jit(solution)/shard_map/ppermute | solution.py:458
  146.3 1.6 copy-start.9
  147.9 1.2 copy-start.20
  149.1 15.0 %copy-start.1 = (bf16[2,512,512]{2,1,0:T(8,128)(2,1)S(1)}, bf16[2,512,512]{2,1,0:T(8,128)(2,1)}, u32[]{:S(2)}) copy-start(bf16[2,512,512]{2,1,0:T(8,128)(2,1)} %copy-done) | copy-start | bytes 3145732
  161.1 3.1 %collective-permute-start.7 = (f32[8,512]{1,0:T(8,128)S(1)}, f32[8,512]{1,0:T(8,128)S(1)}, u32[]{:S(2)}, u32[]{:S(2)}) collective-permute-start(f32[8,512]{1,0:T(8,128)S(1)} %get-tuple-element.63.mine_ref.oo_ref), channel_id=1, source_target_pairs={{0,16},{32,48},{64,80},{96,112},{128,144},{160,176},{192,208},{224... | collective-permute-start | bytes 49160 | tf_op jit(solution)/shard_map/ppermute | solution.py:458
  164.5 4.5 %collective-permute-start.9 = (f32[8,512]{1,0:T(8,128)S(1)}, f32[8,512]{1,0:T(8,128)S(1)}, u32[]{:S(2)}, u32[]{:S(2)}) collective-permute-start(f32[8,512]{1,0:T(8,128)S(1)} %joined.3.mine_ref), channel_id=1, source_target_pairs={{16,48},{48,16},{80,112},{112,80},{144,176},{176,144},{208,240},{2... | collective-permute-start | bytes 49160 | tf_op jit(solution)/shard_map/ppermute | solution.py:458
  169.4 6.0 %collective-permute-start.11 = (f32[8,512]{1,0:T(8,128)S(1)}, f32[8,512]{1,0:T(8,128)S(1)}, u32[]{:S(2)}, u32[]{:S(2)}) collective-permute-start(f32[8,512]{1,0:T(8,128)S(1)} %joined.4.mine_ref), channel_id=1, source_target_pairs={{16,80},{48,112},{80,16},{112,48},{144,208},{176,240},{208,144},{2... | collective-permute-start | bytes 49160 | tf_op jit(solution)/shard_map/ppermute | solution.py:458
  171.3 4.1 %copy-start.3 = (bf16[2,512,512]{2,1,0:T(8,128)(2,1)S(1)}, bf16[2,512,512]{2,1,0:T(8,128)(2,1)}, u32[]{:S(2)}) copy-start(bf16[2,512,512]{2,1,0:T(8,128)(2,1)} %copy-done.2) | copy-start | bytes 3145732
  175.7 5.1 %collective-permute-start.13 = (f32[8,512]{1,0:T(8,128)S(1)}, f32[8,512]{1,0:T(8,128)S(1)}, u32[]{:S(2)}, u32[]{:S(2)}) collective-permute-start(f32[8,512]{1,0:T(8,128)S(1)} %joined.5.off_ref), channel_id=1, source_target_pairs={{144,16},{176,48},{208,80},{240,112},{272,144},{304,176},{336,208}... | collective-permute-start | bytes 49160 | tf_op jit(solution)/shard_map/ppermute | solution.py:458
  181.7 4.5 %collective-permute-start.14 = (f32[8,512]{1,0:T(8,128)S(1)}, f32[8,512]{1,0:T(8,128)S(1)}, u32[]{:S(2)}, u32[]{:S(2)}) collective-permute-start(f32[8,512]{1,0:T(8,128)S(1)} %get-tuple-element.75), channel_id=1, source_target_pairs={{144,16},{176,48},{208,80},{240,112},{272,144},{304,176},{336,208}... | collective-permute-start | bytes 49160 | tf_op jit(solution)/shard_map/ppermute | solution.py:458
  187.1 4.5 %collective-permute-start.15 = (f32[8,512]{1,0:T(8,128)S(1)}, f32[8,512]{1,0:T(8,128)S(1)}, u32[]{:S(2)}, u32[]{:S(2)}) collective-permute-start(f32[8,512]{1,0:T(8,128)S(1)} %get-tuple-element.77), channel_id=1, source_target_pairs={{144,16},{176,48},{208,80},{240,112},{272,144},{304,176},{336,208}... | collective-permute-start | bytes 49160 | tf_op jit(solution)/shard_map/ppermute | solution.py:458
  191.6 3.8 %copy-start.18 = (f32[16,512]{1,0:T(8,128)S(1)}, f32[16,512]{1,0:T(8,128)}, u32[]{:S(2)}) copy-start(f32[16,512]{1,0:T(8,128)} %get-tuple-element.39.x_ref) | copy-start | bytes 98308
  193.3 2.1 %collective-permute-start.16 = (f32[8,512]{1,0:T(8,128)S(1)}, f32[8,512]{1,0:T(8,128)S(1)}, u32[]{:S(2)}, u32[]{:S(2)}) collective-permute-start(f32[8,512]{1,0:T(8,128)S(1)} %get-tuple-element.79), channel_id=1, source_target_pairs={{16,0},{48,32},{80,64},{112,96},{144,128},{176,160},{208,192},{240... | collective-permute-start | bytes 49160 | tf_op jit(solution)/shard_map/ppermute | solution.py:458

commit v3 on v2

--- a/solution.py
+++ b/solution.py
@@ -120,18 +120,23 @@
     return high[:rows] + (high[rows:] + low[:rows] + low[rows:])
 
 
-def call(kernel, name, outs, operands, scratch=(), scalars=1, flops=10**8, moved=1 << 20):
+def call(kernel, name, outs, operands, scratch=(), scalars=1, far=0, flops=10**8, moved=1 << 20, limit=16):
     vmem, smem = pl.BlockSpec(memory_space=pltpu.VMEM), pl.BlockSpec(memory_space=pltpu.SMEM)
+    anywhere = pl.BlockSpec(memory_space=pltpu.MemorySpace.HBM)
+    near_hbm = [
+        pltpu.with_memory_space_constraint(value, pltpu.MemorySpace.HBM)
+        for value in operands[scalars : scalars + far]
+    ]
     return pl.pallas_call(
         kernel,
         out_shape=tuple(jax.ShapeDtypeStruct(*out) for out in outs),
-        in_specs=[smem] * scalars + [vmem] * (len(operands) - scalars),
+        in_specs=[smem] * scalars + [anywhere] * far + [vmem] * (len(operands) - scalars - far),
         out_specs=(vmem,) * len(outs),
         scratch_shapes=list(scratch),
         cost_estimate=pl.CostEstimate(flops=flops, bytes_accessed=moved, transcendentals=0),
-        compiler_params=pltpu.CompilerParams(vmem_limit_bytes=32 << 20),
+        compiler_params=pltpu.CompilerParams(vmem_limit_bytes=limit << 20),
         name=name,
-    )(*operands)
+    )(*operands[:scalars], *near_hbm, *operands[scalars + far :])
 
 
 PARTS = ((2, N, N), BF16)
@@ -181,18 +186,29 @@
     steps = offsets.shape[0]
 
     def kernel(
-        offs_ref, cells_ref, up_ref, c_ref, obs_ref, gains_ref, y_ref,
-        map_ref, parts_ref, off_ref, s_ref, held_ref, moved_ref, picked_ref, ups_ref, cs_ref
+        offs_ref, cells_ref, up_far, c_far, obs_far, y_far, gains_far,
+        map_ref, parts_ref, off_ref, s_ref, held_ref, moved_ref, picked_ref, ups_ref, cs_ref,
+        up_ref, c_ref, obs_ref, y_ref, gains_ref, sem
     ):
+        pairs = ((up_far, up_ref), (c_far, c_ref), (obs_far, obs_ref), (y_far, y_ref))
+        copies = [pltpu.make_async_copy(a, b, sem.at[i]) for i, (a, b) in enumerate(pairs)]
+        for copy in copies:
+            copy.start()
+        fetch = lambda k: pltpu.make_async_copy(gains_far.at[k], gains_ref.at[k], sem.at[4 + k])
+        for k in range(steps):
+            fetch(k).start()
+        start_identity(held_ref)
+        for copy in copies:
+            copy.wait()
         keep_columns(up_ref, ups_ref, 0)
         keep_columns(c_ref, cs_ref, 0)
-        start_identity(held_ref)
         head = lax.broadcasted_iota(jnp.int32, (8, 1), 0) == 0
 
         def one(k, vec):
             step = Step(k, offs_ref, up_ref, c_ref)
             s = one_hot(obs_ref[pl.ds(k, 1), :])
             s_ref[k] = s
+            fetch(k).wait()
             gain = RELAXATION * s.astype(F32) + gains_ref[k]
             for r in range(0, N, CELLS):
                 ups, cs = ups_ref[k, r : r + CELLS, :], cs_ref[k, r : r + CELLS, :]
@@ -233,17 +249,25 @@
         kernel,
         "filter_map",
         (((ROWS, N), F32), PARTS, VECTOR, ((steps, OBS, N), BF16)),
-        (offsets, obs_cells, upwind, courant, obs_cells, gains, observed),
+        (offsets, obs_cells, upwind, courant, obs_cells, observed, gains),
         scratch=[
             pltpu.VMEM((PIECES, N + 2 * REACH, LANES), F32),
             pltpu.VMEM((PIECES, N, LANES), F32),
             pltpu.VMEM((OBS, N), F32),
             pltpu.VMEM((steps, N, LANES), F32),
             pltpu.VMEM((steps, N, LANES), F32),
+            pltpu.VMEM((steps, N), jnp.int32),
+            pltpu.VMEM((steps, N), F32),
+            pltpu.VMEM((steps, OBS), jnp.int32),
+            pltpu.VMEM((steps, OBS), F32),
+            pltpu.VMEM((steps, OBS, N), F32),
+            pltpu.SemaphoreType.DMA((4 + steps,)),
         ],
         scalars=2,
+        far=5,
         flops=16 * 10**9,
         moved=4 << 20,
+        limit=28,
     )
 
 
@@ -300,32 +324,39 @@
         ],
         flops=8 * 10**9,
         moved=2 << 20,
-    )
-
-
-def compose(flag, mine, other):
+        limit=28,
+    )
+
+
+def compose(flag, mine, other, keep=True, parts=False, other_parts=False):
     rows = mine.shape[0]
     affine = rows > N
-
-    def kernel(flag_ref, mine_ref, other_ref, out_ref, parts_ref, other_parts_ref, *offs):
-        keep_parts(other_ref, other_parts_ref)
-        if affine:
-            offs[1][...] = other_ref[N:ROWS, :]
+    kinds = (("out", keep, ((rows, N), F32)), ("off", affine, VECTOR), ("parts", parts, PARTS), ("other", other_parts, PARTS))
+
+    def kernel(flag_ref, mine_ref, other_ref, *out_refs):
+        refs = dict(zip([name for name, wanted, _ in kinds if wanted], out_refs, strict=True))
 
         def product(first_ref, second_ref):
+            if other_parts:
+                keep_parts(other_ref, refs["other"])
             high, low = split2(first_ref[0:N, :])
             for start in (0, 256):
                 at = pl.ds(start, 256)
                 both = stacked(second_ref[at, :])
                 big = dot(both, high)
-                out_ref[at, :] = big[:256] + (big[256:] + dot(both[:256], low))
+                total = big[:256] + (big[256:] + dot(both[:256], low))
+                if keep:
+                    refs["out"][at, :] = total
+                if parts:
+                    refs["parts"][0, at, :], refs["parts"][1, at, :] = split2(total)
             if affine:
                 both = stacked(first_ref[N:ROWS, :])
-                keep = split2(second_ref[0:N, :])
-                big, small = dot(both, keep[0], NT), dot(both, keep[1], NT)
+                halves = split2(second_ref[0:N, :])
+                big, small = dot(both, halves[0], NT), dot(both, halves[1], NT)
                 offset = big[:8] + (big[8:] + small[:8] + small[8:]) + second_ref[N:ROWS, :]
-                out_ref[N:ROWS, :] = offset
-                offs[0][...] = offset
+                refs["off"][...] = offset
+                if keep:
+                    refs["out"][N:ROWS, :] = offset
 
         @pl.when(flag_ref[0] == 1)
         def _():
@@ -335,10 +366,16 @@
         def _():
             product(mine_ref, other_ref)
 
-        keep_parts(out_ref, parts_ref)
-
-    outs = (((rows, N), F32), PARTS, PARTS) + ((VECTOR, VECTOR) if affine else ())
+    outs = tuple(shape for _, wanted, shape in kinds if wanted)
     return call(kernel, "compose", outs, (flag, mine, other), flops=10**9, moved=5 << 20)
+
+
+def parted(maps):
+    def kernel(map_ref, parts_ref, off_ref):
+        keep_parts(map_ref, parts_ref)
+        off_ref[...] = map_ref[N:ROWS, :]
+
+    return call(kernel, "parted", (PARTS, VECTOR), (maps,), scalars=0, flops=10**8, moved=2 << 20)
 
 
 def hop(place, mark, state, got, parts, offset):
@@ -397,12 +434,24 @@
     steps = offsets.shape[0]
 
     def kernel(
-        place_ref, offs_ref, up_ref, c_ref, sg_ref, s_ref, gains_ref, y_ref, state_ref, got_ref, filt_ref, upd_ref, end_ref
+        place_ref, offs_ref, s_far, gains_far, up_ref, c_ref, sg_ref, y_ref, state_ref, got_ref,
+        filt_ref, upd_ref, end_ref, s_ref, gains_ref, sem
     ):
+        def fetch(k):
+            return (
+                pltpu.make_async_copy(s_far.at[k], s_ref.at[k], sem.at[k]),
+                pltpu.make_async_copy(gains_far.at[k], gains_ref.at[k], sem.at[steps + k]),
+            )
+
+        for k in range(steps):
+            for copy in fetch(k):
+                copy.start()
         first = lax.broadcasted_iota(jnp.int32, (8, 1), 0) == 0
 
         def one(k, vec):
             step = Step(k, offs_ref, up_ref, c_ref)
+            for copy in fetch(k):
+                copy.wait()
             s = s_ref[k]
             kk = gain_rows(s, gains_ref[k])
             s4 = jnp.concatenate([s] * 4, axis=0)
@@ -423,8 +472,14 @@
         kernel,
         "forward",
         (((steps, N), F32), ((steps, N), F32), VECTOR),
-        (place, offsets, upwind, courant, smooth_gain, hots, gains, observed, state, got),
+        (place, offsets, hots, gains, upwind, courant, smooth_gain, observed, state, got),
+        scratch=[
+            pltpu.VMEM((steps, OBS, N), BF16),
+            pltpu.VMEM((steps, OBS, N), F32),
+            pltpu.SemaphoreType.DMA((2 * steps,)),
+        ],
         scalars=2,
+        far=2,
         flops=4 * 10**9,
         moved=3 << 20,
     )
@@ -462,39 +517,50 @@
     ints = lambda *values: jnp.stack([jnp.asarray(v, jnp.int32) for v in values])
     never = jnp.zeros((1,), jnp.int32)
     at_core = ints(core)
-    y_odd, y_even, y_high, y_low = ints(y % 2 == 1), ints(y % 2 == 0), ints(y >= 2), ints(y < 2)
+    on_even = lambda flag: ints(jnp.where(core == 0, flag, 2))
+    on_odd = lambda flag: ints(jnp.where(core == 1, flag, 2))
+    y_even, y_low = ints(y % 2 == 0), ints(y < 2)
     start_row = jnp.broadcast_to(initial[None, :], (8, N))
     zeros = jnp.zeros((8, N), F32)
 
+    after = lambda value, *before: lax.optimization_barrier((value, *before))[0]
+
     fmap, fmap_p, fmap_o, hots = filter_map(offsets, upwind, courant, obs_cells, gains, observed)
     fmap_odd = moved(fmap, lambda i: i - 1, odd)
-    fpair, fpair_p, _, _, _ = compose(never, fmap, fmap_odd)
+    fpair, fpair_o = compose(on_even(0), fmap, fmap_odd)
     fpair_other = moved(fpair, lambda i: i ^ 2, even)
-    smap, smap_p = smoother_map(offsets, upwind, courant, smooth_gain)
+    smap, smap_p = smoother_map(offsets, after(upwind, fpair_o), courant, smooth_gain)
     smap_even = moved(smap, lambda i: i + 1, even)
-    fquad, fquad_p, fpair_op, _, fpair_oo = compose(y_odd, fpair, fpair_other)
+    fquad, fquad_o = compose(on_even(y % 2), fpair, fpair_other)
     fquad_other = moved(fquad, lambda i: i ^ 4, even)
-    spair, spair_p, smap_ep = compose(never, smap, smap_even)
-    spair_other = moved(spair, lambda i: i ^ 2, odd)
-    foct, foct_p, fquad_op, foct_o, fquad_oo = compose(y_high, fquad, fquad_other)
+    smap_even = after(smap_even, fquad_o)
+    spair, spair_p, smap_ep = compose(on_odd(0), smap, smap_even, parts=True, other_parts=True)
+    fpair_op, fpair_oo = parted(fpair_other)
+    foct_o, foct_p = compose(on_even(y // 2), fquad, fquad_other, keep=False, parts=True)
+    spair_other = moved(after(spair, foct_o), lambda i: i ^ 2, odd)
 
     place3 = ints(x, y >= 2, y % 2 == 1)
     ahead_of = lambda v: moved(v, lambda i: i + 8, lambda i: even(i) and i < 24)
     state, sent = hop(place3, 0, start_row, start_row, foct_p, foct_o)
     got = ahead_of(sent)
-    squad, squad_p, spair_op = compose(y_even, spair, spair_other)
-    squad_other = moved(squad, lambda i: i ^ 4, odd)
-    state, sent = hop(place3, 1, state, got, foct_p, foct_o)
+    fquad_op, fquad_oo = parted(fquad_other)
+    state, sent = hop(place3, 1, after(state, fquad_oo), got, foct_p, foct_o)
     got = ahead_of(sent)
     state, sent = hop(place3, 2, state, got, foct_p, foct_o)
     got = ahead_of(sent)
+    squad, squad_p, spair_op = compose(
+        on_odd(1 - y % 2), spair, after(spair_other, sent), parts=True, other_parts=True
+    )
+    squad_other = moved(squad, lambda i: i ^ 4, odd)
     state, sent = descend(
-        place3, 3, state, got, fquad_op, fquad_oo, fpair_op, fpair_oo, fmap_p, fmap_o
+        place3, 3, after(state, squad_p), got, fquad_op, fquad_oo, fpair_op, fpair_oo, fmap_p, fmap_o
     )
     got = moved(sent, lambda i: i + 1, even)
-    _, soct_p, squad_op = compose(y_low, squad, squad_other)
     filtered, updates, own = forward(
         at_core, offsets, upwind, courant, smooth_gain, hots, gains, observed, state, got
+    )
+    soct_p, squad_op = compose(
+        on_odd(1 - y // 2), squad, after(squad_other, own), keep=False, parts=True, other_parts=True
     )
 
     pair = joined(never, own, moved(own, lambda i: i + 1, even), smap_p, smap_ep)

time: 200 us -> 178 us (0.89)
  waiting for transfers between devices: 70.7 us -> 53.3 us
  local copies, waits for them, and re-layouts: 10.1 us -> 3.79 us
  starting transfers between devices: 30.9 us -> 33.9 us
    ppermute x17, waiting for transfers between devices: 70.7 us -> 53.3 us  [moved(): lax.ppermute(values, 'tm', [(i, to(i)) for i in range(32) if senders(i)])]
    unnamed x45 -> x35, local copies, waits for them, and re-layouts: 10.1 us -> 3.78 us
    ppermute x17, starting transfers between devices: 30.9 us -> 33.9 us  [moved(): lax.ppermute(values, 'tm', [(i, to(i)) for i in range(32) if senders(i)])]
    pallas_call x20 -> x22, Pallas kernels: 86.4 us -> 85.6 us  [call(): pl.pallas_call(kernel, out_shape=tuple((jax.ShapeDtypeStruct(*out) for ou...]
  transfers between devices with their start and end apart: 17 -> 17, of which waited for: 9 -> 10; matrix products, arithmetic and copies ran while one was open for 0% -> 0% of each run, Pallas kernels for 27% -> 25%
where the time goes in v3:
time: 178 us
  Pallas kernels  85.6 us (48%)
  waiting for transfers between devices  53.3 us (30%)
  starting transfers between devices  33.9 us (19%)
  local copies, waits for them, and re-layouts  3.79 us (2%)
    pallas_call x22, Pallas kernels, call(): pl.pallas_call(kernel, out_shape=tuple((jax.ShapeDtypeStruct(*out) for ou...  85.6 us
    ppermute x17, waiting for transfers between devices, moved(): lax.ppermute(values, 'tm', [(i, to(i)) for i in range(32) if senders(i)])  53.3 us
    ppermute x17, starting transfers between devices, moved(): lax.ppermute(values, 'tm', [(i, to(i)) for i in range(32) if senders(i)])  33.9 us
    unnamed x35, local copies, waits for them, and re-layouts  3.78 us
  transfers between devices with their start and end apart: 17, of which 10 were waited for; matrix products, arithmetic and copies ran while one was open for 0% of the time, Pallas kernels for 25%

profile of v3, /device:TPU:1, one launch (start us, length us, event | category | flops | bytes accessed | tf_op | source)
XLA Modules:
  0.0 177.8 jit_solution(15256436411787699292)
XLA Ops:
  0.6 0.8 copy.12.offs_ref
  1.4 26.4 %filter_map.1 = (f32[520,512]{1,0:T(8,128)S(1)}, bf16[2,512,512]{2,1,0:T(8,128)(2,1)S(1)}, f32[8,512]{1,0:T(8,128)S(1)}, bf16[16,64,512]{2,1,0:T(8,128)(2,1)S(1)}) custom-call(s32[16,4]{1,0:T(8,128)S(1)} %copy.12.offs_ref, s32[16,64]{1,0:T(8,128)} %obs_far.1, s32[16,512]{1,0:T(8,128)} %up_ref.4, f32[16,512]{1,0:T(8,128)} %c_ref.5, s32[16,64]{1,0:T(8,128)} %obs_far.1, ...), custom_call_target="tpu_custom_call" | custom-call | flops 16000000000 | bytes 4194304 | tf_op jit(solution)/shard_map/filter_map/pallas_call | solution.py:130
  27.8 1.0 copy-done.6
  28.8 1.0 copy-done.15
  29.7 8.8 %collective-permute-start = (f32[520,512]{1,0:T(8,128)S(1)}, f32[520,512]{1,0:T(8,128)S(1)}, u32[]{:S(2)}, u32[]{:S(2)}) collective-permute-start(f32[520,512]{1,0:T(8,128)S(1)} %get-tuple-element.47.mine_ref), channel_id=1, source_target_pairs={{16,0},{48,32},{80,64},{112,96},{144,128},{176,160},{208,192},{240... | collective-permute-start | bytes 3194888 | tf_op jit(solution)/shard_map/ppermute | solution.py:513
  38.6 2.2 %collective-permute-done.other_ref = f32[520,512]{1,0:T(8,128)S(1)} collective-permute-done((f32[520,512]{1,0:T(8,128)S(1)}, f32[520,512]{1,0:T(8,128)S(1)}, u32[]{:S(2)}, u32[]{:S(2)}) %collective-permute-start) | collective-permute-done | bytes 1064992 | tf_op jit(solution)/shard_map/ppermute | solution.py:513
  40.8 1.0 compose.6
  41.8 0.7 collective-permute-start.1
  42.6 16.9 %smoother_map.1 = (f32[512,512]{1,0:T(8,128)S(1)}, bf16[2,512,512]{2,1,0:T(8,128)(2,1)S(1)}) custom-call(s32[16,4]{1,0:T(8,128)S(1)} %copy.12.offs_ref, s32[16,512]{1,0:T(8,128)S(1)} %copy-done.10, f32[16,512]{1,0:T(8,128)S(1)} %copy-done.11, f32[16,512]{1,0:T(8,128)S(1)} %copy-done.12), custom_call_target="tpu_custom_call" | custom-call | flops 8000000000 | bytes 2097152 | tf_op jit(solution)/shard_map/smoother_map/pallas_call | solution.py:130
  59.4 1.3 collective-permute-start.5
  60.8 2.2 %compose.7 = (f32[520,512]{1,0:T(8,128)}, f32[8,512]{1,0:T(8,128)}) custom-call(s32[1]{0:T(128)} %bitcast.5.flag_ref, f32[520,512]{1,0:T(8,128)} %get-tuple-element.48.mine_ref, f32[520,512]{1,0:T(8,128)S(1)} %collective-permute-done.1.other_ref.map_ref), custom_call_target="tpu_custom_call" | custom-call | flops 1000000000 | bytes 5242880 | tf_op jit(solution)/shard_map/compose/pallas_call | solution.py:130
  63.0 1.7 collective-permute-start.2
  64.7 1.2 collective-permute-done.5.other_ref
  65.9 3.3 %compose.9 = (f32[512,512]{1,0:T(8,128)}, bf16[2,512,512]{2,1,0:T(8,128)(2,1)S(1)}, bf16[2,512,512]{2,1,0:T(8,128)(2,1)S(1)}) custom-call(s32[1]{0:T(128)} %bitcast.8.flag_ref, f32[512,512]{1,0:T(8,128)S(1)} %get-tuple-element.59.mine_ref, f32[512,512]{1,0:T(8,128)} %collective-permute-done.5.other_ref), custom_call_target="tpu_custom_call" | custom-call | flops 1000000000 | bytes 5242880 | tf_op jit(solution)/shard_map/compose/pallas_call | solution.py:130
  69.2 2.3 %compose.8 = (f32[8,512]{1,0:T(8,128)S(1)}, bf16[2,512,512]{2,1,0:T(8,128)(2,1)S(1)}) custom-call(s32[1]{0:T(128)} %bitcast.4.flag_ref, f32[520,512]{1,0:T(8,128)} %get-tuple-element.49.mine_ref, f32[520,512]{1,0:T(8,128)} %collective-permute-done.2.other_ref.map_ref), custom_call_target="tpu_custom_call" | custom-call | flops 1000000000 | bytes 5242880 | tf_op jit(solution)/shard_map/compose/pallas_call | solution.py:130
  71.5 3.3 %collective-permute-start.6 = (f32[512,512]{1,0:T(8,128)}, f32[512,512]{1,0:T(8,128)}, u32[]{:S(2)}, u32[]{:S(2)}) collective-permute-start(f32[512,512]{1,0:T(8,128)} %get-tuple-element.61.mine_ref), channel_id=1, source_target_pairs={{16,48},{48,16},{80,112},{112,80},{144,176},{176,144},{208,240},{2... | collective-permute-start | bytes 3145736 | tf_op jit(solution)/shard_map/ppermute | solution.py:513
  75.0 0.9 hop.5
  75.9 0.7 collective-permute-start.3
  76.6 1.4 parted.2
  77.9 1.0 copy-done.8
  79.0 0.9 hop.6
  79.9 0.7 collective-permute-start.4
  80.6 0.9 hop.7
  81.5 14.3 %collective-permute-done.6.other_ref = f32[512,512]{1,0:T(8,128)} collective-permute-done((f32[512,512]{1,0:T(8,128)}, f32[512,512]{1,0:T(8,128)}, u32[]{:S(2)}, u32[]{:S(2)}) %collective-permute-start.6) | collective-permute-done | bytes 1048608 | tf_op jit(solution)/shard_map/ppermute | solution.py:513
  95.8 3.7 %compose.10 = (f32[512,512]{1,0:T(8,128)}, bf16[2,512,512]{2,1,0:T(8,128)(2,1)S(1)}, bf16[2,512,512]{2,1,0:T(8,128)(2,1)S(1)}) custom-call(s32[1]{0:T(128)} %bitcast.7.flag_ref, f32[512,512]{1,0:T(8,128)} %get-tuple-element.61.mine_ref, f32[512,512]{1,0:T(8,128)} %collective-permute-done.6.other_ref), custom_call_target="tpu_custom_call" | custom-call | flops 1000000000 | bytes 5242880 | tf_op jit(solution)/shard_map/compose/pallas_call | solution.py:130
  99.6 2.0 %collective-permute-start.12 = (f32[512,512]{1,0:T(8,128)}, f32[512,512]{1,0:T(8,128)}, u32[]{:S(2)}, u32[]{:S(2)}) collective-permute-start(f32[512,512]{1,0:T(8,128)} %get-tuple-element.80.mine_ref), channel_id=1, source_target_pairs={{16,80},{48,112},{80,16},{112,48},{144,208},{176,240},{208,144},{2... | collective-permute-start | bytes 3145736 | tf_op jit(solution)/shard_map/ppermute | solution.py:513
  102.5 0.9 descend.2
  103.4 1.3 collective-permute-start.8
  104.7 21.1 %collective-permute-done.8.got_ref = f32[8,512]{1,0:T(8,128)S(1)} collective-permute-done((f32[8,512]{1,0:T(8,128)S(1)}, f32[8,512]{1,0:T(8,128)S(1)}, u32[]{:S(2)}, u32[]{:S(2)}) %collective-permute-start.8) | collective-permute-done | bytes 16416 | tf_op jit(solution)/shard_map/ppermute | solution.py:513
  125.8 13.3 %forward.1 = (f32[16,512]{1,0:T(8,128)}, f32[16,512]{1,0:T(8,128)S(1)}, f32[8,512]{1,0:T(8,128)S(1)}) custom-call(s32[1]{0:T(128)} %bitcast.place_ref, s32[16,4]{1,0:T(8,128)S(1)} %copy.12.offs_ref, bf16[16,64,512]{2,1,0:T(8,128)(2,1)} %copy-done.15, f32[16,64,512]{2,1,0:T(8,128)} %gains_far.3, s32[16,512]{1,0:T(8,128)S(1)} %copy-done.10, ...), custom_call_target="tpu_custom_call" | custom-call | flops 4000000000 | bytes 3145728 | tf_op jit(solution)/shard_map/forward/pallas_call | solution.py:130
  139.2 1.3 collective-permute-start.9
  140.5 1.8 collective-permute-done.9.other_ref
  142.6 2.6 %collective-permute-start.10 = (f32[8,512]{1,0:T(8,128)S(1)}, f32[8,512]{1,0:T(8,128)S(1)}, u32[]{:S(2)}, u32[]{:S(2)}) collective-permute-start(f32[8,512]{1,0:T(8,128)S(1)} %joined.3.mine_ref), channel_id=1, source_target_pairs={{16,48},{48,16},{80,112},{112,80},{144,176},{176,144},{208,240},{2... | collective-permute-start | bytes 49160 | tf_op jit(solution)/shard_map/ppermute | solution.py:513
  145.2 1.9 %collective-permute-done.10.other_ref.po_ref = f32[8,512]{1,0:T(8,128)S(1)} collective-permute-done((f32[8,512]{1,0:T(8,128)S(1)}, f32[8,512]{1,0:T(8,128)S(1)}, u32[]{:S(2)}, u32[]{:S(2)}) %collective-permute-start.10) | collective-permute-done | bytes 16416 | tf_op jit(solution)/shard_map/ppermute | solution.py:513
  147.5 3.6 %collective-permute-start.11 = (f32[8,512]{1,0:T(8,128)S(1)}, f32[8,512]{1,0:T(8,128)S(1)}, u32[]{:S(2)}, u32[]{:S(2)}) collective-permute-start(f32[8,512]{1,0:T(8,128)S(1)} %joined.4.mine_ref), channel_id=1, source_target_pairs={{16,80},{48,112},{80,16},{112,48},{144,208},{176,240},{208,144},{2... | collective-permute-start | bytes 49160 | tf_op jit(solution)/shard_map/ppermute | solution.py:513
  151.1 2.8 %compose.11 = (bf16[2,512,512]{2,1,0:T(8,128)(2,1)S(1)}, bf16[2,512,512]{2,1,0:T(8,128)(2,1)S(1)}) custom-call(s32[1]{0:T(128)} %bitcast.11.flag_ref, f32[512,512]{1,0:T(8,128)} %get-tuple-element.80.mine_ref, f32[512,512]{1,0:T(8,128)} %collective-permute-done.12.other_ref), custom_call_target="tpu_custom_call" | custom-call | flops 1000000000 | bytes 5242880 | tf_op jit(solution)/shard_map/compose/pallas_call | solution.py:130
  154.3 1.3 collective-permute-start.13
  155.7 3.7 %collective-permute-done.13.got_ref = f32[8,512]{1,0:T(8,128)S(1)} collective-permute-done((f32[8,512]{1,0:T(8,128)S(1)}, f32[8,512]{1,0:T(8,128)S(1)}, u32[]{:S(2)}, u32[]{:S(2)}) %collective-permute-start.13) | collective-permute-done | bytes 16416 | tf_op jit(solution)/shard_map/ppermute | solution.py:513
  159.3 0.9 hop.8
  160.3 1.3 collective-permute-start.14
  161.6 3.2 %collective-permute-done.14.got_ref = f32[8,512]{1,0:T(8,128)S(1)} collective-permute-done((f32[8,512]{1,0:T(8,128)S(1)}, f32[8,512]{1,0:T(8,128)S(1)}, u32[]{:S(2)}, u32[]{:S(2)}) %collective-permute-start.14) | collective-permute-done | bytes 16416 | tf_op jit(solution)/shard_map/ppermute | solution.py:513
  164.8 0.9 hop.9
  165.7 1.3 collective-permute-start.15
  167.0 3.2 %collective-permute-done.15.got_ref = f32[8,512]{1,0:T(8,128)S(1)} collective-permute-done((f32[8,512]{1,0:T(8,128)S(1)}, f32[8,512]{1,0:T(8,128)S(1)}, u32[]{:S(2)}, u32[]{:S(2)}) %collective-permute-start.15) | collective-permute-done | bytes 16416 | tf_op jit(solution)/shard_map/ppermute | solution.py:513
  170.2 1.7 descend.3
  171.9 1.3 collective-permute-start.16
  173.2 0.8 collective-permute-done.16.got_ref
  174.0 3.9 %smooth.1 = f32[16,512]{1,0:T(8,128)} custom-call(s32[1]{0:T(128)} %bitcast.place_ref, s32[16,4]{1,0:T(8,128)S(1)} %copy.12.offs_ref, s32[16,512]{1,0:T(8,128)S(1)} %copy-done.10, f32[16,512]{1,0:T(8,128)S(1)} %copy-done.11, f32[16,512]{1,0:T(8,128)S(1)} %copy-done.12, f32[16,512]{1,0:T(8,128)S(1)} %get-tuple-element.74.u_ref, f32[16,512]{1,0:T(8,128)S(1)} %copy-done.14, ...), custom_call_target="tpu_custom_call" | custom-call | flops 100000000 | bytes 1048576 | tf_op jit(solution)/shard_map/smooth/pallas_call | solution.py:130
  (47 shorter events, 2.2 us)
Async XLA Ops:
  27.8 1.0 copy-start.6
  28.8 1.0 copy-start.15
  29.7 11.1 %collective-permute-start = (f32[520,512]{1,0:T(8,128)S(1)}, f32[520,512]{1,0:T(8,128)S(1)}, u32[]{:S(2)}, u32[]{:S(2)}) collective-permute-start(f32[520,512]{1,0:T(8,128)S(1)} %get-tuple-element.47.mine_ref), channel_id=1, source_target_pairs={{16,0},{48,32},{80,64},{112,96},{144,128},{176,160},{208,192},{240... | collective-permute-start | bytes 3194888 | tf_op jit(solution)/shard_map/ppermute | solution.py:513
  40.8 1.7 copy-start.10
  40.8 1.8 copy-start.11
  40.8 1.8 copy-start.12
  41.8 19.0 %collective-permute-start.1 = (f32[520,512]{1,0:T(8,128)}, f32[520,512]{1,0:T(8,128)S(1)}, u32[]{:S(2)}, u32[]{:S(2)}) collective-permute-start(f32[520,512]{1,0:T(8,128)} %get-tuple-element.48.mine_ref), channel_id=1, source_target_pairs={{0,32},{32,0},{64,96},{96,64},{128,160},{160,128},{192,224},{224,1... | collective-permute-start | bytes 3194888 | tf_op jit(solution)/shard_map/ppermute | solution.py:513
  59.4 6.4 %collective-permute-start.5 = (f32[512,512]{1,0:T(8,128)S(1)}, f32[512,512]{1,0:T(8,128)}, u32[]{:S(2)}, u32[]{:S(2)}) collective-permute-start(f32[512,512]{1,0:T(8,128)S(1)} %get-tuple-element.59.mine_ref), channel_id=1, source_target_pairs={{0,16},{32,48},{64,80},{96,112},{128,144},{160,176},{192,208},{224... | collective-permute-start | bytes 3145736 | tf_op jit(solution)/shard_map/ppermute | solution.py:513
  63.0 6.2 %collective-permute-start.2 = (f32[520,512]{1,0:T(8,128)}, f32[520,512]{1,0:T(8,128)}, u32[]{:S(2)}, u32[]{:S(2)}) collective-permute-start(f32[520,512]{1,0:T(8,128)} %get-tuple-element.49.mine_ref), channel_id=1, source_target_pairs={{0,64},{32,96},{64,0},{96,32},{128,192},{160,224},{192,128},{224,1... | collective-permute-start | bytes 3194888 | tf_op jit(solution)/shard_map/ppermute | solution.py:513
  69.2 2.3 %copy-start = (bf16[2,512,512]{2,1,0:T(8,128)(2,1)}, bf16[2,512,512]{2,1,0:T(8,128)(2,1)S(1)}, u32[]{:S(2)}) copy-start(bf16[2,512,512]{2,1,0:T(8,128)(2,1)S(1)} %get-tuple-element.78.mp_ref) | copy-start | bytes 3145732
  69.2 2.3 %copy-start.2 = (bf16[2,512,512]{2,1,0:T(8,128)(2,1)}, bf16[2,512,512]{2,1,0:T(8,128)(2,1)S(1)}, u32[]{:S(2)}) copy-start(bf16[2,512,512]{2,1,0:T(8,128)(2,1)S(1)} %get-tuple-element.77.op_ref) | copy-start | bytes 3145732
  69.2 5.8 %copy-start.16 = (f32[512]{0:T(512)S(1)}, f32[512]{0:T(512)}, u32[]{:S(2)}) copy-start(f32[512]{0:T(512)} %param.8) | copy-start | bytes 6148
  71.5 24.3 %collective-permute-start.6 = (f32[512,512]{1,0:T(8,128)}, f32[512,512]{1,0:T(8,128)}, u32[]{:S(2)}, u32[]{:S(2)}) collective-permute-start(f32[512,512]{1,0:T(8,128)} %get-tuple-element.61.mine_ref), channel_id=1, source_target_pairs={{16,48},{48,16},{80,112},{112,80},{144,176},{176,144},{208,240},{2... | collective-permute-start | bytes 3145736 | tf_op jit(solution)/shard_map/ppermute | solution.py:513
  75.9 3.1 %collective-permute-start.3 = (f32[8,512]{1,0:T(8,128)S(1)}, f32[8,512]{1,0:T(8,128)S(1)}, u32[]{:S(2)}, u32[]{:S(2)}) collective-permute-start(f32[8,512]{1,0:T(8,128)S(1)} %get-tuple-element.55), channel_id=1, source_target_pairs={{0,128},{32,160},{64,192},{96,224},{128,256},{160,288},{192,320},{... | collective-permute-start | bytes 49160 | tf_op jit(solution)/shard_map/ppermute | solution.py:513
  77.9 1.0 copy-start.8
  79.9 0.7 collective-permute-start.4
  95.8 6.6 %copy-start.9 = (bf16[2,512,512]{2,1,0:T(8,128)(2,1)S(1)}, bf16[2,512,512]{2,1,0:T(8,128)(2,1)}, u32[]{:S(2)}) copy-start(bf16[2,512,512]{2,1,0:T(8,128)(2,1)} %copy-done.8) | copy-start | bytes 3145732
  99.6 2.9 %copy-start.4 = (bf16[2,512,512]{2,1,0:T(8,128)(2,1)}, bf16[2,512,512]{2,1,0:T(8,128)(2,1)S(1)}, u32[]{:S(2)}) copy-start(bf16[2,512,512]{2,1,0:T(8,128)(2,1)S(1)} %get-tuple-element.64.mp_ref) | copy-start | bytes 3145732
  99.6 2.9 %copy-start.7 = (bf16[2,512,512]{2,1,0:T(8,128)(2,1)S(1)}, bf16[2,512,512]{2,1,0:T(8,128)(2,1)}, u32[]{:S(2)}) copy-start(bf16[2,512,512]{2,1,0:T(8,128)(2,1)} %copy-done.6) | copy-start | bytes 3145732
  99.6 51.5 %collective-permute-start.12 = (f32[512,512]{1,0:T(8,128)}, f32[512,512]{1,0:T(8,128)}, u32[]{:S(2)}, u32[]{:S(2)}) collective-permute-start(f32[512,512]{1,0:T(8,128)} %get-tuple-element.80.mine_ref), channel_id=1, source_target_pairs={{16,80},{48,112},{80,16},{112,48},{144,208},{176,240},{208,144},{2... | collective-permute-start | bytes 3145736 | tf_op jit(solution)/shard_map/ppermute | solution.py:513
  101.6 0.8 collective-permute-start.7
  102.4 23.4 %copy-start.13 = (f32[16,64]{1,0:T(8,128)S(1)}, f32[16,64]{1,0:T(8,128)}, u32[]{:S(2)}) copy-start(f32[16,64]{1,0:T(8,128)} %y_ref.1) | copy-start | bytes 12292
  103.4 22.4 %collective-permute-start.8 = (f32[8,512]{1,0:T(8,128)S(1)}, f32[8,512]{1,0:T(8,128)S(1)}, u32[]{:S(2)}, u32[]{:S(2)}) collective-permute-start(f32[8,512]{1,0:T(8,128)S(1)} %get-tuple-element.72), channel_id=1, source_target_pairs={{0,16},{32,48},{64,80},{96,112},{128,144},{160,176},{192,208},{224... | collective-permute-start | bytes 49160 | tf_op jit(solution)/shard_map/ppermute | solution.py:513
  125.8 16.4 %copy-start.3 = (bf16[2,512,512]{2,1,0:T(8,128)(2,1)S(1)}, bf16[2,512,512]{2,1,0:T(8,128)(2,1)}, u32[]{:S(2)}) copy-start(bf16[2,512,512]{2,1,0:T(8,128)(2,1)} %copy-done.2) | copy-start | bytes 3145732
  139.2 3.1 %collective-permute-start.9 = (f32[8,512]{1,0:T(8,128)S(1)}, f32[8,512]{1,0:T(8,128)S(1)}, u32[]{:S(2)}, u32[]{:S(2)}) collective-permute-start(f32[8,512]{1,0:T(8,128)S(1)} %get-tuple-element.75.mine_ref.oo_ref), channel_id=1, source_target_pairs={{0,16},{32,48},{64,80},{96,112},{128,144},{160,176},{192,208},{224... | collective-permute-start | bytes 49160 | tf_op jit(solution)/shard_map/ppermute | solution.py:513
  142.2 4.9 %copy-start.1 = (bf16[2,512,512]{2,1,0:T(8,128)(2,1)S(1)}, bf16[2,512,512]{2,1,0:T(8,128)(2,1)}, u32[]{:S(2)}) copy-start(bf16[2,512,512]{2,1,0:T(8,128)(2,1)} %copy-done) | copy-start | bytes 3145732
  142.6 4.5 %collective-permute-start.10 = (f32[8,512]{1,0:T(8,128)S(1)}, f32[8,512]{1,0:T(8,128)S(1)}, u32[]{:S(2)}, u32[]{:S(2)}) collective-permute-start(f32[8,512]{1,0:T(8,128)S(1)} %joined.3.mine_ref), channel_id=1, source_target_pairs={{16,48},{48,16},{80,112},{112,80},{144,176},{176,144},{208,240},{2... | collective-permute-start | bytes 49160 | tf_op jit(solution)/shard_map/ppermute | solution.py:513
  147.5 6.4 %collective-permute-start.11 = (f32[8,512]{1,0:T(8,128)S(1)}, f32[8,512]{1,0:T(8,128)S(1)}, u32[]{:S(2)}, u32[]{:S(2)}) collective-permute-start(f32[8,512]{1,0:T(8,128)S(1)} %joined.4.mine_ref), channel_id=1, source_target_pairs={{16,80},{48,112},{80,16},{112,48},{144,208},{176,240},{208,144},{2... | collective-permute-start | bytes 49160 | tf_op jit(solution)/shard_map/ppermute | solution.py:513
  151.1 2.8 %copy-start.5 = (bf16[2,512,512]{2,1,0:T(8,128)(2,1)S(1)}, bf16[2,512,512]{2,1,0:T(8,128)(2,1)}, u32[]{:S(2)}) copy-start(bf16[2,512,512]{2,1,0:T(8,128)(2,1)} %copy-done.4) | copy-start | bytes 3145732
  154.3 5.1 %collective-permute-start.13 = (f32[8,512]{1,0:T(8,128)S(1)}, f32[8,512]{1,0:T(8,128)S(1)}, u32[]{:S(2)}, u32[]{:S(2)}) collective-permute-start(f32[8,512]{1,0:T(8,128)S(1)} %joined.5.off_ref), channel_id=1, source_target_pairs={{144,16},{176,48},{208,80},{240,112},{272,144},{304,176},{336,208}... | collective-permute-start | bytes 49160 | tf_op jit(solution)/shard_map/ppermute | solution.py:513
  160.3 4.5 %collective-permute-start.14 = (f32[8,512]{1,0:T(8,128)S(1)}, f32[8,512]{1,0:T(8,128)S(1)}, u32[]{:S(2)}, u32[]{:S(2)}) collective-permute-start(f32[8,512]{1,0:T(8,128)S(1)} %get-tuple-element.85), channel_id=1, source_target_pairs={{144,16},{176,48},{208,80},{240,112},{272,144},{304,176},{336,208}... | collective-permute-start | bytes 49160 | tf_op jit(solution)/shard_map/ppermute | solution.py:513
  165.7 4.5 %collective-permute-start.15 = (f32[8,512]{1,0:T(8,128)S(1)}, f32[8,512]{1,0:T(8,128)S(1)}, u32[]{:S(2)}, u32[]{:S(2)}) collective-permute-start(f32[8,512]{1,0:T(8,128)S(1)} %get-tuple-element.87), channel_id=1, source_target_pairs={{144,16},{176,48},{208,80},{240,112},{272,144},{304,176},{336,208}... | collective-permute-start | bytes 49160 | tf_op jit(solution)/shard_map/ppermute | solution.py:513
  170.2 3.8 %copy-start.14 = (f32[16,512]{1,0:T(8,128)S(1)}, f32[16,512]{1,0:T(8,128)}, u32[]{:S(2)}) copy-start(f32[16,512]{1,0:T(8,128)} %get-tuple-element.44.x_ref) | copy-start | bytes 98308
  171.9 2.1 %collective-permute-start.16 = (f32[8,512]{1,0:T(8,128)S(1)}, f32[8,512]{1,0:T(8,128)S(1)}, u32[]{:S(2)}, u32[]{:S(2)}) collective-permute-start(f32[8,512]{1,0:T(8,128)S(1)} %get-tuple-element.89), channel_id=1, source_target_pairs={{16,0},{48,32},{80,64},{112,96},{144,128},{176,160},{208,192},{240... | collective-permute-start | bytes 49160 | tf_op jit(solution)/shard_map/ppermute | solution.py:513

commit v4 on v3

--- a/solution.py
+++ b/solution.py
@@ -90,9 +90,9 @@
     return jnp.concatenate([hi, v - hi], axis=0).astype(BF16)
 
 
-def observed_part(p, s4):
+def observed_part(p, s2):
     rows = p.shape[0]
-    both = dot(stacked(p), s4, NT)
+    both = dot(stacked(p), s2, NT)
     return both[:rows] + both[rows:]
 
 
@@ -101,10 +101,10 @@
     return jnp.concatenate([hi, hi, lo, lo], axis=0)
 
 
-def correction(e4, kk):
-    hi = e4.astype(BF16).astype(F32)
-    odd = (lanes(1, 4 * OBS) // OBS) % 2 == 1
-    return dot(jnp.where(odd, e4 - hi, hi).astype(BF16), kk)
+def correction(e2, kk):
+    hi = e2.astype(BF16).astype(F32)
+    mixed = jnp.where(lanes(1, 2 * OBS) >= OBS, e2 - hi, hi)
+    return dot(jnp.concatenate([mixed, mixed], axis=1).astype(BF16), kk)
 
 
 def one_hot(obs_row):
@@ -168,13 +168,14 @@
         padded_ref[j, REACH : REACH + N, :] = jnp.where(row == lanes(N, LANES) + LANES * j, 1.0, 0.0)
 
 
-def keep_map(padded_ref, map_ref, parts_ref):
+def keep_map(padded_ref, map_ref, parts_ref=None):
     for r in range(0, N, 64):
         for j in range(PIECES):
             at, cols = slice(r, r + 64), slice(LANES * j, LANES * (j + 1))
             value = padded_ref[j, REACH + r : REACH + r + 64, :]
             map_ref[at, cols] = value
-            parts_ref[0, at, cols], parts_ref[1, at, cols] = split2(value)
+            if parts_ref is not None:
+                parts_ref[0, at, cols], parts_ref[1, at, cols] = split2(value)
 
 
 def diffused(padded_ref, j, first, size, centre):
@@ -187,7 +188,7 @@
 
     def kernel(
         offs_ref, cells_ref, up_far, c_far, obs_far, y_far, gains_far,
-        map_ref, parts_ref, off_ref, s_ref, held_ref, moved_ref, picked_ref, ups_ref, cs_ref,
+        map_ref, held_ref, moved_ref, picked_ref, ups_ref, cs_ref,
         up_ref, c_ref, obs_ref, y_ref, gains_ref, sem
     ):
         pairs = ((up_far, up_ref), (c_far, c_ref), (obs_far, obs_ref), (y_far, y_ref))
@@ -207,7 +208,6 @@
         def one(k, vec):
             step = Step(k, offs_ref, up_ref, c_ref)
             s = one_hot(obs_ref[pl.ds(k, 1), :])
-            s_ref[k] = s
             fetch(k).wait()
             gain = RELAXATION * s.astype(F32) + gains_ref[k]
             for r in range(0, N, CELLS):
@@ -235,20 +235,19 @@
 
             high, low = split2(gain)
             kk = jnp.concatenate([high, high, low, low], axis=0)
-            s4 = jnp.concatenate([s] * 4, axis=0)
-            y4 = jnp.concatenate([y_ref[pl.ds(k, 1), :]] * 4, axis=1)
+            s2 = jnp.concatenate([s] * 2, axis=0)
+            y2 = jnp.concatenate([y_ref[pl.ds(k, 1), :]] * 2, axis=1)
             p = step.apply(vec)
-            return p - correction(observed_part(p, s4) - jnp.where(head, y4, 0.0), kk)
+            return p - correction(observed_part(p, s2) - jnp.where(head, y2, 0.0), kk)
 
         vec = lax.fori_loop(0, steps, one, jnp.zeros((8, N), F32))
-        off_ref[...] = vec
         map_ref[N:ROWS, :] = vec
-        keep_map(held_ref, map_ref, parts_ref)
+        keep_map(held_ref, map_ref)
 
     return call(
         kernel,
         "filter_map",
-        (((ROWS, N), F32), PARTS, VECTOR, ((steps, OBS, N), BF16)),
+        (((ROWS, N), F32),),
         (offsets, obs_cells, upwind, courant, obs_cells, observed, gains),
         scratch=[
             pltpu.VMEM((PIECES, N + 2 * REACH, LANES), F32),
@@ -268,7 +267,7 @@
         flops=16 * 10**9,
         moved=4 << 20,
         limit=28,
-    )
+    )[0]
 
 
 def smoother_map(offsets, upwind, courant, smooth_gain):
@@ -328,13 +327,27 @@
     )
 
 
-def compose(flag, mine, other, keep=True, parts=False, other_parts=False):
+def compose(flag, mine, other, keep=True, parts=False, other_parts=False, far=False):
     rows = mine.shape[0]
     affine = rows > N
     kinds = (("out", keep, ((rows, N), F32)), ("off", affine, VECTOR), ("parts", parts, PARTS), ("other", other_parts, PARTS))
 
-    def kernel(flag_ref, mine_ref, other_ref, *out_refs):
-        refs = dict(zip([name for name, wanted, _ in kinds if wanted], out_refs, strict=True))
+    def kernel(flag_ref, mine_ref, other_ref, *more):
+        names = [name for name, wanted, _ in kinds if wanted]
+        refs = dict(zip(names, more[: len(names)], strict=True))
+        if far:
+            *held, sem = more[len(names) :]
+
+            @pl.when(flag_ref[0] != 2)
+            def _():
+                pairs = enumerate(zip((mine_ref, other_ref), held, strict=True))
+                copies = [pltpu.make_async_copy(a, b, sem.at[i]) for i, (a, b) in pairs]
+                for copy in copies:
+                    copy.start()
+                for copy in copies:
+                    copy.wait()
+
+            mine_ref, other_ref = held
 
         def product(first_ref, second_ref):
             if other_parts:
@@ -367,7 +380,17 @@
             product(mine_ref, other_ref)
 
     outs = tuple(shape for _, wanted, shape in kinds if wanted)
-    return call(kernel, "compose", outs, (flag, mine, other), flops=10**9, moved=5 << 20)
+    scratch = [pltpu.VMEM((rows, N), F32)] * 2 + [pltpu.SemaphoreType.DMA((2,))]
+    return call(
+        kernel,
+        "compose",
+        outs,
+        (flag, mine, other),
+        scratch=scratch if far else (),
+        far=2 if far else 0,
+        flops=10**9,
+        moved=5 << 20,
+    )
 
 
 def parted(maps):
@@ -428,6 +451,16 @@
         return sg_ref[at, :] * step.apply_transposed(diff + u_ref[at, :])
 
     return lax.fori_loop(0, steps, one, diff)
+
+
+def one_hots(obs_cells):
+    steps = obs_cells.shape[0]
+
+    def kernel(obs_ref, hots_ref):
+        for k in range(steps):
+            hots_ref[k] = one_hot(obs_ref[k : k + 1, :])
+
+    return call(kernel, "one_hots", (((steps, OBS, N), BF16),), (obs_cells,), scalars=0)[0]
 
 
 def forward(place, offsets, upwind, courant, smooth_gain, hots, gains, observed, state, got):
@@ -454,10 +487,10 @@
                 copy.wait()
             s = s_ref[k]
             kk = gain_rows(s, gains_ref[k])
-            s4 = jnp.concatenate([s] * 4, axis=0)
-            y4 = jnp.concatenate([y_ref[pl.ds(k, 1), :]] * 4, axis=1)
+            s2 = jnp.concatenate([s] * 2, axis=0)
+            y2 = jnp.concatenate([y_ref[pl.ds(k, 1), :]] * 2, axis=1)
             p = step.apply(vec)
-            update = -correction(observed_part(p, s4) - jnp.where(first, y4, 0.0), kk)
+            update = -correction(observed_part(p, s2) - jnp.where(first, y2, 0.0), kk)
             vec = p + update
             filt_ref[pl.ds(k, 1), :] = vec[0:1]
             upd_ref[pl.ds(k, 1), :] = update[0:1]
@@ -525,33 +558,36 @@
 
     after = lambda value, *before: lax.optimization_barrier((value, *before))[0]
 
-    fmap, fmap_p, fmap_o, hots = filter_map(offsets, upwind, courant, obs_cells, gains, observed)
+    fmap = filter_map(offsets, upwind, courant, obs_cells, gains, observed)
     fmap_odd = moved(fmap, lambda i: i - 1, odd)
     fpair, fpair_o = compose(on_even(0), fmap, fmap_odd)
     fpair_other = moved(fpair, lambda i: i ^ 2, even)
     smap, smap_p = smoother_map(offsets, after(upwind, fpair_o), courant, smooth_gain)
-    smap_even = moved(smap, lambda i: i + 1, even)
     fquad, fquad_o = compose(on_even(y % 2), fpair, fpair_other)
-    fquad_other = moved(fquad, lambda i: i ^ 4, even)
-    smap_even = after(smap_even, fquad_o)
-    spair, spair_p, smap_ep = compose(on_odd(0), smap, smap_even, parts=True, other_parts=True)
+    fquad_other = moved(fquad, lambda i: i ^ 6, even)
+    smap_even = moved(after(smap, fquad_o), lambda i: i + 1, even)
+    spair, spair_p, smap_ep = compose(
+        on_odd(0), smap, smap_even, parts=True, other_parts=True, far=True
+    )
     fpair_op, fpair_oo = parted(fpair_other)
-    foct_o, foct_p = compose(on_even(y // 2), fquad, fquad_other, keep=False, parts=True)
-    spair_other = moved(after(spair, foct_o), lambda i: i ^ 2, odd)
+    fmap_p, fmap_o = parted(fmap)
+    hots = one_hots(after(obs_cells, fquad_o))
+    foct_o, foct_p = compose(after(on_even(y // 2), hots), fquad, fquad_other, keep=False, parts=True)
 
     place3 = ints(x, y >= 2, y % 2 == 1)
     ahead_of = lambda v: moved(v, lambda i: i + 8, lambda i: even(i) and i < 24)
     state, sent = hop(place3, 0, start_row, start_row, foct_p, foct_o)
     got = ahead_of(sent)
+    spair_other = moved(after(spair, sent), lambda i: i ^ 2, odd)
     fquad_op, fquad_oo = parted(fquad_other)
     state, sent = hop(place3, 1, after(state, fquad_oo), got, foct_p, foct_o)
     got = ahead_of(sent)
     state, sent = hop(place3, 2, state, got, foct_p, foct_o)
     got = ahead_of(sent)
     squad, squad_p, spair_op = compose(
-        on_odd(1 - y % 2), spair, after(spair_other, sent), parts=True, other_parts=True
-    )
-    squad_other = moved(squad, lambda i: i ^ 4, odd)
+        on_odd(1 - y % 2), spair, after(spair_other, sent), parts=True, other_parts=True, far=True
+    )
+    squad_other = moved(squad, lambda i: i ^ 6, odd)
     state, sent = descend(
         place3, 3, after(state, squad_p), got, fquad_op, fquad_oo, fpair_op, fpair_oo, fmap_p, fmap_o
     )
@@ -560,13 +596,19 @@
         at_core, offsets, upwind, courant, smooth_gain, hots, gains, observed, state, got
     )
     soct_p, squad_op = compose(
-        on_odd(1 - y // 2), squad, after(squad_other, own), keep=False, parts=True, other_parts=True
+        on_odd(1 - y // 2),
+        squad,
+        after(squad_other, own),
+        keep=False,
+        parts=True,
+        other_parts=True,
+        far=True,
     )
 
     pair = joined(never, own, moved(own, lambda i: i + 1, even), smap_p, smap_ep)
     pair_other = moved(pair, lambda i: i ^ 2, odd)
     quad = joined(y_even, pair, pair_other, spair_p, spair_op)
-    quad_other = moved(quad, lambda i: i ^ 4, odd)
+    quad_other = moved(quad, lambda i: i ^ 6, odd)
     octet = joined(y_low, quad, quad_other, squad_p, squad_op)
     place3 = ints(x, y < 2, y % 2 == 0)
     behind = lambda v: moved(v, lambda i: i - 8, lambda i: odd(i) and i >= 8)

time: 178 us -> 164 us (0.921)
  waiting for transfers between devices: 53.3 us -> 35.5 us
  local copies, waits for them, and re-layouts: 3.79 us -> 5.77 us
    ppermute x17, waiting for transfers between devices: 53.3 us -> 35.5 us  [moved(): lax.ppermute(values, 'tm', [(i, to(i)) for i in range(32) if senders(i)])]
    unnamed x35, local copies, waits for them, and re-layouts: 3.78 us -> 5.76 us
    pallas_call x22 -> x24, Pallas kernels: 85.6 us -> 86 us  [call(): pl.pallas_call(kernel, out_shape=tuple((jax.ShapeDtypeStruct(*out) for ou...]
  transfers between devices with their start and end apart: 17 -> 17, of which waited for: 10 -> 10; matrix products, arithmetic and copies ran while one was open for 0% -> 0% of each run, Pallas kernels for 25% -> 26%
where the time goes in v4:
time: 164 us; the launch traced here: 163 us
  Pallas kernels  86 us (52%)
  waiting for transfers between devices  35.5 us (22%)
  starting transfers between devices  34.8 us (21%)
  local copies, waits for them, and re-layouts  5.77 us (4%)
    pallas_call x24, Pallas kernels, call(): pl.pallas_call(kernel, out_shape=tuple((jax.ShapeDtypeStruct(*out) for ou...  86 us
    ppermute x17, waiting for transfers between devices, moved(): lax.ppermute(values, 'tm', [(i, to(i)) for i in range(32) if senders(i)])  35.5 us
    ppermute x17, starting transfers between devices, moved(): lax.ppermute(values, 'tm', [(i, to(i)) for i in range(32) if senders(i)])  34.8 us
    unnamed x35, local copies, waits for them, and re-layouts  5.76 us
  transfers between devices with their start and end apart: 17, of which 10 were waited for; matrix products, arithmetic and copies ran while one was open for 0% of the time, Pallas kernels for 26%

profile of v4, /device:TPU:1, one launch (start us, length us, event | category | flops | bytes accessed | tf_op | source)
XLA Modules:
  0.0 163.2 jit_solution(6026345729840681800)
XLA Ops:
  1.4 25.5 %filter_map.1.mine_ref.map_ref = f32[520,512]{1,0:T(8,128)S(1)} custom-call(s32[16,4]{1,0:T(8,128)S(1)} %copy.12.offs_ref, s32[16,64]{1,0:T(8,128)} %obs_ref, s32[16,512]{1,0:T(8,128)} %up_ref.4, f32[16,512]{1,0:T(8,128)} %c_ref.5, s32[16,64]{1,0:T(8,128)} %obs_ref, f32[16,64]{1,0:T(8,128)} %y_ref.1, f32[16,64,512]{2,1,0:T(8,128)} %gains_far.3), custom_call_target="tpu_custom_call" | custom-call | flops 16000000000 | bytes 4194304 | tf_op jit(solution)/shard_map/filter_map/pallas_call | solution.py:130
  26.9 8.9 %collective-permute-start = (f32[520,512]{1,0:T(8,128)S(1)}, f32[520,512]{1,0:T(8,128)S(1)}, u32[]{:S(2)}, u32[]{:S(2)}) collective-permute-start(f32[520,512]{1,0:T(8,128)S(1)} %filter_map.1.mine_ref.map_ref), channel_id=1, source_target_pairs={{16,0},{48,32},{80,64},{112,96},{144,128},{176,160},{208,192},{240... | collective-permute-start | bytes 3194888 | tf_op jit(solution)/shard_map/ppermute | solution.py:546
  35.8 2.2 %collective-permute-done.other_ref = f32[520,512]{1,0:T(8,128)S(1)} collective-permute-done((f32[520,512]{1,0:T(8,128)S(1)}, f32[520,512]{1,0:T(8,128)S(1)}, u32[]{:S(2)}, u32[]{:S(2)}) %collective-permute-start) | collective-permute-done | bytes 1064992 | tf_op jit(solution)/shard_map/ppermute | solution.py:546
  38.0 1.0 compose.6
  39.0 1.7 %collective-permute-start.1 = (f32[520,512]{1,0:T(8,128)}, f32[520,512]{1,0:T(8,128)}, u32[]{:S(2)}, u32[]{:S(2)}) collective-permute-start(f32[520,512]{1,0:T(8,128)} %get-tuple-element.48.mine_ref), channel_id=1, source_target_pairs={{0,32},{32,0},{64,96},{96,64},{128,160},{160,128},{192,224},{224,1... | collective-permute-start | bytes 3194888 | tf_op jit(solution)/shard_map/ppermute | solution.py:546
  40.7 16.8 %smoother_map.1 = (f32[512,512]{1,0:T(8,128)S(1)}, bf16[2,512,512]{2,1,0:T(8,128)(2,1)S(1)}) custom-call(s32[16,4]{1,0:T(8,128)S(1)} %copy.12.offs_ref, s32[16,512]{1,0:T(8,128)S(1)} %copy-done.11, f32[16,512]{1,0:T(8,128)S(1)} %copy-done.12, f32[16,512]{1,0:T(8,128)S(1)} %copy-done.13), custom_call_target="tpu_custom_call" | custom-call | flops 8000000000 | bytes 2097152 | tf_op jit(solution)/shard_map/smoother_map/pallas_call | solution.py:130
  57.5 2.9 %compose.7 = (f32[520,512]{1,0:T(8,128)}, f32[8,512]{1,0:T(8,128)}) custom-call(s32[1]{0:T(128)} %bitcast.1.flag_ref, f32[520,512]{1,0:T(8,128)} %get-tuple-element.48.mine_ref, f32[520,512]{1,0:T(8,128)} %collective-permute-done.1.other_ref.map_ref), custom_call_target="tpu_custom_call" | custom-call | flops 1000000000 | bytes 5242880 | tf_op jit(solution)/shard_map/compose/pallas_call | solution.py:130
  60.4 1.3 collective-permute-start.5
  61.7 1.6 %collective-permute-start.2 = (f32[520,512]{1,0:T(8,128)}, f32[520,512]{1,0:T(8,128)}, u32[]{:S(2)}, u32[]{:S(2)}) collective-permute-start(f32[520,512]{1,0:T(8,128)} %get-tuple-element.52.mine_ref), channel_id=1, source_target_pairs={{0,96},{32,64},{64,32},{96,0},{128,224},{160,192},{192,160},{224,1... | collective-permute-start | bytes 3194888 | tf_op jit(solution)/shard_map/ppermute | solution.py:546
  63.8 1.0 copy-done.6
  64.7 2.5 %collective-permute-done.5.other_ref = f32[512,512]{1,0:T(8,128)} collective-permute-done((f32[512,512]{1,0:T(8,128)S(1)}, f32[512,512]{1,0:T(8,128)}, u32[]{:S(2)}, u32[]{:S(2)}) %collective-permute-start.5) | collective-permute-done | bytes 1048608 | tf_op jit(solution)/shard_map/ppermute | solution.py:546
  67.2 3.7 %compose.9 = (f32[512,512]{1,0:T(8,128)}, bf16[2,512,512]{2,1,0:T(8,128)(2,1)S(1)}, bf16[2,512,512]{2,1,0:T(8,128)(2,1)S(1)}) custom-call(s32[1]{0:T(128)} %bitcast.8.flag_ref, f32[512,512]{1,0:T(8,128)} %copy-done.10, f32[512,512]{1,0:T(8,128)} %collective-permute-done.5.other_ref), custom_call_target="tpu_custom_call" | custom-call | flops 1000000000 | bytes 5242880 | tf_op jit(solution)/shard_map/compose/pallas_call | solution.py:130
  70.9 1.0 copy-done
  71.9 1.0 copy-done.2
  72.9 1.6 compose.8
  74.5 0.9 hop.5
  75.4 3.6 %collective-permute-start.6 = (f32[512,512]{1,0:T(8,128)}, f32[512,512]{1,0:T(8,128)}, u32[]{:S(2)}, u32[]{:S(2)}) collective-permute-start(f32[512,512]{1,0:T(8,128)} %get-tuple-element.65.mine_ref), channel_id=1, source_target_pairs={{16,48},{48,16},{80,112},{112,80},{144,176},{176,144},{208,240},{2... | collective-permute-start | bytes 3145736 | tf_op jit(solution)/shard_map/ppermute | solution.py:546
  79.7 1.4 parted.3
  81.0 1.0 copy-done.7
  82.1 0.9 hop.6
  83.7 0.9 hop.7
  84.6 6.9 %collective-permute-done.6.other_ref = f32[512,512]{1,0:T(8,128)} collective-permute-done((f32[512,512]{1,0:T(8,128)}, f32[512,512]{1,0:T(8,128)}, u32[]{:S(2)}, u32[]{:S(2)}) %collective-permute-start.6) | collective-permute-done | bytes 1048608 | tf_op jit(solution)/shard_map/ppermute | solution.py:546
  91.5 3.7 %compose.10 = (f32[512,512]{1,0:T(8,128)}, bf16[2,512,512]{2,1,0:T(8,128)(2,1)S(1)}, bf16[2,512,512]{2,1,0:T(8,128)(2,1)S(1)}) custom-call(s32[1]{0:T(128)} %bitcast.7.flag_ref, f32[512,512]{1,0:T(8,128)} %get-tuple-element.65.mine_ref, f32[512,512]{1,0:T(8,128)} %collective-permute-done.6.other_ref), custom_call_target="tpu_custom_call" | custom-call | flops 1000000000 | bytes 5242880 | tf_op jit(solution)/shard_map/compose/pallas_call | solution.py:130
  95.2 1.0 copy-done.4
  96.1 2.0 %collective-permute-start.12 = (f32[512,512]{1,0:T(8,128)}, f32[512,512]{1,0:T(8,128)}, u32[]{:S(2)}, u32[]{:S(2)}) collective-permute-start(f32[512,512]{1,0:T(8,128)} %get-tuple-element.84.mine_ref), channel_id=1, source_target_pairs={{16,112},{48,80},{80,48},{112,16},{144,240},{176,208},{208,176},{2... | collective-permute-start | bytes 3145736 | tf_op jit(solution)/shard_map/ppermute | solution.py:546
  99.0 1.4 parted.4
  100.4 0.9 descend.2
  101.3 1.3 collective-permute-start.8
  102.6 9.6 %collective-permute-done.8.got_ref = f32[8,512]{1,0:T(8,128)S(1)} collective-permute-done((f32[8,512]{1,0:T(8,128)S(1)}, f32[8,512]{1,0:T(8,128)S(1)}, u32[]{:S(2)}, u32[]{:S(2)}) %collective-permute-start.8) | collective-permute-done | bytes 16416 | tf_op jit(solution)/shard_map/ppermute | solution.py:546
  112.3 12.8 %forward.1 = (f32[16,512]{1,0:T(8,128)}, f32[16,512]{1,0:T(8,128)S(1)}, f32[8,512]{1,0:T(8,128)S(1)}) custom-call(s32[1]{0:T(128)} %bitcast.place_ref, s32[16,4]{1,0:T(8,128)S(1)} %copy.12.offs_ref, bf16[16,64,512]{2,1,0:T(8,128)(2,1)} %copy-done.6, f32[16,64,512]{2,1,0:T(8,128)} %gains_far.3, s32[16,512]{1,0:T(8,128)S(1)} %copy-done.11, ...), custom_call_target="tpu_custom_call" | custom-call | flops 4000000000 | bytes 3145728 | tf_op jit(solution)/shard_map/forward/pallas_call | solution.py:130
  125.1 1.3 collective-permute-start.9
  126.4 1.8 %collective-permute-done.9.other_ref = f32[8,512]{1,0:T(8,128)S(1)} collective-permute-done((f32[8,512]{1,0:T(8,128)S(1)}, f32[8,512]{1,0:T(8,128)S(1)}, u32[]{:S(2)}, u32[]{:S(2)}) %collective-permute-start.9) | collective-permute-done | bytes 16416 | tf_op jit(solution)/shard_map/ppermute | solution.py:546
  128.5 2.8 %collective-permute-start.10 = (f32[8,512]{1,0:T(8,128)S(1)}, f32[8,512]{1,0:T(8,128)S(1)}, u32[]{:S(2)}, u32[]{:S(2)}) collective-permute-start(f32[8,512]{1,0:T(8,128)S(1)} %joined.3.mine_ref), channel_id=1, source_target_pairs={{16,48},{48,16},{80,112},{112,80},{144,176},{176,144},{208,240},{2... | collective-permute-start | bytes 49160 | tf_op jit(solution)/shard_map/ppermute | solution.py:546
  131.3 1.7 %collective-permute-done.10.other_ref.po_ref = f32[8,512]{1,0:T(8,128)S(1)} collective-permute-done((f32[8,512]{1,0:T(8,128)S(1)}, f32[8,512]{1,0:T(8,128)S(1)}, u32[]{:S(2)}, u32[]{:S(2)}) %collective-permute-start.10) | collective-permute-done | bytes 16416 | tf_op jit(solution)/shard_map/ppermute | solution.py:546
  133.4 3.1 %collective-permute-start.11 = (f32[8,512]{1,0:T(8,128)S(1)}, f32[8,512]{1,0:T(8,128)S(1)}, u32[]{:S(2)}, u32[]{:S(2)}) collective-permute-start(f32[8,512]{1,0:T(8,128)S(1)} %joined.4.mine_ref), channel_id=1, source_target_pairs={{16,112},{48,80},{80,48},{112,16},{144,240},{176,208},{208,176},{2... | collective-permute-start | bytes 49160 | tf_op jit(solution)/shard_map/ppermute | solution.py:546
  136.5 2.8 %compose.11 = (bf16[2,512,512]{2,1,0:T(8,128)(2,1)S(1)}, bf16[2,512,512]{2,1,0:T(8,128)(2,1)S(1)}) custom-call(s32[1]{0:T(128)} %bitcast.11.flag_ref, f32[512,512]{1,0:T(8,128)} %get-tuple-element.84.mine_ref, f32[512,512]{1,0:T(8,128)} %collective-permute-done.12.other_ref), custom_call_target="tpu_custom_call" | custom-call | flops 1000000000 | bytes 5242880 | tf_op jit(solution)/shard_map/compose/pallas_call | solution.py:130
  139.7 1.3 collective-permute-start.13
  141.1 3.6 %collective-permute-done.13.got_ref = f32[8,512]{1,0:T(8,128)S(1)} collective-permute-done((f32[8,512]{1,0:T(8,128)S(1)}, f32[8,512]{1,0:T(8,128)S(1)}, u32[]{:S(2)}, u32[]{:S(2)}) %collective-permute-start.13) | collective-permute-done | bytes 16416 | tf_op jit(solution)/shard_map/ppermute | solution.py:546
  144.7 0.9 hop.8
  145.6 1.3 collective-permute-start.14
  146.9 3.2 %collective-permute-done.14.got_ref = f32[8,512]{1,0:T(8,128)S(1)} collective-permute-done((f32[8,512]{1,0:T(8,128)S(1)}, f32[8,512]{1,0:T(8,128)S(1)}, u32[]{:S(2)}, u32[]{:S(2)}) %collective-permute-start.14) | collective-permute-done | bytes 16416 | tf_op jit(solution)/shard_map/ppermute | solution.py:546
  150.1 0.9 hop.9
  151.0 1.3 collective-permute-start.15
  152.3 3.2 %collective-permute-done.15.got_ref = f32[8,512]{1,0:T(8,128)S(1)} collective-permute-done((f32[8,512]{1,0:T(8,128)S(1)}, f32[8,512]{1,0:T(8,128)S(1)}, u32[]{:S(2)}, u32[]{:S(2)}) %collective-permute-start.15) | collective-permute-done | bytes 16416 | tf_op jit(solution)/shard_map/ppermute | solution.py:546
  155.5 1.7 %descend.3 = (f32[8,512]{1,0:T(8,128)S(1)}, f32[8,512]{1,0:T(8,128)S(1)}) custom-call(s32[3]{0:T(128)S(1)} %pad_add_fusion.1.place_ref, f32[8,512]{1,0:T(8,128)S(1)} %get-tuple-element.90.state_ref, f32[8,512]{1,0:T(8,128)S(1)} %collective-permute-done.15.got_ref, bf16[2,512,512]{2,1,0:T(8,128)(2,1)S(1)} %get-tuple-element.86.op_ref.quad_ref, ...), custom_call_target="tpu_custom_call" | custom-call | flops 100000000 | bytes 1048576 | tf_op jit(solution)/shard_map/descend/pallas_call | solution.py:130
  157.2 1.3 collective-permute-start.16
  158.5 0.8 collective-permute-done.16.got_ref
  159.3 3.9 %smooth.1 = f32[16,512]{1,0:T(8,128)} custom-call(s32[1]{0:T(128)} %bitcast.place_ref, s32[16,4]{1,0:T(8,128)S(1)} %copy.12.offs_ref, s32[16,512]{1,0:T(8,128)S(1)} %copy-done.11, f32[16,512]{1,0:T(8,128)S(1)} %copy-done.12, f32[16,512]{1,0:T(8,128)S(1)} %copy-done.13, f32[16,512]{1,0:T(8,128)S(1)} %get-tuple-element.78.u_ref, f32[16,512]{1,0:T(8,128)S(1)} %copy-done.15, ...), custom_call_target="tpu_custom_call" | custom-call | flops 100000000 | bytes 1048576 | tf_op jit(solution)/shard_map/smooth/pallas_call | solution.py:130
  (49 shorter events, 4.6 us)
Async XLA Ops:
  26.9 11.1 %collective-permute-start = (f32[520,512]{1,0:T(8,128)S(1)}, f32[520,512]{1,0:T(8,128)S(1)}, u32[]{:S(2)}, u32[]{:S(2)}) collective-permute-start(f32[520,512]{1,0:T(8,128)S(1)} %filter_map.1.mine_ref.map_ref), channel_id=1, source_target_pairs={{16,0},{48,32},{80,64},{112,96},{144,128},{176,160},{208,192},{240... | collective-permute-start | bytes 3194888 | tf_op jit(solution)/shard_map/ppermute | solution.py:546
  38.0 2.6 %copy-start.11 = (s32[16,512]{1,0:T(8,128)S(1)}, s32[16,512]{1,0:T(8,128)}, u32[]{:S(2)}) copy-start(s32[16,512]{1,0:T(8,128)} %up_ref.4) | copy-start | bytes 98308
  38.0 2.6 %copy-start.12 = (f32[16,512]{1,0:T(8,128)S(1)}, f32[16,512]{1,0:T(8,128)}, u32[]{:S(2)}) copy-start(f32[16,512]{1,0:T(8,128)} %c_ref.5) | copy-start | bytes 98308
  38.0 2.6 %copy-start.13 = (f32[16,512]{1,0:T(8,128)S(1)}, f32[16,512]{1,0:T(8,128)}, u32[]{:S(2)}) copy-start(f32[16,512]{1,0:T(8,128)} %sg_ref.5) | copy-start | bytes 98308
  39.0 18.5 %collective-permute-start.1 = (f32[520,512]{1,0:T(8,128)}, f32[520,512]{1,0:T(8,128)}, u32[]{:S(2)}, u32[]{:S(2)}) collective-permute-start(f32[520,512]{1,0:T(8,128)} %get-tuple-element.48.mine_ref), channel_id=1, source_target_pairs={{0,32},{32,0},{64,96},{96,64},{128,160},{160,128},{192,224},{224,1... | collective-permute-start | bytes 3194888 | tf_op jit(solution)/shard_map/ppermute | solution.py:546
  57.5 3.0 %copy-start.10 = (f32[512,512]{1,0:T(8,128)}, f32[512,512]{1,0:T(8,128)S(1)}, u32[]{:S(2)}) copy-start(f32[512,512]{1,0:T(8,128)S(1)} %get-tuple-element.63.mine_ref) | copy-start | bytes 3145732
  57.5 5.9 %copy-start.9 = (s32[16,64]{1,0:T(8,128)S(1)}, s32[16,64]{1,0:T(8,128)}, u32[]{:S(2)}) copy-start(s32[16,64]{1,0:T(8,128)} %obs_ref) | copy-start | bytes 12292
  60.4 6.8 %collective-permute-start.5 = (f32[512,512]{1,0:T(8,128)S(1)}, f32[512,512]{1,0:T(8,128)}, u32[]{:S(2)}, u32[]{:S(2)}) collective-permute-start(f32[512,512]{1,0:T(8,128)S(1)} %get-tuple-element.63.mine_ref), channel_id=1, source_target_pairs={{0,16},{32,48},{64,80},{96,112},{128,144},{160,176},{192,208},{224... | collective-permute-start | bytes 3145736 | tf_op jit(solution)/shard_map/ppermute | solution.py:546
  61.7 11.2 %collective-permute-start.2 = (f32[520,512]{1,0:T(8,128)}, f32[520,512]{1,0:T(8,128)}, u32[]{:S(2)}, u32[]{:S(2)}) collective-permute-start(f32[520,512]{1,0:T(8,128)} %get-tuple-element.52.mine_ref), channel_id=1, source_target_pairs={{0,96},{32,64},{64,32},{96,0},{128,224},{160,192},{192,160},{224,1... | collective-permute-start | bytes 3194888 | tf_op jit(solution)/shard_map/ppermute | solution.py:546
  63.8 1.0 copy-start.6
  70.9 1.0 copy-start
  71.9 1.0 copy-start.2
  72.9 1.6 copy-start.16
  75.4 16.1 %collective-permute-start.6 = (f32[512,512]{1,0:T(8,128)}, f32[512,512]{1,0:T(8,128)}, u32[]{:S(2)}, u32[]{:S(2)}) collective-permute-start(f32[512,512]{1,0:T(8,128)} %get-tuple-element.65.mine_ref), channel_id=1, source_target_pairs={{16,48},{48,16},{80,112},{112,80},{144,176},{176,144},{208,240},{2... | collective-permute-start | bytes 3145736 | tf_op jit(solution)/shard_map/ppermute | solution.py:546
  79.0 3.1 %collective-permute-start.3 = (f32[8,512]{1,0:T(8,128)S(1)}, f32[8,512]{1,0:T(8,128)S(1)}, u32[]{:S(2)}, u32[]{:S(2)}) collective-permute-start(f32[8,512]{1,0:T(8,128)S(1)} %get-tuple-element.58), channel_id=1, source_target_pairs={{0,128},{32,160},{64,192},{96,224},{128,256},{160,288},{192,320},{... | collective-permute-start | bytes 49160 | tf_op jit(solution)/shard_map/ppermute | solution.py:546
  81.0 1.0 copy-start.7
  83.0 0.7 collective-permute-start.4
  95.2 1.0 copy-start.4
  96.1 4.2 %copy-start.8 = (bf16[2,512,512]{2,1,0:T(8,128)(2,1)S(1)}, bf16[2,512,512]{2,1,0:T(8,128)(2,1)}, u32[]{:S(2)}) copy-start(bf16[2,512,512]{2,1,0:T(8,128)(2,1)} %copy-done.7) | copy-start | bytes 3145732
  96.1 40.4 %collective-permute-start.12 = (f32[512,512]{1,0:T(8,128)}, f32[512,512]{1,0:T(8,128)}, u32[]{:S(2)}, u32[]{:S(2)}) collective-permute-start(f32[512,512]{1,0:T(8,128)} %get-tuple-element.84.mine_ref), channel_id=1, source_target_pairs={{16,112},{48,80},{80,48},{112,16},{144,240},{176,208},{208,176},{2... | collective-permute-start | bytes 3145736 | tf_op jit(solution)/shard_map/ppermute | solution.py:546
  98.2 2.2 %collective-permute-start.7 = (f32[8,512]{1,0:T(8,128)S(1)}, f32[8,512]{1,0:T(8,128)S(1)}, u32[]{:S(2)}, u32[]{:S(2)}) collective-permute-start(f32[8,512]{1,0:T(8,128)S(1)} %get-tuple-element.66), channel_id=1, source_target_pairs={{0,128},{32,160},{64,192},{96,224},{128,256},{160,288},{192,320},{... | collective-permute-start | bytes 49160 | tf_op jit(solution)/shard_map/ppermute | solution.py:546
  100.4 11.9 %copy-start.14 = (f32[16,64]{1,0:T(8,128)S(1)}, f32[16,64]{1,0:T(8,128)}, u32[]{:S(2)}) copy-start(f32[16,64]{1,0:T(8,128)} %y_ref.1) | copy-start | bytes 12292
  101.3 10.9 %collective-permute-start.8 = (f32[8,512]{1,0:T(8,128)S(1)}, f32[8,512]{1,0:T(8,128)S(1)}, u32[]{:S(2)}, u32[]{:S(2)}) collective-permute-start(f32[8,512]{1,0:T(8,128)S(1)} %get-tuple-element.76), channel_id=1, source_target_pairs={{0,16},{32,48},{64,80},{96,112},{128,144},{160,176},{192,208},{224... | collective-permute-start | bytes 49160 | tf_op jit(solution)/shard_map/ppermute | solution.py:546
  112.3 15.9 %copy-start.3 = (bf16[2,512,512]{2,1,0:T(8,128)(2,1)S(1)}, bf16[2,512,512]{2,1,0:T(8,128)(2,1)}, u32[]{:S(2)}) copy-start(bf16[2,512,512]{2,1,0:T(8,128)(2,1)} %copy-done.2) | copy-start | bytes 3145732
  125.1 3.1 %collective-permute-start.9 = (f32[8,512]{1,0:T(8,128)S(1)}, f32[8,512]{1,0:T(8,128)S(1)}, u32[]{:S(2)}, u32[]{:S(2)}) collective-permute-start(f32[8,512]{1,0:T(8,128)S(1)} %get-tuple-element.79.mine_ref.oo_ref), channel_id=1, source_target_pairs={{0,16},{32,48},{64,80},{96,112},{128,144},{160,176},{192,208},{224... | collective-permute-start | bytes 49160 | tf_op jit(solution)/shard_map/ppermute | solution.py:546
  128.2 4.9 %copy-start.1 = (bf16[2,512,512]{2,1,0:T(8,128)(2,1)S(1)}, bf16[2,512,512]{2,1,0:T(8,128)(2,1)}, u32[]{:S(2)}) copy-start(bf16[2,512,512]{2,1,0:T(8,128)(2,1)} %copy-done) | copy-start | bytes 3145732
  128.5 4.5 %collective-permute-start.10 = (f32[8,512]{1,0:T(8,128)S(1)}, f32[8,512]{1,0:T(8,128)S(1)}, u32[]{:S(2)}, u32[]{:S(2)}) collective-permute-start(f32[8,512]{1,0:T(8,128)S(1)} %joined.3.mine_ref), channel_id=1, source_target_pairs={{16,48},{48,16},{80,112},{112,80},{144,176},{176,144},{208,240},{2... | collective-permute-start | bytes 49160 | tf_op jit(solution)/shard_map/ppermute | solution.py:546
  133.4 5.9 %collective-permute-start.11 = (f32[8,512]{1,0:T(8,128)S(1)}, f32[8,512]{1,0:T(8,128)S(1)}, u32[]{:S(2)}, u32[]{:S(2)}) collective-permute-start(f32[8,512]{1,0:T(8,128)S(1)} %joined.4.mine_ref), channel_id=1, source_target_pairs={{16,112},{48,80},{80,48},{112,16},{144,240},{176,208},{208,176},{2... | collective-permute-start | bytes 49160 | tf_op jit(solution)/shard_map/ppermute | solution.py:546
  136.5 2.8 %copy-start.5 = (bf16[2,512,512]{2,1,0:T(8,128)(2,1)S(1)}, bf16[2,512,512]{2,1,0:T(8,128)(2,1)}, u32[]{:S(2)}) copy-start(bf16[2,512,512]{2,1,0:T(8,128)(2,1)} %copy-done.4) | copy-start | bytes 3145732
  139.7 5.0 %collective-permute-start.13 = (f32[8,512]{1,0:T(8,128)S(1)}, f32[8,512]{1,0:T(8,128)S(1)}, u32[]{:S(2)}, u32[]{:S(2)}) collective-permute-start(f32[8,512]{1,0:T(8,128)S(1)} %joined.5.off_ref), channel_id=1, source_target_pairs={{144,16},{176,48},{208,80},{240,112},{272,144},{304,176},{336,208}... | collective-permute-start | bytes 49160 | tf_op jit(solution)/shard_map/ppermute | solution.py:546
  145.6 4.5 %collective-permute-start.14 = (f32[8,512]{1,0:T(8,128)S(1)}, f32[8,512]{1,0:T(8,128)S(1)}, u32[]{:S(2)}, u32[]{:S(2)}) collective-permute-start(f32[8,512]{1,0:T(8,128)S(1)} %get-tuple-element.89), channel_id=1, source_target_pairs={{144,16},{176,48},{208,80},{240,112},{272,144},{304,176},{336,208}... | collective-permute-start | bytes 49160 | tf_op jit(solution)/shard_map/ppermute | solution.py:546
  151.0 4.5 %collective-permute-start.15 = (f32[8,512]{1,0:T(8,128)S(1)}, f32[8,512]{1,0:T(8,128)S(1)}, u32[]{:S(2)}, u32[]{:S(2)}) collective-permute-start(f32[8,512]{1,0:T(8,128)S(1)} %get-tuple-element.91), channel_id=1, source_target_pairs={{144,16},{176,48},{208,80},{240,112},{272,144},{304,176},{336,208}... | collective-permute-start | bytes 49160 | tf_op jit(solution)/shard_map/ppermute | solution.py:546
  155.5 3.8 %copy-start.15 = (f32[16,512]{1,0:T(8,128)S(1)}, f32[16,512]{1,0:T(8,128)}, u32[]{:S(2)}) copy-start(f32[16,512]{1,0:T(8,128)} %get-tuple-element.46.x_ref) | copy-start | bytes 98308
  157.2 2.1 %collective-permute-start.16 = (f32[8,512]{1,0:T(8,128)S(1)}, f32[8,512]{1,0:T(8,128)S(1)}, u32[]{:S(2)}, u32[]{:S(2)}) collective-permute-start(f32[8,512]{1,0:T(8,128)S(1)} %get-tuple-element.93), channel_id=1, source_target_pairs={{16,0},{48,32},{80,64},{112,96},{144,128},{176,160},{208,192},{240... | collective-permute-start | bytes 49160 | tf_op jit(solution)/shard_map/ppermute | solution.py:546

commit v5 on v4

--- a/solution.py
+++ b/solution.py
@@ -4,6 +4,7 @@
 from jax.experimental import pallas as pl
 from jax.experimental.pallas import tpu as pltpu
 from jax.sharding import PartitionSpec as P
+
 
 N = 512
 OBS = 64
@@ -120,7 +121,7 @@
     return high[:rows] + (high[rows:] + low[:rows] + low[rows:])
 
 
-def call(kernel, name, outs, operands, scratch=(), scalars=1, far=0, flops=10**8, moved=1 << 20, limit=16):
+def call(kernel, outs, operands, scratch=(), scalars=1, far=0, flops=10**8, moved=1 << 20, limit=16):
     vmem, smem = pl.BlockSpec(memory_space=pltpu.VMEM), pl.BlockSpec(memory_space=pltpu.SMEM)
     anywhere = pl.BlockSpec(memory_space=pltpu.MemorySpace.HBM)
     near_hbm = [
@@ -135,7 +136,6 @@
         scratch_shapes=list(scratch),
         cost_estimate=pl.CostEstimate(flops=flops, bytes_accessed=moved, transcendentals=0),
         compiler_params=pltpu.CompilerParams(vmem_limit_bytes=limit << 20),
-        name=name,
     )(*operands[:scalars], *near_hbm, *operands[scalars + far :])
 
 
@@ -246,7 +246,6 @@
 
     return call(
         kernel,
-        "filter_map",
         (((ROWS, N), F32),),
         (offsets, obs_cells, upwind, courant, obs_cells, observed, gains),
         scratch=[
@@ -311,7 +310,6 @@
 
     return call(
         kernel,
-        "smoother_map",
         (((N, N), F32), PARTS),
         (offsets, upwind, courant, smooth_gain),
         scratch=[
@@ -383,7 +381,6 @@
     scratch = [pltpu.VMEM((rows, N), F32)] * 2 + [pltpu.SemaphoreType.DMA((2,))]
     return call(
         kernel,
-        "compose",
         outs,
         (flag, mine, other),
         scratch=scratch if far else (),
@@ -398,7 +395,7 @@
         keep_parts(map_ref, parts_ref)
         off_ref[...] = map_ref[N:ROWS, :]
 
-    return call(kernel, "parted", (PARTS, VECTOR), (maps,), scalars=0, flops=10**8, moved=2 << 20)
+    return call(kernel, (PARTS, VECTOR), (maps,), scalars=0, flops=10**8, moved=2 << 20)
 
 
 def hop(place, mark, state, got, parts, offset):
@@ -407,7 +404,7 @@
         new_ref[...] = new
         sent_ref[...] = through(new, parts_ref) + off_ref[...]
 
-    return call(kernel, "hop", (VECTOR, VECTOR), (place, state, got, parts, offset))
+    return call(kernel, (VECTOR, VECTOR), (place, state, got, parts, offset))
 
 
 def descend(place, mark, state, got, quad, quad_off, pair, pair_off, own, own_off):
@@ -425,7 +422,7 @@
         sent_ref[...] = through(new_ref[...], own_ref) + oo_ref[...]
 
     operands = (place, state, got, quad, quad_off, pair, pair_off, own, own_off)
-    return call(kernel, "descend", (VECTOR, VECTOR), operands)
+    return call(kernel, (VECTOR, VECTOR), operands)
 
 
 def joined(flag, mine, other, my_parts, other_parts):
@@ -438,7 +435,7 @@
         def _():
             out_ref[...] = through(mine_ref[...], op_ref) + other_ref[...]
 
-    return call(kernel, "joined", (VECTOR,), (flag, mine, other, my_parts, other_parts))[0]
+    return call(kernel, (VECTOR,), (flag, mine, other, my_parts, other_parts))[0]
 
 
 def smoothing(steps, diff, offs_ref, up_ref, c_ref, sg_ref, u_ref, store=None):
@@ -460,7 +457,7 @@
         for k in range(steps):
             hots_ref[k] = one_hot(obs_ref[k : k + 1, :])
 
-    return call(kernel, "one_hots", (((steps, OBS, N), BF16),), (obs_cells,), scalars=0)[0]
+    return call(kernel, (((steps, OBS, N), BF16),), (obs_cells,), scalars=0)[0]
 
 
 def forward(place, offsets, upwind, courant, smooth_gain, hots, gains, observed, state, got):
@@ -503,7 +500,6 @@
 
     return call(
         kernel,
-        "forward",
         (((steps, N), F32), ((steps, N), F32), VECTOR),
         (place, offsets, hots, gains, upwind, courant, smooth_gain, observed, state, got),
         scratch=[
@@ -531,7 +527,6 @@
 
     return call(
         kernel,
-        "smooth",
         (((steps, N), F32),),
         (place, offsets, upwind, courant, smooth_gain, updates, filtered, top, got),
         scalars=2,
@@ -582,7 +577,7 @@
     fquad_op, fquad_oo = parted(fquad_other)
     state, sent = hop(place3, 1, after(state, fquad_oo), got, foct_p, foct_o)
     got = ahead_of(sent)
-    state, sent = hop(place3, 2, state, got, foct_p, foct_o)
+    state, sent = hop(place3, 2, after(state, fpair_oo, fmap_o), got, foct_p, foct_o)
     got = ahead_of(sent)
     squad, squad_p, spair_op = compose(
         on_odd(1 - y % 2), spair, after(spair_other, sent), parts=True, other_parts=True, far=True

time: 164 us -> 164 us (level)
  waiting for transfers between devices: 35.5 us -> 37.2 us
    ppermute x17, waiting for transfers between devices: 35.5 us -> 37.2 us  [moved(): lax.ppermute(values, 'tm', [(i, to(i)) for i in range(32) if senders(i)])]
    unnamed x35 -> x31, local copies, waits for them, and re-layouts: 5.76 us -> 4.72 us
where the time goes in v5:
time: 164 us; the launch traced here: 163 us
  Pallas kernels  86.3 us (53%)
  waiting for transfers between devices  37.2 us (23%)
  starting transfers between devices  33.7 us (21%)
  local copies, waits for them, and re-layouts  4.72 us (3%)
    pallas_call x24, Pallas kernels, call(): pl.pallas_call(kernel, out_shape=tuple((jax.ShapeDtypeStruct(*out) for ou...  86.3 us
    ppermute x17, waiting for transfers between devices, moved(): lax.ppermute(values, 'tm', [(i, to(i)) for i in range(32) if senders(i)])  37.2 us
    ppermute x17, starting transfers between devices, moved(): lax.ppermute(values, 'tm', [(i, to(i)) for i in range(32) if senders(i)])  33.7 us
    unnamed x31, local copies, waits for them, and re-layouts  4.72 us
  transfers between devices with their start and end apart: 17, of which 10 were waited for; matrix products, arithmetic and copies ran while one was open for 0% of the time, Pallas kernels for 26%

profile of v5, /device:TPU:1, one launch (start us, length us, event | category | flops | bytes accessed | tf_op | source)
XLA Modules:
  0.0 163.0 jit_solution(7398869611592273652)
XLA Ops:
  0.6 0.8 copy.12.offs_ref
  1.4 25.7 %shard_map.95.mine_ref.map_ref = f32[520,512]{1,0:T(8,128)S(1)} custom-call(s32[16,4]{1,0:T(8,128)S(1)} %copy.12.offs_ref, s32[16,64]{1,0:T(8,128)} %obs_ref, s32[16,512]{1,0:T(8,128)} %up_ref.4, f32[16,512]{1,0:T(8,128)} %c_ref.5, s32[16,64]{1,0:T(8,128)} %obs_ref, f32[16,64]{1,0:T(8,128)} %y_ref.1, f32[16,64,512]{2,1,0:T(8,128)} %gains_far.3), custom_call_target="tpu_custom_call" | custom-call | flops 16000000000 | bytes 4194304 | tf_op jit(solution)/shard_map/pallas_call | solution.py:131
  27.1 8.8 %collective-permute-start = (f32[520,512]{1,0:T(8,128)S(1)}, f32[520,512]{1,0:T(8,128)S(1)}, u32[]{:S(2)}, u32[]{:S(2)}) collective-permute-start(f32[520,512]{1,0:T(8,128)S(1)} %shard_map.95.mine_ref.map_ref), channel_id=1, source_target_pairs={{16,0},{48,32},{80,64},{112,96},{144,128},{176,160},{208,192},{240... | collective-permute-start | bytes 3194888 | tf_op jit(solution)/shard_map/ppermute | solution.py:541
  35.9 2.2 %collective-permute-done.other_ref = f32[520,512]{1,0:T(8,128)S(1)} collective-permute-done((f32[520,512]{1,0:T(8,128)S(1)}, f32[520,512]{1,0:T(8,128)S(1)}, u32[]{:S(2)}, u32[]{:S(2)}) %collective-permute-start) | collective-permute-done | bytes 1064992 | tf_op jit(solution)/shard_map/ppermute | solution.py:541
  38.1 1.0 shard_map.96
  39.1 1.7 %collective-permute-start.1 = (f32[520,512]{1,0:T(8,128)}, f32[520,512]{1,0:T(8,128)}, u32[]{:S(2)}, u32[]{:S(2)}) collective-permute-start(f32[520,512]{1,0:T(8,128)} %get-tuple-element.49.mine_ref), channel_id=1, source_target_pairs={{0,32},{32,0},{64,96},{96,64},{128,160},{160,128},{192,224},{224,1... | collective-permute-start | bytes 3194888 | tf_op jit(solution)/shard_map/ppermute | solution.py:541
  40.8 16.9 %shard_map.106 = (f32[512,512]{1,0:T(8,128)S(1)}, bf16[2,512,512]{2,1,0:T(8,128)(2,1)S(1)}) custom-call(s32[16,4]{1,0:T(8,128)S(1)} %copy.12.offs_ref, s32[16,512]{1,0:T(8,128)S(1)} %copy-done.9, f32[16,512]{1,0:T(8,128)S(1)} %copy-done.10, f32[16,512]{1,0:T(8,128)S(1)} %copy-done.11), custom_call_target="tpu_custom_call" | custom-call | flops 8000000000 | bytes 2097152 | tf_op jit(solution)/shard_map/pallas_call | solution.py:131
  57.7 2.9 %shard_map.97 = (f32[520,512]{1,0:T(8,128)}, f32[8,512]{1,0:T(8,128)}) custom-call(s32[1]{0:T(128)} %bitcast.1.flag_ref, f32[520,512]{1,0:T(8,128)} %get-tuple-element.49.mine_ref, f32[520,512]{1,0:T(8,128)} %collective-permute-done.1.other_ref.map_ref), custom_call_target="tpu_custom_call" | custom-call | flops 1000000000 | bytes 5242880 | tf_op jit(solution)/shard_map/pallas_call | solution.py:131
  60.7 1.3 collective-permute-start.5
  61.9 1.6 %collective-permute-start.2 = (f32[520,512]{1,0:T(8,128)}, f32[520,512]{1,0:T(8,128)}, u32[]{:S(2)}, u32[]{:S(2)}) collective-permute-start(f32[520,512]{1,0:T(8,128)} %get-tuple-element.53.mine_ref), channel_id=1, source_target_pairs={{0,96},{32,64},{64,32},{96,0},{128,224},{160,192},{192,160},{224,1... | collective-permute-start | bytes 3194888 | tf_op jit(solution)/shard_map/ppermute | solution.py:541
  64.0 1.0 copy-done.6
  65.0 2.4 %collective-permute-done.5.other_ref = f32[512,512]{1,0:T(8,128)} collective-permute-done((f32[512,512]{1,0:T(8,128)S(1)}, f32[512,512]{1,0:T(8,128)}, u32[]{:S(2)}, u32[]{:S(2)}) %collective-permute-start.5) | collective-permute-done | bytes 1048608 | tf_op jit(solution)/shard_map/ppermute | solution.py:541
  67.4 3.7 %shard_map.107 = (f32[512,512]{1,0:T(8,128)}, bf16[2,512,512]{2,1,0:T(8,128)(2,1)S(1)}, bf16[2,512,512]{2,1,0:T(8,128)(2,1)S(1)}) custom-call(s32[1]{0:T(128)} %bitcast.8.flag_ref, f32[512,512]{1,0:T(8,128)} %copy-done.8, f32[512,512]{1,0:T(8,128)} %collective-permute-done.5.other_ref), custom_call_target="tpu_custom_call" | custom-call | flops 1000000000 | bytes 5242880 | tf_op jit(solution)/shard_map/pallas_call | solution.py:131
  71.1 1.0 copy-done
  72.1 1.0 copy-done.2
  73.1 1.6 shard_map.99
  74.7 0.9 shard_map.100
  75.6 3.3 %collective-permute-start.6 = (f32[512,512]{1,0:T(8,128)}, f32[512,512]{1,0:T(8,128)}, u32[]{:S(2)}, u32[]{:S(2)}) collective-permute-start(f32[512,512]{1,0:T(8,128)} %get-tuple-element.69.mine_ref), channel_id=1, source_target_pairs={{16,48},{48,16},{80,112},{112,80},{144,176},{176,144},{208,240},{2... | collective-permute-start | bytes 3145736 | tf_op jit(solution)/shard_map/ppermute | solution.py:541
  79.5 1.4 shard_map.101
  80.9 0.9 shard_map.102
  82.6 1.4 shard_map.103
  84.0 0.9 shard_map.105
  84.9 6.5 %collective-permute-done.6.other_ref = f32[512,512]{1,0:T(8,128)} collective-permute-done((f32[512,512]{1,0:T(8,128)}, f32[512,512]{1,0:T(8,128)}, u32[]{:S(2)}, u32[]{:S(2)}) %collective-permute-start.6) | collective-permute-done | bytes 1048608 | tf_op jit(solution)/shard_map/ppermute | solution.py:541
  91.4 3.7 %shard_map.108 = (f32[512,512]{1,0:T(8,128)}, bf16[2,512,512]{2,1,0:T(8,128)(2,1)S(1)}, bf16[2,512,512]{2,1,0:T(8,128)(2,1)S(1)}) custom-call(s32[1]{0:T(128)} %bitcast.7.flag_ref, f32[512,512]{1,0:T(8,128)} %get-tuple-element.69.mine_ref, f32[512,512]{1,0:T(8,128)} %collective-permute-done.6.other_ref), custom_call_target="tpu_custom_call" | custom-call | flops 1000000000 | bytes 5242880 | tf_op jit(solution)/shard_map/pallas_call | solution.py:131
  95.1 1.0 copy-done.4
  96.1 1.9 %collective-permute-start.12 = (f32[512,512]{1,0:T(8,128)}, f32[512,512]{1,0:T(8,128)}, u32[]{:S(2)}, u32[]{:S(2)}) collective-permute-start(f32[512,512]{1,0:T(8,128)} %get-tuple-element.86.mine_ref), channel_id=1, source_target_pairs={{16,112},{48,80},{80,48},{112,16},{144,240},{176,208},{208,176},{2... | collective-permute-start | bytes 3145736 | tf_op jit(solution)/shard_map/ppermute | solution.py:541
  98.7 0.9 shard_map.109
  99.7 1.3 collective-permute-start.8
  101.0 11.3 %collective-permute-done.8.got_ref = f32[8,512]{1,0:T(8,128)S(1)} collective-permute-done((f32[8,512]{1,0:T(8,128)S(1)}, f32[8,512]{1,0:T(8,128)S(1)}, u32[]{:S(2)}, u32[]{:S(2)}) %collective-permute-start.8) | collective-permute-done | bytes 16416 | tf_op jit(solution)/shard_map/ppermute | solution.py:541
  112.3 12.8 %shard_map.110 = (f32[16,512]{1,0:T(8,128)}, f32[16,512]{1,0:T(8,128)S(1)}, f32[8,512]{1,0:T(8,128)S(1)}) custom-call(s32[1]{0:T(128)} %bitcast.place_ref, s32[16,4]{1,0:T(8,128)S(1)} %copy.12.offs_ref, bf16[16,64,512]{2,1,0:T(8,128)(2,1)} %copy-done.6, f32[16,64,512]{2,1,0:T(8,128)} %gains_far.3, s32[16,512]{1,0:T(8,128)S(1)} %copy-done.9, ...), custom_call_target="tpu_custom_call" | custom-call | flops 4000000000 | bytes 3145728 | tf_op jit(solution)/shard_map/pallas_call | solution.py:131
  125.1 1.3 collective-permute-start.9
  126.4 1.8 %collective-permute-done.9.other_ref = f32[8,512]{1,0:T(8,128)S(1)} collective-permute-done((f32[8,512]{1,0:T(8,128)S(1)}, f32[8,512]{1,0:T(8,128)S(1)}, u32[]{:S(2)}, u32[]{:S(2)}) %collective-permute-start.9) | collective-permute-done | bytes 16416 | tf_op jit(solution)/shard_map/ppermute | solution.py:541
  128.6 2.4 %collective-permute-start.10 = (f32[8,512]{1,0:T(8,128)S(1)}, f32[8,512]{1,0:T(8,128)S(1)}, u32[]{:S(2)}, u32[]{:S(2)}) collective-permute-start(f32[8,512]{1,0:T(8,128)S(1)} %shard_map.111.mine_ref), channel_id=1, source_target_pairs={{16,48},{48,16},{80,112},{112,80},{144,176},{176,144},{208,240},{2... | collective-permute-start | bytes 49160 | tf_op jit(solution)/shard_map/ppermute | solution.py:541
  131.0 2.0 %collective-permute-done.10.other_ref.po_ref = f32[8,512]{1,0:T(8,128)S(1)} collective-permute-done((f32[8,512]{1,0:T(8,128)S(1)}, f32[8,512]{1,0:T(8,128)S(1)}, u32[]{:S(2)}, u32[]{:S(2)}) %collective-permute-start.10) | collective-permute-done | bytes 16416 | tf_op jit(solution)/shard_map/ppermute | solution.py:541
  133.4 2.9 %collective-permute-start.11 = (f32[8,512]{1,0:T(8,128)S(1)}, f32[8,512]{1,0:T(8,128)S(1)}, u32[]{:S(2)}, u32[]{:S(2)}) collective-permute-start(f32[8,512]{1,0:T(8,128)S(1)} %shard_map.112.mine_ref), channel_id=1, source_target_pairs={{16,112},{48,80},{80,48},{112,16},{144,240},{176,208},{208,176},{2... | collective-permute-start | bytes 49160 | tf_op jit(solution)/shard_map/ppermute | solution.py:541
  136.3 2.8 %shard_map.113 = (bf16[2,512,512]{2,1,0:T(8,128)(2,1)S(1)}, bf16[2,512,512]{2,1,0:T(8,128)(2,1)S(1)}) custom-call(s32[1]{0:T(128)} %bitcast.11.flag_ref, f32[512,512]{1,0:T(8,128)} %get-tuple-element.86.mine_ref, f32[512,512]{1,0:T(8,128)} %collective-permute-done.12.other_ref), custom_call_target="tpu_custom_call" | custom-call | flops 1000000000 | bytes 5242880 | tf_op jit(solution)/shard_map/pallas_call | solution.py:131
  139.5 1.3 collective-permute-start.13
  140.9 3.7 %collective-permute-done.13.got_ref = f32[8,512]{1,0:T(8,128)S(1)} collective-permute-done((f32[8,512]{1,0:T(8,128)S(1)}, f32[8,512]{1,0:T(8,128)S(1)}, u32[]{:S(2)}, u32[]{:S(2)}) %collective-permute-start.13) | collective-permute-done | bytes 16416 | tf_op jit(solution)/shard_map/ppermute | solution.py:541
  144.5 0.9 shard_map.115
  145.5 1.3 collective-permute-start.14
  146.8 3.2 %collective-permute-done.14.got_ref = f32[8,512]{1,0:T(8,128)S(1)} collective-permute-done((f32[8,512]{1,0:T(8,128)S(1)}, f32[8,512]{1,0:T(8,128)S(1)}, u32[]{:S(2)}, u32[]{:S(2)}) %collective-permute-start.14) | collective-permute-done | bytes 16416 | tf_op jit(solution)/shard_map/ppermute | solution.py:541
  150.0 0.9 shard_map.116
  150.9 1.3 collective-permute-start.15
  152.2 3.2 %collective-permute-done.15.got_ref = f32[8,512]{1,0:T(8,128)S(1)} collective-permute-done((f32[8,512]{1,0:T(8,128)S(1)}, f32[8,512]{1,0:T(8,128)S(1)}, u32[]{:S(2)}, u32[]{:S(2)}) %collective-permute-start.15) | collective-permute-done | bytes 16416 | tf_op jit(solution)/shard_map/ppermute | solution.py:541
  155.4 1.7 %shard_map.117 = (f32[8,512]{1,0:T(8,128)S(1)}, f32[8,512]{1,0:T(8,128)S(1)}) custom-call(s32[3]{0:T(128)S(1)} %pad_add_fusion.1.place_ref, f32[8,512]{1,0:T(8,128)S(1)} %get-tuple-element.92.state_ref, f32[8,512]{1,0:T(8,128)S(1)} %collective-permute-done.15.got_ref, bf16[2,512,512]{2,1,0:T(8,128)(2,1)S(1)} %get-tuple-element.88.op_ref.quad_ref, ...), custom_call_target="tpu_custom_call" | custom-call | flops 100000000 | bytes 1048576 | tf_op jit(solution)/shard_map/pallas_call | solution.py:131
  157.1 1.3 collective-permute-start.16
  158.4 0.8 collective-permute-done.16.got_ref
  159.2 3.9 %shard_map.118 = f32[16,512]{1,0:T(8,128)} custom-call(s32[1]{0:T(128)} %bitcast.place_ref, s32[16,4]{1,0:T(8,128)S(1)} %copy.12.offs_ref, s32[16,512]{1,0:T(8,128)S(1)} %copy-done.9, f32[16,512]{1,0:T(8,128)S(1)} %copy-done.10, f32[16,512]{1,0:T(8,128)S(1)} %copy-done.11, f32[16,512]{1,0:T(8,128)S(1)} %get-tuple-element.80.u_ref, f32[16,512]{1,0:T(8,128)S(1)} %copy-done.13, ...), custom_call_target="tpu_custom_call" | custom-call | flops 100000000 | bytes 1048576 | tf_op jit(solution)/shard_map/pallas_call | solution.py:131
  (45 shorter events, 3.8 us)
Async XLA Ops:
  27.1 11.1 %collective-permute-start = (f32[520,512]{1,0:T(8,128)S(1)}, f32[520,512]{1,0:T(8,128)S(1)}, u32[]{:S(2)}, u32[]{:S(2)}) collective-permute-start(f32[520,512]{1,0:T(8,128)S(1)} %shard_map.95.mine_ref.map_ref), channel_id=1, source_target_pairs={{16,0},{48,32},{80,64},{112,96},{144,128},{176,160},{208,192},{240... | collective-permute-start | bytes 3194888 | tf_op jit(solution)/shard_map/ppermute | solution.py:541
  38.1 2.6 %copy-start.9 = (s32[16,512]{1,0:T(8,128)S(1)}, s32[16,512]{1,0:T(8,128)}, u32[]{:S(2)}) copy-start(s32[16,512]{1,0:T(8,128)} %up_ref.4) | copy-start | bytes 98308
  38.1 2.6 %copy-start.10 = (f32[16,512]{1,0:T(8,128)S(1)}, f32[16,512]{1,0:T(8,128)}, u32[]{:S(2)}) copy-start(f32[16,512]{1,0:T(8,128)} %c_ref.5) | copy-start | bytes 98308
  38.1 2.6 %copy-start.11 = (f32[16,512]{1,0:T(8,128)S(1)}, f32[16,512]{1,0:T(8,128)}, u32[]{:S(2)}) copy-start(f32[16,512]{1,0:T(8,128)} %sg_ref.5) | copy-start | bytes 98308
  39.1 18.6 %collective-permute-start.1 = (f32[520,512]{1,0:T(8,128)}, f32[520,512]{1,0:T(8,128)}, u32[]{:S(2)}, u32[]{:S(2)}) collective-permute-start(f32[520,512]{1,0:T(8,128)} %get-tuple-element.49.mine_ref), channel_id=1, source_target_pairs={{0,32},{32,0},{64,96},{96,64},{128,160},{160,128},{192,224},{224,1... | collective-permute-start | bytes 3194888 | tf_op jit(solution)/shard_map/ppermute | solution.py:541
  57.7 3.0 %copy-start.8 = (f32[512,512]{1,0:T(8,128)}, f32[512,512]{1,0:T(8,128)S(1)}, u32[]{:S(2)}) copy-start(f32[512,512]{1,0:T(8,128)S(1)} %get-tuple-element.67.mine_ref) | copy-start | bytes 3145732
  57.7 6.0 %copy-start.7 = (s32[16,64]{1,0:T(8,128)S(1)}, s32[16,64]{1,0:T(8,128)}, u32[]{:S(2)}) copy-start(s32[16,64]{1,0:T(8,128)} %obs_ref) | copy-start | bytes 12292
  60.7 6.8 %collective-permute-start.5 = (f32[512,512]{1,0:T(8,128)S(1)}, f32[512,512]{1,0:T(8,128)}, u32[]{:S(2)}, u32[]{:S(2)}) collective-permute-start(f32[512,512]{1,0:T(8,128)S(1)} %get-tuple-element.67.mine_ref), channel_id=1, source_target_pairs={{0,16},{32,48},{64,80},{96,112},{128,144},{160,176},{192,208},{224... | collective-permute-start | bytes 3145736 | tf_op jit(solution)/shard_map/ppermute | solution.py:541
  61.9 11.2 %collective-permute-start.2 = (f32[520,512]{1,0:T(8,128)}, f32[520,512]{1,0:T(8,128)}, u32[]{:S(2)}, u32[]{:S(2)}) collective-permute-start(f32[520,512]{1,0:T(8,128)} %get-tuple-element.53.mine_ref), channel_id=1, source_target_pairs={{0,96},{32,64},{64,32},{96,0},{128,224},{160,192},{192,160},{224,1... | collective-permute-start | bytes 3194888 | tf_op jit(solution)/shard_map/ppermute | solution.py:541
  64.0 1.0 copy-start.6
  71.1 1.0 copy-start
  72.1 1.0 copy-start.2
  73.1 1.6 copy-start.14
  75.6 15.9 %collective-permute-start.6 = (f32[512,512]{1,0:T(8,128)}, f32[512,512]{1,0:T(8,128)}, u32[]{:S(2)}, u32[]{:S(2)}) collective-permute-start(f32[512,512]{1,0:T(8,128)} %get-tuple-element.69.mine_ref), channel_id=1, source_target_pairs={{16,48},{48,16},{80,112},{112,80},{144,176},{176,144},{208,240},{2... | collective-permute-start | bytes 3145736 | tf_op jit(solution)/shard_map/ppermute | solution.py:541
  78.8 2.0 %collective-permute-start.3 = (f32[8,512]{1,0:T(8,128)S(1)}, f32[8,512]{1,0:T(8,128)S(1)}, u32[]{:S(2)}, u32[]{:S(2)}) collective-permute-start(f32[8,512]{1,0:T(8,128)S(1)} %get-tuple-element.59), channel_id=1, source_target_pairs={{0,128},{32,160},{64,192},{96,224},{128,256},{160,288},{192,320},{... | collective-permute-start | bytes 49160 | tf_op jit(solution)/shard_map/ppermute | solution.py:541
  81.8 2.2 %collective-permute-start.4 = (f32[8,512]{1,0:T(8,128)S(1)}, f32[8,512]{1,0:T(8,128)S(1)}, u32[]{:S(2)}, u32[]{:S(2)}) collective-permute-start(f32[8,512]{1,0:T(8,128)S(1)} %get-tuple-element.64), channel_id=1, source_target_pairs={{0,128},{32,160},{64,192},{96,224},{128,256},{160,288},{192,320},{... | collective-permute-start | bytes 49160 | tf_op jit(solution)/shard_map/ppermute | solution.py:541
  95.1 1.0 copy-start.4
  96.1 40.2 %collective-permute-start.12 = (f32[512,512]{1,0:T(8,128)}, f32[512,512]{1,0:T(8,128)}, u32[]{:S(2)}, u32[]{:S(2)}) collective-permute-start(f32[512,512]{1,0:T(8,128)} %get-tuple-element.86.mine_ref), channel_id=1, source_target_pairs={{16,112},{48,80},{80,48},{112,16},{144,240},{176,208},{208,176},{2... | collective-permute-start | bytes 3145736 | tf_op jit(solution)/shard_map/ppermute | solution.py:541
  98.0 0.7 collective-permute-start.7
  98.7 13.6 %copy-start.12 = (f32[16,64]{1,0:T(8,128)S(1)}, f32[16,64]{1,0:T(8,128)}, u32[]{:S(2)}) copy-start(f32[16,64]{1,0:T(8,128)} %y_ref.1) | copy-start | bytes 12292
  99.7 12.6 %collective-permute-start.8 = (f32[8,512]{1,0:T(8,128)S(1)}, f32[8,512]{1,0:T(8,128)S(1)}, u32[]{:S(2)}, u32[]{:S(2)}) collective-permute-start(f32[8,512]{1,0:T(8,128)S(1)} %get-tuple-element.78), channel_id=1, source_target_pairs={{0,16},{32,48},{64,80},{96,112},{128,144},{160,176},{192,208},{224... | collective-permute-start | bytes 49160 | tf_op jit(solution)/shard_map/ppermute | solution.py:541
  112.3 15.9 %copy-start.3 = (bf16[2,512,512]{2,1,0:T(8,128)(2,1)S(1)}, bf16[2,512,512]{2,1,0:T(8,128)(2,1)}, u32[]{:S(2)}) copy-start(bf16[2,512,512]{2,1,0:T(8,128)(2,1)} %copy-done.2) | copy-start | bytes 3145732
  125.1 3.1 %collective-permute-start.9 = (f32[8,512]{1,0:T(8,128)S(1)}, f32[8,512]{1,0:T(8,128)S(1)}, u32[]{:S(2)}, u32[]{:S(2)}) collective-permute-start(f32[8,512]{1,0:T(8,128)S(1)} %get-tuple-element.81.mine_ref.oo_ref), channel_id=1, source_target_pairs={{0,16},{32,48},{64,80},{96,112},{128,144},{160,176},{192,208},{224... | collective-permute-start | bytes 49160 | tf_op jit(solution)/shard_map/ppermute | solution.py:541
  128.2 4.9 %copy-start.1 = (bf16[2,512,512]{2,1,0:T(8,128)(2,1)S(1)}, bf16[2,512,512]{2,1,0:T(8,128)(2,1)}, u32[]{:S(2)}) copy-start(bf16[2,512,512]{2,1,0:T(8,128)(2,1)} %copy-done) | copy-start | bytes 3145732
  128.6 4.5 %collective-permute-start.10 = (f32[8,512]{1,0:T(8,128)S(1)}, f32[8,512]{1,0:T(8,128)S(1)}, u32[]{:S(2)}, u32[]{:S(2)}) collective-permute-start(f32[8,512]{1,0:T(8,128)S(1)} %shard_map.111.mine_ref), channel_id=1, source_target_pairs={{16,48},{48,16},{80,112},{112,80},{144,176},{176,144},{208,240},{2... | collective-permute-start | bytes 49160 | tf_op jit(solution)/shard_map/ppermute | solution.py:541
  133.4 5.7 %collective-permute-start.11 = (f32[8,512]{1,0:T(8,128)S(1)}, f32[8,512]{1,0:T(8,128)S(1)}, u32[]{:S(2)}, u32[]{:S(2)}) collective-permute-start(f32[8,512]{1,0:T(8,128)S(1)} %shard_map.112.mine_ref), channel_id=1, source_target_pairs={{16,112},{48,80},{80,48},{112,16},{144,240},{176,208},{208,176},{2... | collective-permute-start | bytes 49160 | tf_op jit(solution)/shard_map/ppermute | solution.py:541
  136.3 2.8 %copy-start.5 = (bf16[2,512,512]{2,1,0:T(8,128)(2,1)S(1)}, bf16[2,512,512]{2,1,0:T(8,128)(2,1)}, u32[]{:S(2)}) copy-start(bf16[2,512,512]{2,1,0:T(8,128)(2,1)} %copy-done.4) | copy-start | bytes 3145732
  139.5 5.1 %collective-permute-start.13 = (f32[8,512]{1,0:T(8,128)S(1)}, f32[8,512]{1,0:T(8,128)S(1)}, u32[]{:S(2)}, u32[]{:S(2)}) collective-permute-start(f32[8,512]{1,0:T(8,128)S(1)} %shard_map.114.off_ref), channel_id=1, source_target_pairs={{144,16},{176,48},{208,80},{240,112},{272,144},{304,176},{336,208}... | collective-permute-start | bytes 49160 | tf_op jit(solution)/shard_map/ppermute | solution.py:541
  145.5 4.5 %collective-permute-start.14 = (f32[8,512]{1,0:T(8,128)S(1)}, f32[8,512]{1,0:T(8,128)S(1)}, u32[]{:S(2)}, u32[]{:S(2)}) collective-permute-start(f32[8,512]{1,0:T(8,128)S(1)} %get-tuple-element.91), channel_id=1, source_target_pairs={{144,16},{176,48},{208,80},{240,112},{272,144},{304,176},{336,208}... | collective-permute-start | bytes 49160 | tf_op jit(solution)/shard_map/ppermute | solution.py:541
  150.9 4.5 %collective-permute-start.15 = (f32[8,512]{1,0:T(8,128)S(1)}, f32[8,512]{1,0:T(8,128)S(1)}, u32[]{:S(2)}, u32[]{:S(2)}) collective-permute-start(f32[8,512]{1,0:T(8,128)S(1)} %get-tuple-element.93), channel_id=1, source_target_pairs={{144,16},{176,48},{208,80},{240,112},{272,144},{304,176},{336,208}... | collective-permute-start | bytes 49160 | tf_op jit(solution)/shard_map/ppermute | solution.py:541
  155.4 3.8 %copy-start.13 = (f32[16,512]{1,0:T(8,128)S(1)}, f32[16,512]{1,0:T(8,128)}, u32[]{:S(2)}) copy-start(f32[16,512]{1,0:T(8,128)} %get-tuple-element.47.x_ref) | copy-start | bytes 98308
  157.1 2.1 %collective-permute-start.16 = (f32[8,512]{1,0:T(8,128)S(1)}, f32[8,512]{1,0:T(8,128)S(1)}, u32[]{:S(2)}, u32[]{:S(2)}) collective-permute-start(f32[8,512]{1,0:T(8,128)S(1)} %get-tuple-element.95), channel_id=1, source_target_pairs={{16,0},{48,32},{80,64},{112,96},{144,128},{176,160},{208,192},{240... | collective-permute-start | bytes 49160 | tf_op jit(solution)/shard_map/ppermute | solution.py:541

commit v6 on v5

--- a/solution.py
+++ b/solution.py
@@ -149,9 +149,9 @@
         parts_ref[0, at, :], parts_ref[1, at, :] = split2(values_ref[at, :])
 
 
-def keep_columns(rows_ref, kept_ref, start):
-    turned = jnp.transpose(rows_ref[...].astype(F32))
-    for k in range(rows_ref.shape[0]):
+def keep_columns(rows, kept_ref, start):
+    turned = jnp.transpose(rows)
+    for k in range(rows.shape[0]):
         kept_ref[k, start : start + N, :] = jnp.broadcast_to(turned[:, k : k + 1], (N, LANES))
 
 
@@ -188,7 +188,7 @@
 
     def kernel(
         offs_ref, cells_ref, up_far, c_far, obs_far, y_far, gains_far,
-        map_ref, held_ref, moved_ref, picked_ref, ups_ref, cs_ref,
+        map_ref, held_ref, moved_ref, picked_ref, both_ref,
         up_ref, c_ref, obs_ref, y_ref, gains_ref, sem
     ):
         pairs = ((up_far, up_ref), (c_far, c_ref), (obs_far, obs_ref), (y_far, y_ref))
@@ -201,8 +201,7 @@
         start_identity(held_ref)
         for copy in copies:
             copy.wait()
-        keep_columns(up_ref, ups_ref, 0)
-        keep_columns(c_ref, cs_ref, 0)
+        keep_columns(up_ref[...].astype(F32) + c_ref[...], both_ref, 0)
         head = lax.broadcasted_iota(jnp.int32, (8, 1), 0) == 0
 
         def one(k, vec):
@@ -211,7 +210,9 @@
             fetch(k).wait()
             gain = RELAXATION * s.astype(F32) + gains_ref[k]
             for r in range(0, N, CELLS):
-                ups, cs = ups_ref[k, r : r + CELLS, :], cs_ref[k, r : r + CELLS, :]
+                both = both_ref[k, r : r + CELLS, :]
+                ups = jnp.floor(both)
+                cs = both - ups
                 for j in range(PIECES):
                     at = lambda by: held_ref[j, pl.ds(REACH + r + by, CELLS), :]
                     arrived = at(step.offs[0])
@@ -253,7 +254,6 @@
             pltpu.VMEM((PIECES, N, LANES), F32),
             pltpu.VMEM((OBS, N), F32),
             pltpu.VMEM((steps, N, LANES), F32),
-            pltpu.VMEM((steps, N, LANES), F32),
             pltpu.VMEM((steps, N), jnp.int32),
             pltpu.VMEM((steps, N), F32),
             pltpu.VMEM((steps, OBS), jnp.int32),
@@ -272,14 +272,13 @@
 def smoother_map(offsets, upwind, courant, smooth_gain):
     steps = offsets.shape[0]
 
-    def kernel(offs_ref, up_ref, c_ref, sg_ref, map_ref, parts_ref, held_ref, out_ref, ups_ref, cs_ref, gains_ref):
+    def kernel(offs_ref, up_ref, c_ref, sg_ref, map_ref, parts_ref, held_ref, out_ref, both_ref, gains_ref):
         outside = jnp.full((REACH, LANES), -1.0, F32)
         for k in range(steps):
-            ups_ref[k, 0:REACH, :] = outside
-            ups_ref[k, REACH + N : N + 2 * REACH, :] = outside
-        keep_columns(up_ref, ups_ref, REACH)
-        keep_columns(c_ref, cs_ref, 0)
-        keep_columns(sg_ref, gains_ref, 0)
+            both_ref[k, 0:REACH, :] = outside
+            both_ref[k, REACH + N : N + 2 * REACH, :] = outside
+        keep_columns(up_ref[...].astype(F32) + c_ref[...], both_ref, REACH)
+        keep_columns(sg_ref[...], gains_ref, 0)
         start_identity(held_ref.at[0])
         clear_edges(held_ref.at[1])
         clear_edges(out_ref)
@@ -289,14 +288,16 @@
             offs = [offs_ref[k, band] for band in range(BANDS)]
             now, later = held_ref.at[lax.rem(i, 2)], held_ref.at[lax.rem(i + 1, 2)]
             for r in range(0, N, CELLS):
-                cs = cs_ref[k, r : r + CELLS, :]
+                both = both_ref[k, REACH + r : REACH + r + CELLS, :]
+                cs = both - jnp.floor(both)
                 for j in range(PIECES):
                     at = slice(REACH + r, REACH + r + CELLS)
                     out_ref[j, at, :] = cs * now[j, at, :]
             for r in range(0, N, CELLS):
                 froms = [pl.ds(REACH + r - offs[band], CELLS) for band in range(BANDS)]
-                taken = [ups_ref[k, froms[band], :] == band for band in range(BANDS)]
-                centre = 1.0 - cs_ref[k, r : r + CELLS, :] - DIFFUSION
+                taken = [jnp.floor(both_ref[k, froms[band], :]) == band for band in range(BANDS)]
+                both = both_ref[k, REACH + r : REACH + r + CELLS, :]
+                centre = 1.0 - (both - jnp.floor(both)) - DIFFUSION
                 gain = gains_ref[k, r : r + CELLS, :]
                 for j in range(PIECES):
                     total = diffused(now, j, REACH + r, CELLS, centre)
@@ -316,7 +317,6 @@
             pltpu.VMEM((2, PIECES, N + 2 * REACH, LANES), F32),
             pltpu.VMEM((PIECES, N + 2 * REACH, LANES), F32),
             pltpu.VMEM((steps, N + 2 * REACH, LANES), F32),
-            pltpu.VMEM((steps, N, LANES), F32),
             pltpu.VMEM((steps, N, LANES), F32),
         ],
         flops=8 * 10**9,

time: 164 us -> 161 us (0.982)
  Pallas kernels: 86.3 us -> 83.7 us
    pallas_call x24, Pallas kernels: 86.3 us -> 83.7 us  [call(): pl.pallas_call(kernel, out_shape=tuple((jax.ShapeDtypeStruct(*out) for ou...]
where the time goes in v6:
time: 161 us; the launch traced here: 160 us
  Pallas kernels  83.7 us (52%)
  waiting for transfers between devices  36.8 us (23%)
  starting transfers between devices  33.9 us (21%)
  local copies, waits for them, and re-layouts  4.72 us (3%)
    pallas_call x24, Pallas kernels, call(): pl.pallas_call(kernel, out_shape=tuple((jax.ShapeDtypeStruct(*out) for ou...  83.7 us
    ppermute x17, waiting for transfers between devices, moved(): lax.ppermute(values, 'tm', [(i, to(i)) for i in range(32) if senders(i)])  36.8 us
    ppermute x17, starting transfers between devices, moved(): lax.ppermute(values, 'tm', [(i, to(i)) for i in range(32) if senders(i)])  33.9 us
    unnamed x31, local copies, waits for them, and re-layouts  4.72 us
  transfers between devices with their start and end apart: 17, of which 10 were waited for; matrix products, arithmetic and copies ran while one was open for 0% of the time, Pallas kernels for 26%

profile of v6, /device:TPU:1, one launch (start us, length us, event | category | flops | bytes accessed | tf_op | source)
XLA Modules:
  0.0 160.3 jit_solution(8345628282465194720)
XLA Ops:
  0.6 0.8 copy.12.offs_ref
  1.4 24.1 %shard_map.95.mine_ref.map_ref = f32[520,512]{1,0:T(8,128)S(1)} custom-call(s32[16,4]{1,0:T(8,128)S(1)} %copy.12.offs_ref, s32[16,64]{1,0:T(8,128)} %obs_ref, s32[16,512]{1,0:T(8,128)} %up_ref.4, f32[16,512]{1,0:T(8,128)} %c_ref.5, s32[16,64]{1,0:T(8,128)} %obs_ref, f32[16,64]{1,0:T(8,128)} %y_ref.1, f32[16,64,512]{2,1,0:T(8,128)} %gains_far.3), custom_call_target="tpu_custom_call" | custom-call | flops 16000000000 | bytes 4194304 | tf_op jit(solution)/shard_map/pallas_call | solution.py:131
  25.5 8.8 %collective-permute-start = (f32[520,512]{1,0:T(8,128)S(1)}, f32[520,512]{1,0:T(8,128)S(1)}, u32[]{:S(2)}, u32[]{:S(2)}) collective-permute-start(f32[520,512]{1,0:T(8,128)S(1)} %shard_map.95.mine_ref.map_ref), channel_id=1, source_target_pairs={{16,0},{48,32},{80,64},{112,96},{144,128},{176,160},{208,192},{240... | collective-permute-start | bytes 3194888 | tf_op jit(solution)/shard_map/ppermute | solution.py:541
  34.3 2.2 %collective-permute-done.other_ref = f32[520,512]{1,0:T(8,128)S(1)} collective-permute-done((f32[520,512]{1,0:T(8,128)S(1)}, f32[520,512]{1,0:T(8,128)S(1)}, u32[]{:S(2)}, u32[]{:S(2)}) %collective-permute-start) | collective-permute-done | bytes 1064992 | tf_op jit(solution)/shard_map/ppermute | solution.py:541
  36.5 1.0 shard_map.96
  37.4 1.7 %collective-permute-start.1 = (f32[520,512]{1,0:T(8,128)}, f32[520,512]{1,0:T(8,128)}, u32[]{:S(2)}, u32[]{:S(2)}) collective-permute-start(f32[520,512]{1,0:T(8,128)} %get-tuple-element.49.mine_ref), channel_id=1, source_target_pairs={{0,32},{32,0},{64,96},{96,64},{128,160},{160,128},{192,224},{224,1... | collective-permute-start | bytes 3194888 | tf_op jit(solution)/shard_map/ppermute | solution.py:541
  39.1 15.8 %shard_map.106 = (f32[512,512]{1,0:T(8,128)S(1)}, bf16[2,512,512]{2,1,0:T(8,128)(2,1)S(1)}) custom-call(s32[16,4]{1,0:T(8,128)S(1)} %copy.12.offs_ref, s32[16,512]{1,0:T(8,128)S(1)} %copy-done.9, f32[16,512]{1,0:T(8,128)S(1)} %copy-done.10, f32[16,512]{1,0:T(8,128)S(1)} %copy-done.11), custom_call_target="tpu_custom_call" | custom-call | flops 8000000000 | bytes 2097152 | tf_op jit(solution)/shard_map/pallas_call | solution.py:131
  55.0 2.9 %shard_map.97 = (f32[520,512]{1,0:T(8,128)}, f32[8,512]{1,0:T(8,128)}) custom-call(s32[1]{0:T(128)} %bitcast.1.flag_ref, f32[520,512]{1,0:T(8,128)} %get-tuple-element.49.mine_ref, f32[520,512]{1,0:T(8,128)} %collective-permute-done.1.other_ref.map_ref), custom_call_target="tpu_custom_call" | custom-call | flops 1000000000 | bytes 5242880 | tf_op jit(solution)/shard_map/pallas_call | solution.py:131
  57.9 1.3 collective-permute-start.5
  59.2 1.6 %collective-permute-start.2 = (f32[520,512]{1,0:T(8,128)}, f32[520,512]{1,0:T(8,128)}, u32[]{:S(2)}, u32[]{:S(2)}) collective-permute-start(f32[520,512]{1,0:T(8,128)} %get-tuple-element.53.mine_ref), channel_id=1, source_target_pairs={{0,96},{32,64},{64,32},{96,0},{128,224},{160,192},{192,160},{224,1... | collective-permute-start | bytes 3194888 | tf_op jit(solution)/shard_map/ppermute | solution.py:541
  61.3 1.0 copy-done.6
  62.2 2.4 %collective-permute-done.5.other_ref = f32[512,512]{1,0:T(8,128)} collective-permute-done((f32[512,512]{1,0:T(8,128)S(1)}, f32[512,512]{1,0:T(8,128)}, u32[]{:S(2)}, u32[]{:S(2)}) %collective-permute-start.5) | collective-permute-done | bytes 1048608 | tf_op jit(solution)/shard_map/ppermute | solution.py:541
  64.6 3.7 %shard_map.107 = (f32[512,512]{1,0:T(8,128)}, bf16[2,512,512]{2,1,0:T(8,128)(2,1)S(1)}, bf16[2,512,512]{2,1,0:T(8,128)(2,1)S(1)}) custom-call(s32[1]{0:T(128)} %bitcast.8.flag_ref, f32[512,512]{1,0:T(8,128)} %copy-done.8, f32[512,512]{1,0:T(8,128)} %collective-permute-done.5.other_ref), custom_call_target="tpu_custom_call" | custom-call | flops 1000000000 | bytes 5242880 | tf_op jit(solution)/shard_map/pallas_call | solution.py:131
  68.3 1.0 copy-done
  69.3 1.0 copy-done.2
  70.3 1.6 shard_map.99
  71.9 0.9 shard_map.100
  72.8 3.4 %collective-permute-start.6 = (f32[512,512]{1,0:T(8,128)}, f32[512,512]{1,0:T(8,128)}, u32[]{:S(2)}, u32[]{:S(2)}) collective-permute-start(f32[512,512]{1,0:T(8,128)} %get-tuple-element.69.mine_ref), channel_id=1, source_target_pairs={{16,48},{48,16},{80,112},{112,80},{144,176},{176,144},{208,240},{2... | collective-permute-start | bytes 3145736 | tf_op jit(solution)/shard_map/ppermute | solution.py:541
  76.9 1.4 shard_map.101
  78.2 0.9 shard_map.102
  80.0 1.4 shard_map.103
  81.3 0.9 shard_map.105
  82.3 6.4 %collective-permute-done.6.other_ref = f32[512,512]{1,0:T(8,128)} collective-permute-done((f32[512,512]{1,0:T(8,128)}, f32[512,512]{1,0:T(8,128)}, u32[]{:S(2)}, u32[]{:S(2)}) %collective-permute-start.6) | collective-permute-done | bytes 1048608 | tf_op jit(solution)/shard_map/ppermute | solution.py:541
  88.7 3.7 %shard_map.108 = (f32[512,512]{1,0:T(8,128)}, bf16[2,512,512]{2,1,0:T(8,128)(2,1)S(1)}, bf16[2,512,512]{2,1,0:T(8,128)(2,1)S(1)}) custom-call(s32[1]{0:T(128)} %bitcast.7.flag_ref, f32[512,512]{1,0:T(8,128)} %get-tuple-element.69.mine_ref, f32[512,512]{1,0:T(8,128)} %collective-permute-done.6.other_ref), custom_call_target="tpu_custom_call" | custom-call | flops 1000000000 | bytes 5242880 | tf_op jit(solution)/shard_map/pallas_call | solution.py:131
  92.4 1.0 copy-done.4
  93.4 1.9 %collective-permute-start.12 = (f32[512,512]{1,0:T(8,128)}, f32[512,512]{1,0:T(8,128)}, u32[]{:S(2)}, u32[]{:S(2)}) collective-permute-start(f32[512,512]{1,0:T(8,128)} %get-tuple-element.86.mine_ref), channel_id=1, source_target_pairs={{16,112},{48,80},{80,48},{112,16},{144,240},{176,208},{208,176},{2... | collective-permute-start | bytes 3145736 | tf_op jit(solution)/shard_map/ppermute | solution.py:541
  96.0 0.9 shard_map.109
  96.9 1.3 collective-permute-start.8
  98.2 11.3 %collective-permute-done.8.got_ref = f32[8,512]{1,0:T(8,128)S(1)} collective-permute-done((f32[8,512]{1,0:T(8,128)S(1)}, f32[8,512]{1,0:T(8,128)S(1)}, u32[]{:S(2)}, u32[]{:S(2)}) %collective-permute-start.8) | collective-permute-done | bytes 16416 | tf_op jit(solution)/shard_map/ppermute | solution.py:541
  109.5 12.8 %shard_map.110 = (f32[16,512]{1,0:T(8,128)}, f32[16,512]{1,0:T(8,128)S(1)}, f32[8,512]{1,0:T(8,128)S(1)}) custom-call(s32[1]{0:T(128)} %bitcast.place_ref, s32[16,4]{1,0:T(8,128)S(1)} %copy.12.offs_ref, bf16[16,64,512]{2,1,0:T(8,128)(2,1)} %copy-done.6, f32[16,64,512]{2,1,0:T(8,128)} %gains_far.3, s32[16,512]{1,0:T(8,128)S(1)} %copy-done.9, ...), custom_call_target="tpu_custom_call" | custom-call | flops 4000000000 | bytes 3145728 | tf_op jit(solution)/shard_map/pallas_call | solution.py:131
  122.3 1.3 collective-permute-start.9
  123.6 1.8 %collective-permute-done.9.other_ref = f32[8,512]{1,0:T(8,128)S(1)} collective-permute-done((f32[8,512]{1,0:T(8,128)S(1)}, f32[8,512]{1,0:T(8,128)S(1)}, u32[]{:S(2)}, u32[]{:S(2)}) %collective-permute-start.9) | collective-permute-done | bytes 16416 | tf_op jit(solution)/shard_map/ppermute | solution.py:541
  125.8 2.6 %collective-permute-start.10 = (f32[8,512]{1,0:T(8,128)S(1)}, f32[8,512]{1,0:T(8,128)S(1)}, u32[]{:S(2)}, u32[]{:S(2)}) collective-permute-start(f32[8,512]{1,0:T(8,128)S(1)} %shard_map.111.mine_ref), channel_id=1, source_target_pairs={{16,48},{48,16},{80,112},{112,80},{144,176},{176,144},{208,240},{2... | collective-permute-start | bytes 49160 | tf_op jit(solution)/shard_map/ppermute | solution.py:541
  128.4 1.9 %collective-permute-done.10.other_ref.po_ref = f32[8,512]{1,0:T(8,128)S(1)} collective-permute-done((f32[8,512]{1,0:T(8,128)S(1)}, f32[8,512]{1,0:T(8,128)S(1)}, u32[]{:S(2)}, u32[]{:S(2)}) %collective-permute-start.10) | collective-permute-done | bytes 16416 | tf_op jit(solution)/shard_map/ppermute | solution.py:541
  130.6 2.9 %collective-permute-start.11 = (f32[8,512]{1,0:T(8,128)S(1)}, f32[8,512]{1,0:T(8,128)S(1)}, u32[]{:S(2)}, u32[]{:S(2)}) collective-permute-start(f32[8,512]{1,0:T(8,128)S(1)} %shard_map.112.mine_ref), channel_id=1, source_target_pairs={{16,112},{48,80},{80,48},{112,16},{144,240},{176,208},{208,176},{2... | collective-permute-start | bytes 49160 | tf_op jit(solution)/shard_map/ppermute | solution.py:541
  133.6 2.8 %shard_map.113 = (bf16[2,512,512]{2,1,0:T(8,128)(2,1)S(1)}, bf16[2,512,512]{2,1,0:T(8,128)(2,1)S(1)}) custom-call(s32[1]{0:T(128)} %bitcast.11.flag_ref, f32[512,512]{1,0:T(8,128)} %get-tuple-element.86.mine_ref, f32[512,512]{1,0:T(8,128)} %collective-permute-done.12.other_ref), custom_call_target="tpu_custom_call" | custom-call | flops 1000000000 | bytes 5242880 | tf_op jit(solution)/shard_map/pallas_call | solution.py:131
  136.7 1.3 collective-permute-start.13
  138.1 3.7 %collective-permute-done.13.got_ref = f32[8,512]{1,0:T(8,128)S(1)} collective-permute-done((f32[8,512]{1,0:T(8,128)S(1)}, f32[8,512]{1,0:T(8,128)S(1)}, u32[]{:S(2)}, u32[]{:S(2)}) %collective-permute-start.13) | collective-permute-done | bytes 16416 | tf_op jit(solution)/shard_map/ppermute | solution.py:541
  141.8 0.9 shard_map.115
  142.7 1.3 collective-permute-start.14
  144.0 3.2 %collective-permute-done.14.got_ref = f32[8,512]{1,0:T(8,128)S(1)} collective-permute-done((f32[8,512]{1,0:T(8,128)S(1)}, f32[8,512]{1,0:T(8,128)S(1)}, u32[]{:S(2)}, u32[]{:S(2)}) %collective-permute-start.14) | collective-permute-done | bytes 16416 | tf_op jit(solution)/shard_map/ppermute | solution.py:541
  147.2 0.9 shard_map.116
  148.1 1.3 collective-permute-start.15
  149.4 3.2 %collective-permute-done.15.got_ref = f32[8,512]{1,0:T(8,128)S(1)} collective-permute-done((f32[8,512]{1,0:T(8,128)S(1)}, f32[8,512]{1,0:T(8,128)S(1)}, u32[]{:S(2)}, u32[]{:S(2)}) %collective-permute-start.15) | collective-permute-done | bytes 16416 | tf_op jit(solution)/shard_map/ppermute | solution.py:541
  152.6 1.7 %shard_map.117 = (f32[8,512]{1,0:T(8,128)S(1)}, f32[8,512]{1,0:T(8,128)S(1)}) custom-call(s32[3]{0:T(128)S(1)} %pad_add_fusion.1.place_ref, f32[8,512]{1,0:T(8,128)S(1)} %get-tuple-element.92.state_ref, f32[8,512]{1,0:T(8,128)S(1)} %collective-permute-done.15.got_ref, bf16[2,512,512]{2,1,0:T(8,128)(2,1)S(1)} %get-tuple-element.88.op_ref.quad_ref, ...), custom_call_target="tpu_custom_call" | custom-call | flops 100000000 | bytes 1048576 | tf_op jit(solution)/shard_map/pallas_call | solution.py:131
  154.3 1.3 collective-permute-start.16
  155.6 0.8 collective-permute-done.16.got_ref
  156.4 3.9 %shard_map.118 = f32[16,512]{1,0:T(8,128)} custom-call(s32[1]{0:T(128)} %bitcast.place_ref, s32[16,4]{1,0:T(8,128)S(1)} %copy.12.offs_ref, s32[16,512]{1,0:T(8,128)S(1)} %copy-done.9, f32[16,512]{1,0:T(8,128)S(1)} %copy-done.10, f32[16,512]{1,0:T(8,128)S(1)} %copy-done.11, f32[16,512]{1,0:T(8,128)S(1)} %get-tuple-element.80.u_ref, f32[16,512]{1,0:T(8,128)S(1)} %copy-done.13, ...), custom_call_target="tpu_custom_call" | custom-call | flops 100000000 | bytes 1048576 | tf_op jit(solution)/shard_map/pallas_call | solution.py:131
  (45 shorter events, 3.8 us)
Async XLA Ops:
  25.5 11.0 %collective-permute-start = (f32[520,512]{1,0:T(8,128)S(1)}, f32[520,512]{1,0:T(8,128)S(1)}, u32[]{:S(2)}, u32[]{:S(2)}) collective-permute-start(f32[520,512]{1,0:T(8,128)S(1)} %shard_map.95.mine_ref.map_ref), channel_id=1, source_target_pairs={{16,0},{48,32},{80,64},{112,96},{144,128},{176,160},{208,192},{240... | collective-permute-start | bytes 3194888 | tf_op jit(solution)/shard_map/ppermute | solution.py:541
  36.5 2.6 %copy-start.9 = (s32[16,512]{1,0:T(8,128)S(1)}, s32[16,512]{1,0:T(8,128)}, u32[]{:S(2)}) copy-start(s32[16,512]{1,0:T(8,128)} %up_ref.4) | copy-start | bytes 98308
  36.5 2.6 %copy-start.10 = (f32[16,512]{1,0:T(8,128)S(1)}, f32[16,512]{1,0:T(8,128)}, u32[]{:S(2)}) copy-start(f32[16,512]{1,0:T(8,128)} %c_ref.5) | copy-start | bytes 98308
  36.5 2.6 %copy-start.11 = (f32[16,512]{1,0:T(8,128)S(1)}, f32[16,512]{1,0:T(8,128)}, u32[]{:S(2)}) copy-start(f32[16,512]{1,0:T(8,128)} %sg_ref.5) | copy-start | bytes 98308
  37.4 17.5 %collective-permute-start.1 = (f32[520,512]{1,0:T(8,128)}, f32[520,512]{1,0:T(8,128)}, u32[]{:S(2)}, u32[]{:S(2)}) collective-permute-start(f32[520,512]{1,0:T(8,128)} %get-tuple-element.49.mine_ref), channel_id=1, source_target_pairs={{0,32},{32,0},{64,96},{96,64},{128,160},{160,128},{192,224},{224,1... | collective-permute-start | bytes 3194888 | tf_op jit(solution)/shard_map/ppermute | solution.py:541
  55.0 3.0 %copy-start.8 = (f32[512,512]{1,0:T(8,128)}, f32[512,512]{1,0:T(8,128)S(1)}, u32[]{:S(2)}) copy-start(f32[512,512]{1,0:T(8,128)S(1)} %get-tuple-element.67.mine_ref) | copy-start | bytes 3145732
  55.0 6.0 %copy-start.7 = (s32[16,64]{1,0:T(8,128)S(1)}, s32[16,64]{1,0:T(8,128)}, u32[]{:S(2)}) copy-start(s32[16,64]{1,0:T(8,128)} %obs_ref) | copy-start | bytes 12292
  57.9 6.7 %collective-permute-start.5 = (f32[512,512]{1,0:T(8,128)S(1)}, f32[512,512]{1,0:T(8,128)}, u32[]{:S(2)}, u32[]{:S(2)}) collective-permute-start(f32[512,512]{1,0:T(8,128)S(1)} %get-tuple-element.67.mine_ref), channel_id=1, source_target_pairs={{0,16},{32,48},{64,80},{96,112},{128,144},{160,176},{192,208},{224... | collective-permute-start | bytes 3145736 | tf_op jit(solution)/shard_map/ppermute | solution.py:541
  59.2 11.1 %collective-permute-start.2 = (f32[520,512]{1,0:T(8,128)}, f32[520,512]{1,0:T(8,128)}, u32[]{:S(2)}, u32[]{:S(2)}) collective-permute-start(f32[520,512]{1,0:T(8,128)} %get-tuple-element.53.mine_ref), channel_id=1, source_target_pairs={{0,96},{32,64},{64,32},{96,0},{128,224},{160,192},{192,160},{224,1... | collective-permute-start | bytes 3194888 | tf_op jit(solution)/shard_map/ppermute | solution.py:541
  61.3 1.0 copy-start.6
  68.3 1.0 copy-start
  69.3 1.0 copy-start.2
  70.3 1.6 copy-start.14
  72.8 15.9 %collective-permute-start.6 = (f32[512,512]{1,0:T(8,128)}, f32[512,512]{1,0:T(8,128)}, u32[]{:S(2)}, u32[]{:S(2)}) collective-permute-start(f32[512,512]{1,0:T(8,128)} %get-tuple-element.69.mine_ref), channel_id=1, source_target_pairs={{16,48},{48,16},{80,112},{112,80},{144,176},{176,144},{208,240},{2... | collective-permute-start | bytes 3145736 | tf_op jit(solution)/shard_map/ppermute | solution.py:541
  76.2 2.0 %collective-permute-start.3 = (f32[8,512]{1,0:T(8,128)S(1)}, f32[8,512]{1,0:T(8,128)S(1)}, u32[]{:S(2)}, u32[]{:S(2)}) collective-permute-start(f32[8,512]{1,0:T(8,128)S(1)} %get-tuple-element.59), channel_id=1, source_target_pairs={{0,128},{32,160},{64,192},{96,224},{128,256},{160,288},{192,320},{... | collective-permute-start | bytes 49160 | tf_op jit(solution)/shard_map/ppermute | solution.py:541
  79.2 2.2 %collective-permute-start.4 = (f32[8,512]{1,0:T(8,128)S(1)}, f32[8,512]{1,0:T(8,128)S(1)}, u32[]{:S(2)}, u32[]{:S(2)}) collective-permute-start(f32[8,512]{1,0:T(8,128)S(1)} %get-tuple-element.64), channel_id=1, source_target_pairs={{0,128},{32,160},{64,192},{96,224},{128,256},{160,288},{192,320},{... | collective-permute-start | bytes 49160 | tf_op jit(solution)/shard_map/ppermute | solution.py:541
  92.4 1.0 copy-start.4
  93.4 40.2 %collective-permute-start.12 = (f32[512,512]{1,0:T(8,128)}, f32[512,512]{1,0:T(8,128)}, u32[]{:S(2)}, u32[]{:S(2)}) collective-permute-start(f32[512,512]{1,0:T(8,128)} %get-tuple-element.86.mine_ref), channel_id=1, source_target_pairs={{16,112},{48,80},{80,48},{112,16},{144,240},{176,208},{208,176},{2... | collective-permute-start | bytes 3145736 | tf_op jit(solution)/shard_map/ppermute | solution.py:541
  95.3 0.7 collective-permute-start.7
  96.0 13.5 %copy-start.12 = (f32[16,64]{1,0:T(8,128)S(1)}, f32[16,64]{1,0:T(8,128)}, u32[]{:S(2)}) copy-start(f32[16,64]{1,0:T(8,128)} %y_ref.1) | copy-start | bytes 12292
  96.9 12.6 %collective-permute-start.8 = (f32[8,512]{1,0:T(8,128)S(1)}, f32[8,512]{1,0:T(8,128)S(1)}, u32[]{:S(2)}, u32[]{:S(2)}) collective-permute-start(f32[8,512]{1,0:T(8,128)S(1)} %get-tuple-element.78), channel_id=1, source_target_pairs={{0,16},{32,48},{64,80},{96,112},{128,144},{160,176},{192,208},{224... | collective-permute-start | bytes 49160 | tf_op jit(solution)/shard_map/ppermute | solution.py:541
  109.5 15.9 %copy-start.3 = (bf16[2,512,512]{2,1,0:T(8,128)(2,1)S(1)}, bf16[2,512,512]{2,1,0:T(8,128)(2,1)}, u32[]{:S(2)}) copy-start(bf16[2,512,512]{2,1,0:T(8,128)(2,1)} %copy-done.2) | copy-start | bytes 3145732
  122.3 3.1 %collective-permute-start.9 = (f32[8,512]{1,0:T(8,128)S(1)}, f32[8,512]{1,0:T(8,128)S(1)}, u32[]{:S(2)}, u32[]{:S(2)}) collective-permute-start(f32[8,512]{1,0:T(8,128)S(1)} %get-tuple-element.81.mine_ref.oo_ref), channel_id=1, source_target_pairs={{0,16},{32,48},{64,80},{96,112},{128,144},{160,176},{192,208},{224... | collective-permute-start | bytes 49160 | tf_op jit(solution)/shard_map/ppermute | solution.py:541
  125.4 4.9 %copy-start.1 = (bf16[2,512,512]{2,1,0:T(8,128)(2,1)S(1)}, bf16[2,512,512]{2,1,0:T(8,128)(2,1)}, u32[]{:S(2)}) copy-start(bf16[2,512,512]{2,1,0:T(8,128)(2,1)} %copy-done) | copy-start | bytes 3145732
  125.8 4.5 %collective-permute-start.10 = (f32[8,512]{1,0:T(8,128)S(1)}, f32[8,512]{1,0:T(8,128)S(1)}, u32[]{:S(2)}, u32[]{:S(2)}) collective-permute-start(f32[8,512]{1,0:T(8,128)S(1)} %shard_map.111.mine_ref), channel_id=1, source_target_pairs={{16,48},{48,16},{80,112},{112,80},{144,176},{176,144},{208,240},{2... | collective-permute-start | bytes 49160 | tf_op jit(solution)/shard_map/ppermute | solution.py:541
  130.6 5.7 %collective-permute-start.11 = (f32[8,512]{1,0:T(8,128)S(1)}, f32[8,512]{1,0:T(8,128)S(1)}, u32[]{:S(2)}, u32[]{:S(2)}) collective-permute-start(f32[8,512]{1,0:T(8,128)S(1)} %shard_map.112.mine_ref), channel_id=1, source_target_pairs={{16,112},{48,80},{80,48},{112,16},{144,240},{176,208},{208,176},{2... | collective-permute-start | bytes 49160 | tf_op jit(solution)/shard_map/ppermute | solution.py:541
  133.6 2.8 %copy-start.5 = (bf16[2,512,512]{2,1,0:T(8,128)(2,1)S(1)}, bf16[2,512,512]{2,1,0:T(8,128)(2,1)}, u32[]{:S(2)}) copy-start(bf16[2,512,512]{2,1,0:T(8,128)(2,1)} %copy-done.4) | copy-start | bytes 3145732
  136.7 5.1 %collective-permute-start.13 = (f32[8,512]{1,0:T(8,128)S(1)}, f32[8,512]{1,0:T(8,128)S(1)}, u32[]{:S(2)}, u32[]{:S(2)}) collective-permute-start(f32[8,512]{1,0:T(8,128)S(1)} %shard_map.114.off_ref), channel_id=1, source_target_pairs={{144,16},{176,48},{208,80},{240,112},{272,144},{304,176},{336,208}... | collective-permute-start | bytes 49160 | tf_op jit(solution)/shard_map/ppermute | solution.py:541
  142.7 4.5 %collective-permute-start.14 = (f32[8,512]{1,0:T(8,128)S(1)}, f32[8,512]{1,0:T(8,128)S(1)}, u32[]{:S(2)}, u32[]{:S(2)}) collective-permute-start(f32[8,512]{1,0:T(8,128)S(1)} %get-tuple-element.91), channel_id=1, source_target_pairs={{144,16},{176,48},{208,80},{240,112},{272,144},{304,176},{336,208}... | collective-permute-start | bytes 49160 | tf_op jit(solution)/shard_map/ppermute | solution.py:541
  148.1 4.5 %collective-permute-start.15 = (f32[8,512]{1,0:T(8,128)S(1)}, f32[8,512]{1,0:T(8,128)S(1)}, u32[]{:S(2)}, u32[]{:S(2)}) collective-permute-start(f32[8,512]{1,0:T(8,128)S(1)} %get-tuple-element.93), channel_id=1, source_target_pairs={{144,16},{176,48},{208,80},{240,112},{272,144},{304,176},{336,208}... | collective-permute-start | bytes 49160 | tf_op jit(solution)/shard_map/ppermute | solution.py:541
  152.6 3.8 %copy-start.13 = (f32[16,512]{1,0:T(8,128)S(1)}, f32[16,512]{1,0:T(8,128)}, u32[]{:S(2)}) copy-start(f32[16,512]{1,0:T(8,128)} %get-tuple-element.47.x_ref) | copy-start | bytes 98308
  154.3 2.1 %collective-permute-start.16 = (f32[8,512]{1,0:T(8,128)S(1)}, f32[8,512]{1,0:T(8,128)S(1)}, u32[]{:S(2)}, u32[]{:S(2)}) collective-permute-start(f32[8,512]{1,0:T(8,128)S(1)} %get-tuple-element.95), channel_id=1, source_target_pairs={{16,0},{48,32},{80,64},{112,96},{144,128},{176,160},{208,192},{240... | collective-permute-start | bytes 49160 | tf_op jit(solution)/shard_map/ppermute | solution.py:541
